TPU v7x, 128 devices: a whole 4x4x4 slice. The times are simulated.
128 devices in a mesh: fem: 8 (over x, y_lo), bem: 16 (over y_hi, z, core).
Axes of the slice: x: 4, y: 4 (y_hi: 2, y_lo: 2; y = y_hi * 2 + y_lo), z: 4, core: 2. Of those that a mesh axis runs over, the one named last changes fastest.
Arguments:
- fem_field: float32 [64, 128, 32, 128], P('fem', 'bem'), may hold values from -6 to 6
- fem_source: float32 [64, 128, 32, 128], P('fem', 'bem'), may hold values from -6 to 6
- reaction: float32 [64, 128, 32], P('fem', 'bem'), may hold values from 0.5 to 3
- bem_density: float32 [128, 16384], P(None, 'bem'), may hold values from -6 to 6
- bem_source: float32 [128, 16384], P(None, 'bem'), may hold values from -6 to 6
- bem_diagonal: float32 [16384], P('bem'), may hold values from 2 to 6
- near_blocks: bfloat16 [32, 48, 512, 512], P('bem', 'fem'), may hold values from -0.0390625 to 0.0390625
- near_pairs: int32 [32, 48], P('bem'), may hold values from 0 to 31, as said below
- low_left: bfloat16 [32, 32, 512], P('bem'), may hold values from -1 to 1
- low_right: bfloat16 [32, 32, 512], replicated, may hold values from -0.25 to 0.25
- centers: float32 [32, 3], replicated, may hold values from 0 to 4
- trace_cell: int32 [32768], P(('fem', 'bem')), may hold values from 0 to 2047
- trace_bank: int32 [32768, 1], P(('fem', 'bem')), may hold values from 0 to 15; in each aligned block of 256 rows (0 to 255, 256 to 511, ...) at most 32 rows name the same one
- trace_row: int32 [32768], P(('fem', 'bem')), may hold values from 0 to 1023
Outputs:
- fem_out: float32 [64, 128, 32, 128], P('fem', 'bem')
- bem_out: float32 [128, 16384], P('fem', 'bem')
Inputs may be any that keep to these rules, and one draw needn't show every extreme that they name: `trace_bank`: among the 256 slots of one device no bem index is named more than 32 times, and some device names some index exactly 32 times. Panel p's near-field source panels are held by bem indices within two of p's own, counted around the bem axis: near_pairs[p, k] // 2 - p // 2 is -2, -1, 0, 1 or 2 modulo 16.
All inputs are finite; a program needn't handle non-finite values.
Results may differ from a plain program's by a relative error of at most 0.0028.
Values may be sent and summed in bfloat16 or wider, within the bound.
No kernel may reach another device: no remote copies, remote signals or barrier semaphores. Data moves between devices by JAX's collectives and lax.ppermute only.
A program may use at most 128 MiB of HBM per device.

v0:
```python
import jax
import jax.numpy as jnp
from jax import lax
from jax.experimental import pallas as pl
from jax.experimental.pallas import tpu as pltpu
from jax.sharding import PartitionSpec as P

CAP = 32
ITERS = 3
HIGHEST = lax.Precision.HIGHEST
BF16 = jnp.bfloat16
F32 = jnp.float32


def matmul(left, right, dims):
    return lax.dot_general(left, right, (dims, ((), ())), preferred_element_type=F32)


def near_kernel(table, *refs):
    blocks, received, hot, weights, factors, out, panels, total = refs[6:]
    step = pl.program_id(0)
    rows = total.shape[2]
    per_dev = total.shape[0]
    share = received.shape[1] - CAP

    @pl.when(step == 0)
    def start():
        for place, ref in enumerate(refs[:6]):
            for half in range(per_dev):
                panels[place * per_dev + half] = ref[:, half * rows : (half + 1) * rows]
        values = received[:, :CAP, :].reshape(-1, received.shape[2])
        traced = matmul(values, hot[...], ((0,), (0,)))
        first = pl.multiple_of(table[table.shape[0] - 1], share)
        for half in range(per_dev):
            total[half] = traced[:, half * rows : (half + 1) * rows]
            mixed = jnp.zeros((share, received.shape[2]), F32)
            for bank in range(received.shape[0]):
                mixed = mixed + weights[bank, half : half + 1, :] * received[bank, CAP:, :].astype(
                    F32
                )
            upper = mixed.astype(BF16)
            lower = (mixed - upper.astype(F32)).astype(BF16)
            far = matmul(upper, factors[half], ((1,), (0,))) + matmul(
                lower, factors[half], ((1,), (0,))
            )
            total[half, pl.ds(first, share), :] += far

    for half in range(per_dev):
        place = table[half * pl.num_programs(0) + step]
        total[half] += matmul(panels[place], blocks[half, 0], ((1,), (0,)))

    @pl.when(step == pl.num_programs(0) - 1)
    def finish():
        for half in range(per_dev):
            out[:, half * rows : (half + 1) * rows] = total[half].astype(BF16)


def near_call(table, parts, near_blocks, received, hot, weights, factors):
    per_dev, group, rows, _ = near_blocks.shape
    excitations = parts[0].shape[0]

    def whole(x):
        return pl.BlockSpec(x.shape, lambda *_: (0,) * x.ndim, pipeline_mode=pl.Buffered(1))

    return pl.pallas_call(
        near_kernel,
        out_shape=jax.ShapeDtypeStruct((excitations, per_dev * rows), BF16),
        grid_spec=pltpu.PrefetchScalarGridSpec(
            num_scalar_prefetch=1,
            grid=(group,),
            in_specs=[whole(x) for x in parts]
            + [pl.BlockSpec((per_dev, 1, rows, rows), lambda k, _: (0, k, 0, 0))]
            + [whole(x) for x in (received, hot, weights, factors)],
            out_specs=pl.BlockSpec((excitations, per_dev * rows), lambda k, _: (0, 0)),
            scratch_shapes=[
                pltpu.VMEM((6 * per_dev, excitations, rows), BF16),
                pltpu.VMEM((per_dev, excitations, rows), F32),
            ],
        ),
        compiler_params=pltpu.CompilerParams(vmem_limit_bytes=24 << 20),
        cost_estimate=pl.CostEstimate(
            flops=2 * excitations * per_dev * group * rows * rows,
            bytes_accessed=2 * per_dev * group * rows * rows,
            transcendentals=0,
        ),
        name="near",
    )(table, *parts, near_blocks, received, hot, weights, factors)


def fem_kernel(state, source, inverse, spread, returned, low0, high0, low1, high1, *refs):
    out, padded, coupled = refs[0], refs[-2], refs[-1]
    cx, cy, cz, lanes = state.shape
    coupled[...] = matmul(spread[...], returned[...], ((1,), (0,)))
    padded[0, 1 : cy + 1] = low0[...].astype(F32)
    padded[cx + 1, 1 : cy + 1] = high0[...].astype(F32)
    for i in range(cx):
        padded[i + 1, 0] = low1[i].astype(F32)
        padded[i + 1, 1 : cy + 1] = state[i]
        padded[i + 1, cy + 1] = high1[i].astype(F32)
    depth = lax.broadcasted_iota(jnp.int32, (cz, lanes), 0)

    def plane(m, carry):
        i, j = m // cy, m % cy
        here = padded[i + 1, j + 1]
        beside = padded[i + 2, j + 1] + padded[i, j + 1]
        beside = beside + padded[i + 1, j + 2] + padded[i + 1, j]
        beside = beside + jnp.where(depth == cz - 1, 0.0, pltpu.roll(here, cz - 1, 0))
        beside = beside + jnp.where(depth == 0, 0.0, pltpu.roll(here, 1, 0))
        first = pl.multiple_of(m * cz, cz)
        value = source[i, j] + beside - coupled[pl.ds(first, cz), :]
        out[i, j] = value * inverse[i, j]
        return carry

    lax.fori_loop(0, cx * cy, plane, 0, unroll=4)
    if len(refs) > 3:
        take = refs[1]
        values, edge0l, edge0h, edge1l, edge1h = refs[2:7]
        narrow = out[...].reshape(cx * cy * cz, lanes).astype(BF16)
        values[...] = matmul(take[...], narrow, ((1,), (0,))).astype(BF16)
        edge0l[...] = out[0].astype(BF16)
        edge0h[...] = out[cx - 1].astype(BF16)
        for i in range(cx):
            edge1l[i] = out[i, 0].astype(BF16)
            edge1h[i] = out[i, cy - 1].astype(BF16)


def fem_body_last(*refs):
    fem_kernel(*refs)


def fem_body(*refs):
    fem_kernel(*refs[:9], refs[10], refs[9], *refs[11:])


def fem_call(state, source, inverse, spread, returned, halos, take, last):
    cx, cy, cz, lanes = state.shape
    outs = [jax.ShapeDtypeStruct(state.shape, F32)]
    ins = [state, source, inverse, spread, returned, *halos]
    if not last:
        ins.append(take)
        outs.append(jax.ShapeDtypeStruct((take.shape[0], lanes), BF16))
        outs += [jax.ShapeDtypeStruct((cy, cz, lanes), BF16)] * 2
        outs += [jax.ShapeDtypeStruct((cx, cz, lanes), BF16)] * 2
    vmem = pl.BlockSpec(memory_space=pltpu.VMEM)
    return pl.pallas_call(
        fem_body_last if last else fem_body,
        out_shape=outs,
        in_specs=[vmem] * len(ins),
        out_specs=[vmem] * len(outs),
        scratch_shapes=[
            pltpu.VMEM((cx + 2, cy + 2, cz, lanes), F32),
            pltpu.VMEM((cx * cy * cz, lanes), F32),
        ],
        compiler_params=pltpu.CompilerParams(vmem_limit_bytes=32 << 20),
        cost_estimate=pl.CostEstimate(
            flops=4 * spread.size * lanes, bytes_accessed=8 << 20, transcendentals=0
        ),
        name="fem_last" if last else "fem_step",
    )(*ins)


def exchange(x, axis):
    return lax.all_to_all(x, axis, split_axis=0, concat_axis=0, tiled=True)


def along(x, axis, shift):
    size = lax.axis_size(axis)
    pairs = [(i, i + shift) for i in range(size) if 0 <= i + shift < size]
    return lax.ppermute(x, axis, pairs)


def around(x, axis, shift):
    size = lax.axis_size(axis)
    return lax.ppermute(x, axis, [(i, (i + shift) % size) for i in range(size)])


def partner(x, axis):
    return lax.ppermute(x, axis, [(i, i ^ 1) for i in range(lax.axis_size(axis))])


def shards(
    fem_field,
    fem_source,
    reaction,
    bem_density,
    bem_source,
    bem_diagonal,
    near_blocks,
    near_pairs,
    low_left,
    low_right,
    centers,
    trace_cell,
    trace_bank,
    trace_row,
):
    fem_count = lax.axis_size("fem")
    bem_count = lax.axis_size("bem")
    fem_rank = lax.axis_index("fem")
    bem_rank = lax.axis_index("bem")
    excitations, local_rows = bem_density.shape
    share = excitations // fem_count
    per_dev, group, panel_rows, _ = near_blocks.shape
    panel_total, rank, _ = low_right.shape
    cells = reaction.size
    slots = trace_cell.shape[0]
    places = bem_count * CAP
    first_col = fem_rank * share
    own_first = bem_rank * per_dev

    bank = trace_bank[:, 0]
    order = jnp.arange(slots, dtype=jnp.int32)
    earlier = (bank[:, None] == bank[None, :]) & (order[:, None] < order[None, :])
    place = bank * CAP + jnp.sum(earlier.astype(jnp.int32), axis=0)
    hit = jnp.arange(places, dtype=jnp.int32)[:, None] == place[None, :]
    row_code = jnp.sum(jnp.where(hit, trace_row[None, :] + 1, 0), axis=1)
    cell_code = jnp.sum(jnp.where(hit, trace_cell[None, :] + 1, 0), axis=1)
    cell_ids = jnp.arange(1, cells + 1, dtype=jnp.int32)
    take = (cell_code[:, None] == cell_ids[None, :]).astype(BF16)
    spread = (cell_ids[:, None] == cell_code[None, :]).astype(BF16)

    own_centers = lax.dynamic_slice_in_dim(centers, own_first, per_dev, 0)
    offsets = own_centers[:, None, :] - centers[None, :, :]
    kernel_rows = 1.0 / (1.0 + jnp.sum(offsets * offsets, axis=-1))
    panel_ids = jnp.arange(panel_total, dtype=jnp.int32)
    own_ids = own_first + jnp.arange(per_dev, dtype=jnp.int32)
    listed = jnp.any(near_pairs[:, :, None] == panel_ids[None, None, :], axis=1)
    listed = listed | (own_ids[:, None] == panel_ids[None, :])
    kernel_rows = jnp.where(listed, 0.0, kernel_rows)
    weights = jnp.repeat(kernel_rows.reshape(per_dev, bem_count, per_dev), rank, axis=2)
    weights = jnp.pad(weights.transpose(1, 0, 2), ((0, 0), (0, 0), (0, 128 - per_dev * rank)))
    factors = jnp.concatenate([low_left] * per_dev, axis=1)
    factors = jnp.pad(factors, ((0, 0), (0, 128 - per_dev * rank), (0, 0)))
    own_right = lax.dynamic_slice_in_dim(low_right, own_first, per_dev, 0)

    sources = lax.dynamic_slice_in_dim(near_pairs, fem_rank * group, group, 1)
    source_bank = sources // per_dev
    chip = jnp.mod(source_bank // 2 - bem_rank // 2 + 1, bem_count // 2)
    other = (source_bank + bem_rank) % 2
    table = ((chip * 2 + other) * per_dev + sources % per_dev).reshape(-1)
    table = jnp.concatenate([table, first_col[None]]).astype(jnp.int32)

    inverse = jnp.broadcast_to((1.0 / (6.0 + reaction))[..., None], fem_field.shape)
    density = lax.dynamic_slice_in_dim(bem_density, first_col, share, 0)
    source_part = lax.dynamic_slice_in_dim(bem_source, first_col, share, 0)
    diag_row = bem_diagonal[None, :]

    def moments(narrow):
        grouped = narrow.reshape(share, per_dev, panel_rows)
        reduced = jnp.einsum("eqn,qrn->eqr", grouped, own_right, preferred_element_type=F32)
        return reduced.astype(BF16).reshape(share, per_dev * rank)

    narrow = density.astype(BF16)
    full = bem_density.astype(BF16)
    fem_state = fem_field
    edges = (fem_field[0], fem_field[-1], fem_field[:, 0], fem_field[:, -1])
    edges = [x.astype(BF16) for x in edges]
    values = matmul(take, fem_field.reshape(cells, excitations).astype(BF16), ((1,), (0,)))
    values = values.astype(BF16)
    digits = jnp.stack([row_code // 32, row_code % 32]).reshape(2, bem_count, CAP)
    digits = digits.transpose(1, 0, 2).reshape(bem_count, 1, 2 * CAP).astype(BF16)
    digits = jnp.pad(digits, ((0, 0), (0, share - 1), (0, 0)))
    hot = None
    for sweep in range(ITERS):
        if sweep > 0:
            copies = jnp.broadcast_to(narrow, (fem_count, share, local_rows))
            full = exchange(copies, "fem").reshape(excitations, local_rows)
        far = jnp.broadcast_to(moments(narrow), (bem_count, share, per_dev * rank))
        tail = digits if sweep == 0 else jnp.zeros_like(digits)
        far = jnp.concatenate([far, tail], axis=2)
        sent = jnp.concatenate([values.reshape(bem_count, CAP, excitations), far], axis=1)
        received = exchange(sent, "bem")
        if hot is None:
            coded = received[:, CAP, 2 * CAP :].astype(F32)
            rows = (coded[:, :CAP] * 32.0 + coded[:, CAP:]).astype(jnp.int32).reshape(-1)
            hot = (rows[:, None] == jnp.arange(1, local_rows + 1, dtype=jnp.int32)).astype(BF16)
        left = around(full, "bem", 2)
        right = around(full, "bem", -2)
        parts = [
            left,
            partner(left, "bem"),
            full,
            partner(full, "bem"),
            right,
            partner(right, "bem"),
        ]
        picked = matmul(hot, full, ((1,), (1,))).astype(BF16)
        returned = exchange(picked.reshape(bem_count, CAP, excitations), "bem")
        low0 = along(edges[1], "fem", 1)
        high0 = along(edges[0], "fem", -1)
        low1 = along(edges[3], "bem", 1)
        high1 = along(edges[2], "bem", -1)
        partial = near_call(table, parts, near_blocks, received, hot, weights, factors)
        summed = exchange(partial.reshape(fem_count, share, local_rows), "fem")
        applied = summed.astype(F32).sum(axis=0)
        last = sweep == ITERS - 1
        fem_state, *rest = fem_call(
            fem_state,
            fem_source,
            inverse,
            spread,
            returned.reshape(places, excitations),
            (low0, high0, low1, high1),
            take,
            last,
        )
        density = density + (source_part - applied) / diag_row
        if not last:
            narrow = density.astype(BF16)
            values, *edges = rest
    return (fem_state, density)


def solution(mesh):
    return jax.shard_map(
        shards,
        mesh=mesh,
        in_specs=(
            P("fem", "bem", None, None),
            P("fem", "bem", None, None),
            P("fem", "bem", None),
            P(None, "bem"),
            P(None, "bem"),
            P("bem"),
            P("bem", "fem", None, None),
            P("bem", None),
            P("bem", None, None),
            P(),
            P(),
            P(("fem", "bem")),
            P(("fem", "bem"), None),
            P(("fem", "bem")),
        ),
        out_specs=(P("fem", "bem", None, None), P("fem", "bem")),
        check_vma=False,
    )
```

profile of v0, /device:TPU:99, one launch (start us, length us, event | category | flops | bytes accessed | tf_op | source)
XLA Modules:
  0.0 256.6 jit_solution(74892408067273646)
XLA Ops:
  12.1 7.4 %all-to-all-start = ((bf16[16,48,128]{2,1,0:T(8,128)(2,1)}), bf16[16,48,128]{2,1,0:T(8,128)(2,1)}, u32[]{:S(2)}, u32[]{:S(2)}) async-start(bf16[16,48,128]{2,1,0:T(8,128)(2,1)} %fusion.41), calls=%async_computation | async-start | bytes 393216 | tf_op jit(solution)/shard_map/all_to_all | solution.py:163
  23.4 3.9 %collective-permute-start.1 = (bf16[8,32,128]{2,1,0:T(8,128)(2,1)}, bf16[8,32,128]{2,1,0:T(8,128)(2,1)}, u32[]{:S(2)}, u32[]{:S(2)}) collective-permute-start(bf16[8,32,128]{2,1,0:T(8,128)(2,1)} %get-tuple-element.36), channel_id=1, source_target_pairs={{16,0},{32,16},{48,32},{64,48},{80,64},{96,80},{112,96},{17,1},{33... | collective-permute-start | bytes 196616 | tf_op jit(solution)/shard_map/ppermute | solution.py:169
  33.0 4.9 %collective-permute-start.2 = (bf16[8,32,128]{2,1,0:T(8,128)(2,1)}, bf16[8,32,128]{2,1,0:T(8,128)(2,1)}, u32[]{:S(2)}, u32[]{:S(2)}) collective-permute-start(bf16[8,32,128]{2,1,0:T(8,128)(2,1)} %get-tuple-element.35), channel_id=1, source_target_pairs={{0,1},{1,2},{2,3},{3,4},{4,5},{5,6},{6,7},{7,8},{8,9},{9,10},{10,1... | collective-permute-start | bytes 196616 | tf_op jit(solution)/shard_map/ppermute | solution.py:169
  42.6 4.9 %near.3 = bf16[128,1024]{1,0:T(8,128)(2,1)S(1)} custom-call(s32[13]{0:T(128)S(1)} %pad_add_fusion.table, bf16[128,1024]{1,0:T(8,128)(2,1)} %collective-permute-done.4.refs_0_, bf16[128,1024]{1,0:T(8,128)(2,1)} %collective-permute-done.5.refs_1_, bf16[128,1024]{1,0:T(8,128)(2,1)} %convert_element_type.128.refs_2_, ...), custom_call_target="tpu_custom_call" | custom-call | flops 805306368 | bytes 6291456 | tf_op jit(solution)/shard_map/near/pallas_call | solution.py:65
  48.2 4.4 %all-to-all-start.2 = ((bf16[8,16,1024]{2,1,0:T(8,128)(2,1)}), bf16[8,16,1024]{2,1,0:T(8,128)(2,1)}, u32[]{:S(2)}, u32[]{:S(2)}) async-start(bf16[8,16,1024]{2,1,0:T(8,128)(2,1)} %bitcast.54), calls=%async_computation.2 | async-start | bytes 524288 | tf_op jit(solution)/shard_map/all_to_all | solution.py:163
  54.3 4.2 %all-to-all-done.2 = bf16[8,16,1024]{2,1,0:T(8,128)(2,1)} async-done(((bf16[8,16,1024]{2,1,0:T(8,128)(2,1)}), bf16[8,16,1024]{2,1,0:T(8,128)(2,1)}, u32[]{:S(2)}, u32[]{:S(2)}) %all-to-all-start.2) | async-done | bytes 262176 | tf_op jit(solution)/shard_map/all_to_all | solution.py:163
  62.4 5.1 %all-to-all-start.3 = ((bf16[8,16,1024]{2,1,0:T(8,128)(2,1)}), bf16[8,16,1024]{2,1,0:T(8,128)(2,1)}, u32[]{:S(2)}, u32[]{:S(2)}) async-start(bf16[8,16,1024]{2,1,0:T(8,128)(2,1)} %broadcast_in_dim.75), calls=%async_computation.3 | async-start | bytes 524288 | tf_op jit(solution)/shard_map/all_to_all | solution.py:163
  72.8 7.9 %all-to-all-start.1 = ((bf16[16,32,128]{2,1,0:T(8,128)(2,1)}), bf16[16,32,128]{2,1,0:T(8,128)(2,1)S(1)}, u32[]{:S(2)}, u32[]{:S(2)}) async-start(bf16[16,32,128]{2,1,0:T(8,128)(2,1)} %bitcast.64), calls=%async_computation.1 | async-start | bytes 262144 | tf_op jit(solution)/shard_map/all_to_all | solution.py:163
  92.0 4.5 %fem_step.2 = (f32[8,8,32,128]{3,2,1,0:T(8,128)S(1)}, bf16[512,128]{1,0:T(8,128)(2,1)S(1)}, bf16[8,32,128]{2,1,0:T(8,128)(2,1)S(1)}, bf16[8,32,128]{2,1,0:T(8,12...) custom-call(f32[8,8,32,128]{3,2,1,0:T(8,128)S(1)} %copy-done.15, ...), custom_call_target="tpu_custom_call" | custom-call | flops 536870912 | bytes 8388608 | tf_op jit(solution)/shard_map/fem_step/pallas_call | solution.py:145
  102.7 12.2 %all_to_all.55.refs_7_ = bf16[16,48,128]{2,1,0:T(8,128)(2,1)S(1)} all-to-all(bf16[16,48,128]{2,1,0:T(8,128)(2,1)S(1)} %fusion.42), channel_id=1, replica_groups=mesh['fem'=8,'bem'=16] {'bem'}, dimensions={0} | all-to-all | bytes 393216 | tf_op jit(solution)/shard_map/all_to_all | solution.py:163
  119.5 4.5 %near.4 = bf16[128,1024]{1,0:T(8,128)(2,1)S(1)} custom-call(s32[13]{0:T(128)S(1)} %copy-done.26, bf16[128,1024]{1,0:T(8,128)(2,1)} %collective-permute-done.13.refs_0_, bf16[128,1024]{1,0:T(8,128)(2,1)S(1)} %collective-permute-done.14.refs_1_, bf16[128,1024]{1,0:T(8,128)(2,1)} %bitcast.15.refs_2_, bf16[128,1024]{1,0:T(8,128)(2,1)S(1)} %collective-permute-done.15.refs_3_, ...), custom_call_target="tpu_custom_call" | custom-call | flops 805306368 | bytes 6291456 | tf_op jit(solution)/shard_map/near/pallas_call | solution.py:65
  124.7 5.3 %all-to-all-start.6 = ((bf16[8,16,1024]{2,1,0:T(8,128)(2,1)}), bf16[8,16,1024]{2,1,0:T(8,128)(2,1)}, u32[]{:S(2)}, u32[]{:S(2)}) async-start(bf16[8,16,1024]{2,1,0:T(8,128)(2,1)} %bitcast.55), calls=%async_computation.6 | async-start | bytes 524288 | tf_op jit(solution)/shard_map/all_to_all | solution.py:163
  135.6 5.8 %all-to-all-start.4 = ((bf16[16,32,128]{2,1,0:T(8,128)(2,1)}), bf16[16,32,128]{2,1,0:T(8,128)(2,1)S(1)}, u32[]{:S(2)}, u32[]{:S(2)}) async-start(bf16[16,32,128]{2,1,0:T(8,128)(2,1)} %bitcast.66), calls=%async_computation.4 | async-start | bytes 262144 | tf_op jit(solution)/shard_map/all_to_all | solution.py:163
  144.0 3.6 %all-to-all-done.4 = bf16[16,32,128]{2,1,0:T(8,128)(2,1)S(1)} async-done(((bf16[16,32,128]{2,1,0:T(8,128)(2,1)}), bf16[16,32,128]{2,1,0:T(8,128)(2,1)S(1)}, u32[]{:S(2)}, u32[]{:S(2)}) %all-to-all-start.4) | async-done | bytes 131104 | tf_op jit(solution)/shard_map/all_to_all | solution.py:163
  149.1 5.4 %all-to-all-start.7 = ((bf16[8,16,1024]{2,1,0:T(8,128)(2,1)}), bf16[8,16,1024]{2,1,0:T(8,128)(2,1)}, u32[]{:S(2)}, u32[]{:S(2)}) async-start(bf16[8,16,1024]{2,1,0:T(8,128)(2,1)} %broadcast_in_dim.77), calls=%async_computation.7 | async-start | bytes 524288 | tf_op jit(solution)/shard_map/all_to_all | solution.py:163
  157.6 4.6 %collective-permute-start.11 = (bf16[8,32,128]{2,1,0:T(8,128)(2,1)}, bf16[8,32,128]{2,1,0:T(8,128)(2,1)S(1)}, u32[]{:S(2)}, u32[]{:S(2)}) collective-permute-start(bf16[8,32,128]{2,1,0:T(8,128)(2,1)} %copy-done.34), channel_id=1, source_target_pairs={{0,1},{1,2},{2,3},{3,4},{4,5},{5,6},{6,7},{7,8},{8,9},{9,10},{10,1... | collective-permute-start | bytes 196616 | tf_op jit(solution)/shard_map/ppermute | solution.py:169
  166.1 5.5 %collective-permute-done.12.refs_8_ = bf16[8,32,128]{2,1,0:T(8,128)(2,1)S(1)} collective-permute-done((bf16[8,32,128]{2,1,0:T(8,128)(2,1)}, bf16[8,32,128]{2,1,0:T(8,128)(2,1)S(1)}, u32[]{:S(2)}, u32[]{:S(2)}) %collective-permute-start.12) | collective-permute-done | bytes 65568 | tf_op jit(solution)/shard_map/ppermute | solution.py:169
  188.2 11.2 %all-to-all-start.9 = ((bf16[16,48,128]{2,1,0:T(8,128)(2,1)}), bf16[16,48,128]{2,1,0:T(8,128)(2,1)}, u32[]{:S(2)}, u32[]{:S(2)}) async-start(bf16[16,48,128]{2,1,0:T(8,128)(2,1)} %fusion.43), calls=%async_computation.9 | async-start | bytes 393216 | tf_op jit(solution)/shard_map/all_to_all | solution.py:163
  202.4 4.0 %all-to-all-done.9.refs_7_ = bf16[16,48,128]{2,1,0:T(8,128)(2,1)} async-done(((bf16[16,48,128]{2,1,0:T(8,128)(2,1)}), bf16[16,48,128]{2,1,0:T(8,128)(2,1)}, u32[]{:S(2)}, u32[]{:S(2)}) %all-to-all-start.9) | async-done | bytes 196640 | tf_op jit(solution)/shard_map/all_to_all | solution.py:163
  206.4 5.5 %all-to-all-start.8 = ((bf16[16,32,128]{2,1,0:T(8,128)(2,1)}), bf16[16,32,128]{2,1,0:T(8,128)(2,1)S(1)}, u32[]{:S(2)}, u32[]{:S(2)}) async-start(bf16[16,32,128]{2,1,0:T(8,128)(2,1)} %bitcast.65), calls=%async_computation.8 | async-start | bytes 262144 | tf_op jit(solution)/shard_map/all_to_all | solution.py:163
  216.5 4.9 %near.5 = bf16[128,1024]{1,0:T(8,128)(2,1)S(1)} custom-call(s32[13]{0:T(128)S(1)} %copy-done.27, bf16[128,1024]{1,0:T(8,128)(2,1)} %collective-permute-done.22.refs_0_, bf16[128,1024]{1,0:T(8,128)(2,1)} %collective-permute-done.23.refs_1_, bf16[128,1024]{1,0:T(8,128)(2,1)} %bitcast.21.refs_2_, bf16[128,1024]{1,0:T(8,128)(2,1)} %collective-permute-done.24.refs_3_, ...), custom_call_target="tpu_custom_call" | custom-call | flops 805306368 | bytes 6291456 | tf_op jit(solution)/shard_map/near/pallas_call | solution.py:65
  222.1 4.3 %all-to-all-start.10 = ((bf16[8,16,1024]{2,1,0:T(8,128)(2,1)}), bf16[8,16,1024]{2,1,0:T(8,128)(2,1)}, u32[]{:S(2)}, u32[]{:S(2)}) async-start(bf16[8,16,1024]{2,1,0:T(8,128)(2,1)} %bitcast.53), calls=%async_computation.10 | async-start | bytes 524288 | tf_op jit(solution)/shard_map/all_to_all | solution.py:163
  232.6 6.0 %collective-permute-start.20 = (bf16[8,32,128]{2,1,0:T(8,128)(2,1)}, bf16[8,32,128]{2,1,0:T(8,128)(2,1)S(1)}, u32[]{:S(2)}, u32[]{:S(2)}) collective-permute-start(bf16[8,32,128]{2,1,0:T(8,128)(2,1)} %copy-done.29), channel_id=1, source_target_pairs={{0,1},{1,2},{2,3},{3,4},{4,5},{5,6},{6,7},{7,8},{8,9},{9,10},{10,1... | collective-permute-start | bytes 196616 | tf_op jit(solution)/shard_map/ppermute | solution.py:169
  240.5 7.4 %collective-permute-done.21.refs_8_ = bf16[8,32,128]{2,1,0:T(8,128)(2,1)S(1)} collective-permute-done((bf16[8,32,128]{2,1,0:T(8,128)(2,1)}, bf16[8,32,128]{2,1,0:T(8,128)(2,1)S(1)}, u32[]{:S(2)}, u32[]{:S(2)}) %collective-permute-start.21) | collective-permute-done | bytes 65568 | tf_op jit(solution)/shard_map/ppermute | solution.py:169
  (220 shorter events, 117.8 us)
Async XLA Ops:
  2.5 28.9 %collective-permute-start.4 = (bf16[128,1024]{1,0:T(8,128)(2,1)}, bf16[128,1024]{1,0:T(8,128)(2,1)}, u32[]{:S(2)}, u32[]{:S(2)}) collective-permute-start(bf16[128,1024]{1,0:T(8,128)(2,1)} %convert_element_type.128.refs_2_), channel_id=1, source_target_pairs={{0,2},{1,3},{2,4},{3,5},{4,6},{5,7},{6,8},{7,9},{8,10},{9,11},{10,... | collective-permute-start | bytes 786440 | tf_op jit(solution)/shard_map/ppermute | solution.py:174
  4.1 28.4 %collective-permute-start.7 = (bf16[128,1024]{1,0:T(8,128)(2,1)}, bf16[128,1024]{1,0:T(8,128)(2,1)}, u32[]{:S(2)}, u32[]{:S(2)}) collective-permute-start(bf16[128,1024]{1,0:T(8,128)(2,1)} %convert_element_type.128.refs_2_), channel_id=1, source_target_pairs={{0,14},{1,15},{2,0},{3,1},{4,2},{5,3},{6,4},{7,5},{8,6},{9,7},{10,... | collective-permute-start | bytes 786440 | tf_op jit(solution)/shard_map/ppermute | solution.py:174
  4.1 28.9 %collective-permute-start.6 = (bf16[128,1024]{1,0:T(8,128)(2,1)}, bf16[128,1024]{1,0:T(8,128)(2,1)}, u32[]{:S(2)}, u32[]{:S(2)}) collective-permute-start(bf16[128,1024]{1,0:T(8,128)(2,1)} %convert_element_type.128.refs_2_), channel_id=1, source_target_pairs={{0,1},{1,0},{2,3},{3,2},{4,5},{5,4},{6,7},{7,6},{8,9},{9,8},{10,11... | collective-permute-start | bytes 786440 | tf_op jit(solution)/shard_map/ppermute | solution.py:178
  12.1 18.5 %all-to-all-start = ((bf16[16,48,128]{2,1,0:T(8,128)(2,1)}), bf16[16,48,128]{2,1,0:T(8,128)(2,1)}, u32[]{:S(2)}, u32[]{:S(2)}) async-start(bf16[16,48,128]{2,1,0:T(8,128)(2,1)} %fusion.41), calls=%async_computation | async-start | bytes 393216 | tf_op jit(solution)/shard_map/all_to_all | solution.py:163
  21.1 63.7 %collective-permute-start = (bf16[8,32,128]{2,1,0:T(8,128)(2,1)}, bf16[8,32,128]{2,1,0:T(8,128)(2,1)}, u32[]{:S(2)}, u32[]{:S(2)}) collective-permute-start(bf16[8,32,128]{2,1,0:T(8,128)(2,1)} %get-tuple-element.37), channel_id=1, source_target_pairs={{0,16},{16,32},{32,48},{48,64},{64,80},{80,96},{96,112},{1,17},{17... | collective-permute-start | bytes 196616 | tf_op jit(solution)/shard_map/ppermute | solution.py:169
  23.4 61.4 %collective-permute-start.1 = (bf16[8,32,128]{2,1,0:T(8,128)(2,1)}, bf16[8,32,128]{2,1,0:T(8,128)(2,1)}, u32[]{:S(2)}, u32[]{:S(2)}) collective-permute-start(bf16[8,32,128]{2,1,0:T(8,128)(2,1)} %get-tuple-element.36), channel_id=1, source_target_pairs={{16,0},{32,16},{48,32},{64,48},{80,64},{96,80},{112,96},{17,1},{33... | collective-permute-start | bytes 196616 | tf_op jit(solution)/shard_map/ppermute | solution.py:169
  33.0 51.8 %collective-permute-start.2 = (bf16[8,32,128]{2,1,0:T(8,128)(2,1)}, bf16[8,32,128]{2,1,0:T(8,128)(2,1)}, u32[]{:S(2)}, u32[]{:S(2)}) collective-permute-start(bf16[8,32,128]{2,1,0:T(8,128)(2,1)} %get-tuple-element.35), channel_id=1, source_target_pairs={{0,1},{1,2},{2,3},{3,4},{4,5},{5,6},{6,7},{7,8},{8,9},{9,10},{10,1... | collective-permute-start | bytes 196616 | tf_op jit(solution)/shard_map/ppermute | solution.py:169
  37.9 46.9 %collective-permute-start.3 = (bf16[8,32,128]{2,1,0:T(8,128)(2,1)}, bf16[8,32,128]{2,1,0:T(8,128)(2,1)}, u32[]{:S(2)}, u32[]{:S(2)}) collective-permute-start(bf16[8,32,128]{2,1,0:T(8,128)(2,1)} %get-tuple-element.34), channel_id=1, source_target_pairs={{1,0},{2,1},{3,2},{4,3},{5,4},{6,5},{7,6},{8,7},{9,8},{10,9},{11,1... | collective-permute-start | bytes 196616 | tf_op jit(solution)/shard_map/ppermute | solution.py:169
  72.8 14.1 %all-to-all-start.1 = ((bf16[16,32,128]{2,1,0:T(8,128)(2,1)}), bf16[16,32,128]{2,1,0:T(8,128)(2,1)S(1)}, u32[]{:S(2)}, u32[]{:S(2)}) async-start(bf16[16,32,128]{2,1,0:T(8,128)(2,1)} %bitcast.64), calls=%async_computation.1 | async-start | bytes 262144 | tf_op jit(solution)/shard_map/all_to_all | solution.py:163
  82.1 19.1 %collective-permute-start.13 = (bf16[128,1024]{1,0:T(8,128)(2,1)}, bf16[128,1024]{1,0:T(8,128)(2,1)}, u32[]{:S(2)}, u32[]{:S(2)}) collective-permute-start(bf16[128,1024]{1,0:T(8,128)(2,1)} %bitcast.15.refs_2_), channel_id=1, source_target_pairs={{0,2},{1,3},{2,4},{3,5},{4,6},{5,7},{6,8},{7,9},{8,10},{9,11},{10,... | collective-permute-start | bytes 786440 | tf_op jit(solution)/shard_map/ppermute | solution.py:174
  84.8 16.6 %collective-permute-start.16 = (bf16[128,1024]{1,0:T(8,128)(2,1)}, bf16[128,1024]{1,0:T(8,128)(2,1)}, u32[]{:S(2)}, u32[]{:S(2)}) collective-permute-start(bf16[128,1024]{1,0:T(8,128)(2,1)} %bitcast.15.refs_2_), channel_id=1, source_target_pairs={{0,14},{1,15},{2,0},{3,1},{4,2},{5,3},{6,4},{7,5},{8,6},{9,7},{10,... | collective-permute-start | bytes 786440 | tf_op jit(solution)/shard_map/ppermute | solution.py:174
  100.9 14.0 %collective-permute-start.15 = (bf16[128,1024]{1,0:T(8,128)(2,1)}, bf16[128,1024]{1,0:T(8,128)(2,1)S(1)}, u32[]{:S(2)}, u32[]{:S(2)}) collective-permute-start(bf16[128,1024]{1,0:T(8,128)(2,1)} %bitcast.15.refs_2_), channel_id=1, source_target_pairs={{0,1},{1,0},{2,3},{3,2},{4,5},{5,4},{6,7},{7,6},{8,9},{9,8},{10,11... | collective-permute-start | bytes 786440 | tf_op jit(solution)/shard_map/ppermute | solution.py:178
  101.2 13.6 %collective-permute-start.14 = (bf16[128,1024]{1,0:T(8,128)(2,1)}, bf16[128,1024]{1,0:T(8,128)(2,1)S(1)}, u32[]{:S(2)}, u32[]{:S(2)}) collective-permute-start(bf16[128,1024]{1,0:T(8,128)(2,1)} %collective-permute-done.13.refs_0_), channel_id=1, source_target_pairs={{0,1},{1,0},{2,3},{3,2},{4,5},{5,4},{6,7},{7,6},{8,9},{9,8},{10,11... | collective-permute-start | bytes 786440 | tf_op jit(solution)/shard_map/ppermute | solution.py:178
  101.4 13.5 %collective-permute-start.17 = (bf16[128,1024]{1,0:T(8,128)(2,1)}, bf16[128,1024]{1,0:T(8,128)(2,1)S(1)}, u32[]{:S(2)}, u32[]{:S(2)}) collective-permute-start(bf16[128,1024]{1,0:T(8,128)(2,1)} %collective-permute-done.16.refs_4_), channel_id=1, source_target_pairs={{0,1},{1,0},{2,3},{3,2},{4,5},{5,4},{6,7},{7,6},{8,9},{9,8},{10,11... | collective-permute-start | bytes 786440 | tf_op jit(solution)/shard_map/ppermute | solution.py:178
  135.6 12.0 %all-to-all-start.4 = ((bf16[16,32,128]{2,1,0:T(8,128)(2,1)}), bf16[16,32,128]{2,1,0:T(8,128)(2,1)S(1)}, u32[]{:S(2)}, u32[]{:S(2)}) async-start(bf16[16,32,128]{2,1,0:T(8,128)(2,1)} %bitcast.66), calls=%async_computation.4 | async-start | bytes 262144 | tf_op jit(solution)/shard_map/all_to_all | solution.py:163
  149.1 35.1 %all-to-all-start.7 = ((bf16[8,16,1024]{2,1,0:T(8,128)(2,1)}), bf16[8,16,1024]{2,1,0:T(8,128)(2,1)}, u32[]{:S(2)}, u32[]{:S(2)}) async-start(bf16[8,16,1024]{2,1,0:T(8,128)(2,1)} %broadcast_in_dim.77), calls=%async_computation.7 | async-start | bytes 524288 | tf_op jit(solution)/shard_map/all_to_all | solution.py:163
  184.2 15.6 %collective-permute-start.22 = (bf16[128,1024]{1,0:T(8,128)(2,1)}, bf16[128,1024]{1,0:T(8,128)(2,1)}, u32[]{:S(2)}, u32[]{:S(2)}) collective-permute-start(bf16[128,1024]{1,0:T(8,128)(2,1)} %bitcast.21.refs_2_), channel_id=1, source_target_pairs={{0,2},{1,3},{2,4},{3,5},{4,6},{5,7},{6,8},{7,9},{8,10},{9,11},{10,... | collective-permute-start | bytes 786440 | tf_op jit(solution)/shard_map/ppermute | solution.py:174
  184.2 15.8 %collective-permute-start.25 = (bf16[128,1024]{1,0:T(8,128)(2,1)}, bf16[128,1024]{1,0:T(8,128)(2,1)}, u32[]{:S(2)}, u32[]{:S(2)}) collective-permute-start(bf16[128,1024]{1,0:T(8,128)(2,1)} %bitcast.21.refs_2_), channel_id=1, source_target_pairs={{0,14},{1,15},{2,0},{3,1},{4,2},{5,3},{6,4},{7,5},{8,6},{9,7},{10,... | collective-permute-start | bytes 786440 | tf_op jit(solution)/shard_map/ppermute | solution.py:174
  188.2 18.1 %all-to-all-start.9 = ((bf16[16,48,128]{2,1,0:T(8,128)(2,1)}), bf16[16,48,128]{2,1,0:T(8,128)(2,1)}, u32[]{:S(2)}, u32[]{:S(2)}) async-start(bf16[16,48,128]{2,1,0:T(8,128)(2,1)} %fusion.43), calls=%async_computation.9 | async-start | bytes 393216 | tf_op jit(solution)/shard_map/all_to_all | solution.py:163
  199.4 12.4 %collective-permute-start.24 = (bf16[128,1024]{1,0:T(8,128)(2,1)}, bf16[128,1024]{1,0:T(8,128)(2,1)}, u32[]{:S(2)}, u32[]{:S(2)}) collective-permute-start(bf16[128,1024]{1,0:T(8,128)(2,1)} %bitcast.21.refs_2_), channel_id=1, source_target_pairs={{0,1},{1,0},{2,3},{3,2},{4,5},{5,4},{6,7},{7,6},{8,9},{9,8},{10,11... | collective-permute-start | bytes 786440 | tf_op jit(solution)/shard_map/ppermute | solution.py:178
  199.8 12.1 %collective-permute-start.23 = (bf16[128,1024]{1,0:T(8,128)(2,1)}, bf16[128,1024]{1,0:T(8,128)(2,1)}, u32[]{:S(2)}, u32[]{:S(2)}) collective-permute-start(bf16[128,1024]{1,0:T(8,128)(2,1)} %collective-permute-done.22.refs_0_), channel_id=1, source_target_pairs={{0,1},{1,0},{2,3},{3,2},{4,5},{5,4},{6,7},{7,6},{8,9},{9,8},{10,11... | collective-permute-start | bytes 786440 | tf_op jit(solution)/shard_map/ppermute | solution.py:178
  206.4 15.7 %all-to-all-start.8 = ((bf16[16,32,128]{2,1,0:T(8,128)(2,1)}), bf16[16,32,128]{2,1,0:T(8,128)(2,1)S(1)}, u32[]{:S(2)}, u32[]{:S(2)}) async-start(bf16[16,32,128]{2,1,0:T(8,128)(2,1)} %bitcast.65), calls=%async_computation.8 | async-start | bytes 262144 | tf_op jit(solution)/shard_map/all_to_all | solution.py:163
  222.1 31.9 %all-to-all-start.10 = ((bf16[8,16,1024]{2,1,0:T(8,128)(2,1)}), bf16[8,16,1024]{2,1,0:T(8,128)(2,1)}, u32[]{:S(2)}, u32[]{:S(2)}) async-start(bf16[8,16,1024]{2,1,0:T(8,128)(2,1)} %bitcast.53), calls=%async_computation.10 | async-start | bytes 524288 | tf_op jit(solution)/shard_map/all_to_all | solution.py:163
  226.4 14.1 %collective-permute-start.18 = (bf16[8,32,128]{2,1,0:T(8,128)(2,1)}, bf16[8,32,128]{2,1,0:T(8,128)(2,1)S(1)}, u32[]{:S(2)}, u32[]{:S(2)}) collective-permute-start(bf16[8,32,128]{2,1,0:T(8,128)(2,1)} %copy-done.31), channel_id=1, source_target_pairs={{0,16},{16,32},{32,48},{48,64},{64,80},{80,96},{96,112},{1,17},{17... | collective-permute-start | bytes 196616 | tf_op jit(solution)/shard_map/ppermute | solution.py:169
  (60 other events, 406.1 us)
where the time goes:
time: 260 us; the launch traced here: 257 us
  starting transfers between devices  111 us (43%)
  local copies, waits for them, and re-layouts  45.8 us (18%)
  waiting for transfers between devices  33.5 us (13%)
  Pallas kernels  24.3 us (9%)
  other arithmetic  20.6 us (8%)
  blocking collectives  12.2 us (5%)
  matrix products  8.2 us (3%)
    all_to_all x10, starting transfers between devices, exchange(): return lax.all_to_all(x, axis, split_axis=0, concat_axis=0, tiled=True)  62.4 us
    ppermute x12, starting transfers between devices, along(): return lax.ppermute(x, axis, pairs)  38.5 us
    unnamed x95, local copies, waits for them, and re-layouts  37.3 us
    all_to_all x10, waiting for transfers between devices, exchange(): return lax.all_to_all(x, axis, split_axis=0, concat_axis=0, tiled=True)  20.5 us
    pallas_call x3, Pallas kernels, near_call(): pl.pallas_call(near_kernel, out_shape=jax.ShapeDtypeStruct((excitations,...  14.2 us
    ppermute x12, waiting for transfers between devices, along(): return lax.ppermute(x, axis, pairs)  13 us
    all_to_all x1, blocking collectives, exchange(): return lax.all_to_all(x, axis, split_axis=0, concat_axis=0, tiled=True)  12.2 us
    pallas_call x3, Pallas kernels, fem_call(): pl.pallas_call(fem_body_last if last else fem_body, out_shape=outs, in_sp...  10.1 us
  transfers between devices with their start and end apart: 37, of which 8 were waited for; matrix products, arithmetic and copies ran while one was open for 13% of the time, Pallas kernels for 8%

commit v1 on v0

v1 whole, which is shorter than its diff:
```python
import functools

import jax
import jax.numpy as jnp
from jax import lax
from jax.experimental import pallas as pl
from jax.experimental.pallas import tpu as pltpu
from jax.sharding import PartitionSpec as P

CAP = 32
ITERS = 3
HIGHEST = lax.Precision.HIGHEST
BF16 = jnp.bfloat16
F32 = jnp.float32


def matmul(left, right, dims):
    return lax.dot_general(left, right, (dims, ((), ())), preferred_element_type=F32)


def kernel_call(body, args, outs, scratch, copies, flops, name, smem=()):
    hbm = pl.BlockSpec(memory_space=pltpu.HBM)
    scalar = pl.BlockSpec(memory_space=pltpu.SMEM)
    args = [*smem, *args]
    return pl.pallas_call(
        body,
        out_shape=outs,
        in_specs=[scalar] * len(smem) + [hbm] * (len(args) - len(smem)),
        out_specs=[hbm] * len(outs),
        scratch_shapes=[pltpu.VMEM(s, t) for s, t in scratch] + [pltpu.SemaphoreType.DMA((copies,))],
        compiler_params=pltpu.CompilerParams(vmem_limit_bytes=64 << 20),
        cost_estimate=pl.CostEstimate(
            flops=flops,
            bytes_accessed=sum(x.size * x.dtype.itemsize for x in args),
            transcendentals=0,
        ),
        name=name,
    )(*args)


class Copies:
    def __init__(self, sems):
        self.sems, self.count = sems, 0

    def start(self, source, target):
        copy = pltpu.make_async_copy(source, target, self.sems.at[self.count])
        self.count += 1
        copy.start()
        return copy


def near_body(table, *refs):
    parts = refs[:6]
    blocks, received, hot, weights, factors, out = refs[6:12]
    panels, held, got, mask, mix, factor, total, narrow, sems = refs[12:]
    per_dev, group, rows, _ = blocks.shape
    share = panels.shape[1] // 8
    copies = Copies(sems)
    small = [
        copies.start(received, got),
        copies.start(hot, mask),
        copies.start(weights, mix),
        copies.start(factors, factor),
    ]
    moved = []
    for place, ref in enumerate(parts):
        for half in range(per_dev):
            moved.append(
                copies.start(
                    ref.at[:, half * rows : (half + 1) * rows], panels.at[place * per_dev + half]
                )
            )
    loads = []
    for half in range(per_dev):
        for step in range(group):
            loads.append(copies.start(blocks.at[half, step], held.at[half * group + step]))
    for copy in small:
        copy.wait()
    values = got[:, :CAP, :].reshape(-1, got.shape[2])
    traced = matmul(values, mask[...], ((0,), (0,)))
    first = pl.multiple_of(table[table.shape[0] - 1], share)
    for half in range(per_dev):
        total[half] = traced[:, half * rows : (half + 1) * rows]
        mixed = jnp.zeros((share, got.shape[2]), F32)
        for bank in range(got.shape[0]):
            mixed = mixed + mix[bank, half : half + 1, :] * got[
                bank, got.shape[1] - share :, :
            ].astype(F32)
        upper = mixed.astype(BF16)
        lower = (mixed - upper.astype(F32)).astype(BF16)
        far = matmul(upper, factor[half], ((1,), (0,))) + matmul(lower, factor[half], ((1,), (0,)))
        total[half, pl.ds(first, share), :] += far
    for copy in moved:
        copy.wait()
    done = []
    for half in range(per_dev):
        summed = total[half]
        for step in range(group):
            loads[half * group + step].wait()
            place = table[half * group + step]
            summed = summed + matmul(panels[place], held[half * group + step], ((1,), (0,)))
        narrow[half] = summed.astype(BF16)
        done.append(copies.start(narrow.at[half], out.at[:, half * rows : (half + 1) * rows]))
    for copy in done:
        copy.wait()


def near_call(table, parts, near_blocks, received, hot, weights, factors):
    per_dev, group, rows, _ = near_blocks.shape
    excitations = parts[0].shape[0]
    (out,) = kernel_call(
        near_body,
        [*parts, near_blocks, received, hot, weights, factors],
        [jax.ShapeDtypeStruct((excitations, per_dev * rows), BF16)],
        [
            ((6 * per_dev, excitations, rows), BF16),
            ((per_dev * group, rows, rows), BF16),
            (received.shape, BF16),
            (hot.shape, BF16),
            (weights.shape, F32),
            (factors.shape, BF16),
            ((per_dev, excitations, rows), F32),
            ((per_dev, excitations, rows), BF16),
        ],
        4 + 6 * per_dev + per_dev * group + per_dev,
        2 * excitations * near_blocks.size // rows * rows,
        "near",
        smem=[table],
    )
    return out


def write_edges(state, take, values, edges, chosen, rims, parity, copies):
    cx, cy, cz, lanes = state.shape
    rims[0] = state[0].astype(BF16)
    rims[1] = state[cx - 1].astype(BF16)
    for i in range(cx):
        rims[2, i] = state[i, 0].astype(BF16)
        rims[3, i] = state[i, cy - 1].astype(BF16)
    done = [copies.start(rims.at[place], edges[k]) for k, place in enumerate(rim_places(parity))]
    narrow = state[...].reshape(cx * cy * cz, lanes).astype(BF16)
    chosen[...] = matmul(take[...], narrow, ((1,), (0,))).astype(BF16)
    if values is not None:
        done.append(copies.start(chosen, values))
    return done


def rim_places(parity):
    return (1 - parity[0], parity[0], 3 - parity[1], 2 + parity[1])


def setup_body(parity, first, *refs):
    bank, cell, row, state, density, right = refs[:6]
    sent, take, codes = refs[6:9]
    edges = refs[9:13]
    banks_v, cells_v, rows_v, here, share_v, factor, packed, picks, coded, chosen, rims, sems = refs[
        13:
    ]
    copies = Copies(sems)
    small = [copies.start(bank, banks_v), copies.start(cell, cells_v), copies.start(row, rows_v)]
    share = share_v.shape[0]
    start = pl.multiple_of(first[0], share)
    large = [
        copies.start(density.at[pl.ds(start, share)], share_v),
        copies.start(right.at[pl.ds(first[1], factor.shape[0])], factor),
        copies.start(state, here),
    ]
    for copy in small:
        copy.wait()
    slots, banks, lanes = bank.shape[1], sent.shape[0], sent.shape[2]
    places, cells = take.shape
    down = lax.broadcasted_iota(jnp.int32, (slots, slots), 0)
    over = lax.broadcasted_iota(jnp.int32, (slots, slots), 1)

    def column(x):
        return jnp.sum(jnp.where(down == over, x, 0), axis=1, keepdims=True)

    bank_r, cell_r, code_r = banks_v[...], cells_v[...] + 1, rows_v[...] + 1
    bank_c = column(bank_r)
    same = bank_c == bank_r
    place_r = bank_r * CAP + jnp.sum(
        jnp.where(same & (down < over), 1, 0), axis=0, keepdims=True
    )
    within_c = jnp.sum(jnp.where(same & (over < down), 1, 0), axis=1, keepdims=True)
    place_c = bank_c * CAP + within_c
    hit = lax.broadcasted_iota(jnp.int32, (places, slots), 0) == place_r
    cell_c = jnp.sum(jnp.where(hit, cell_r, 0), axis=1, keepdims=True)
    ids = lax.broadcasted_iota(jnp.int32, (places, cells), 1) + 1
    picks[...] = (cell_c == ids).astype(F32).astype(BF16)
    out = [copies.start(picks, take)]
    hit = lax.broadcasted_iota(jnp.int32, (slots, places), 1) == place_c
    coded[...] = jnp.sum(jnp.where(hit, column(cell_r), 0), axis=0, keepdims=True)
    out.append(copies.start(coded, codes))
    lane = lax.broadcasted_iota(jnp.int32, (slots, lanes), 1)
    named = lax.broadcasted_iota(jnp.int32, (banks, slots), 0) == bank_r
    digits = jnp.zeros((banks, lanes), F32)
    for digit, base in ((code_r // 32, lanes - 2 * CAP), (code_r % 32, lanes - CAP)):
        mine = jnp.where(named, digit, 0).astype(F32).astype(BF16)
        where = (lane == within_c + base).astype(F32).astype(BF16)
        digits = digits + matmul(mine, where, ((1,), (0,)))
    for copy in large:
        copy.wait()
    out += write_edges(here, picks, None, edges, chosen, rims, parity, copies)
    moment = moments(share_v[...].astype(BF16), factor)
    top = lax.broadcasted_iota(jnp.int32, moment.shape, 0) == 0
    packed[:, :CAP] = chosen[...].reshape(banks, CAP, lanes)
    for k in range(banks):
        packed[k, CAP:] = (moment + jnp.where(top, digits[k : k + 1], 0.0)).astype(BF16)
    out.append(copies.start(packed, sent))
    for copy in out:
        copy.wait()


def moments(rounded, factor):
    per_dev, rank, rows = factor.shape
    sums = [
        matmul(rounded[:, q * rows : (q + 1) * rows], factor[q], ((1,), (1,)))
        for q in range(per_dev)
    ]
    sums.append(jnp.zeros((rounded.shape[0], 128 - per_dev * rank), F32))
    return jnp.concatenate(sums, axis=1)


def setup_call(parity, first, bank, cell, row, state, density, right, banks, share, per_dev):
    cx, cy, cz, lanes = state.shape
    slots = bank.shape[1]
    take = jax.ShapeDtypeStruct((banks * CAP, cx * cy * cz), BF16)
    return kernel_call(
        setup_body,
        [bank, cell, row, state, density, right],
        [
            jax.ShapeDtypeStruct((banks, CAP + share, lanes), BF16),
            take,
            jax.ShapeDtypeStruct((1, banks * CAP), jnp.int32),
        ]
        + edge_shapes(state),
        [
            ((1, slots), jnp.int32),
            ((1, slots), jnp.int32),
            ((1, slots), jnp.int32),
            (state.shape, F32),
            ((share, density.shape[1]), F32),
            ((per_dev, *right.shape[1:]), BF16),
            ((banks, CAP + share, lanes), BF16),
            (take.shape, BF16),
            ((1, banks * CAP), jnp.int32),
            ((banks * CAP, lanes), BF16),
            ((4, cx, cz, lanes), BF16),
        ],
        13,
        2 * take.size * lanes,
        "setup",
        smem=[parity, first],
    )


def edge_shapes(state):
    cx, cy, cz, lanes = state.shape
    return [jax.ShapeDtypeStruct((cx, cz, lanes), BF16)] * 4


def fem_body(last, parity, *refs):
    state, source, inverse, spread, returned = refs[:5]
    halos = refs[5:9]
    if last:
        out = refs[9]
        padded, load, scale, wide, back, rim, coupled, fresh, sems = refs[10:]
    else:
        take, out, values = refs[9:12]
        edges = refs[12:16]
        padded, load, scale, wide, back, rim, coupled, fresh = refs[16:24]
        picks, chosen, rims, sems = refs[24:]
    cx, cy, cz, lanes = state.shape
    first_row = 0 if returned.shape[1] == CAP else CAP
    copies = Copies(sems)
    early = [
        copies.start(spread, wide),
        copies.start(returned.at[:, first_row : first_row + CAP], back),
    ]
    early_b = [
        copies.start(halos[k], rim.at[place]) for k, place in enumerate(rim_places(parity))
    ]
    early_b += [
        copies.start(state, padded.at[pl.ds(1, cx), pl.ds(1, cy)]),
        copies.start(source, load),
        copies.start(inverse, scale),
    ]
    if not last:
        picking = copies.start(take, picks)
    for copy in early:
        copy.wait()
    narrow = back[...].reshape(-1, lanes)
    coupled[...] = matmul(wide[...], narrow, ((1,), (0,)))
    for copy in early_b:
        copy.wait()
    padded[0, 1 : cy + 1] = rim[0].astype(F32)
    padded[cx + 1, 1 : cy + 1] = rim[1].astype(F32)
    for i in range(cx):
        padded[i + 1, 0] = rim[2, i].astype(F32)
        padded[i + 1, cy + 1] = rim[3, i].astype(F32)
    depth = lax.broadcasted_iota(jnp.int32, (cz, lanes), 0)

    def plane(m, carry):
        i, j = m // cy, m % cy
        here = padded[i + 1, j + 1]
        beside = padded[i + 2, j + 1] + padded[i, j + 1]
        beside = beside + padded[i + 1, j + 2] + padded[i + 1, j]
        beside = beside + jnp.where(depth == cz - 1, 0.0, pltpu.roll(here, cz - 1, 0))
        beside = beside + jnp.where(depth == 0, 0.0, pltpu.roll(here, 1, 0))
        first = pl.multiple_of(m * cz, cz)
        value = load[i, j] + beside - coupled[pl.ds(first, cz), :]
        fresh[i, j] = value * scale[i, j]
        return carry

    lax.fori_loop(0, cx * cy, plane, 0, unroll=4)
    done = [copies.start(fresh, out)]
    if not last:
        picking.wait()
        done += write_edges(fresh, picks, values, edges, chosen, rims, parity, copies)
    for copy in done:
        copy.wait()


def fem_call(parity, state, source, inverse, spread, returned, halos, take, last):
    cx, cy, cz, lanes = state.shape
    outs = [jax.ShapeDtypeStruct(state.shape, F32)]
    ins = [state, source, inverse, spread, returned, *halos]
    scratch = [
        ((cx + 2, cy + 2, cz, lanes), F32),
        (state.shape, F32),
        (state.shape, F32),
        (spread.shape, BF16),
        ((returned.shape[0], CAP, lanes), BF16),
        ((4, cx, cz, lanes), BF16),
        ((cx * cy * cz, lanes), F32),
        (state.shape, F32),
    ]
    if not last:
        ins.append(take)
        outs.append(jax.ShapeDtypeStruct((take.shape[0], lanes), BF16))
        outs += edge_shapes(state)
        scratch += [
            (take.shape, BF16),
            ((take.shape[0], lanes), BF16),
            ((4, cx, cz, lanes), BF16),
        ]
    return kernel_call(
        functools.partial(fem_body, last),
        ins,
        outs,
        scratch,
        16,
        4 * spread.size * lanes,
        "fem_last" if last else "fem_step",
        smem=[parity],
    )


def update_body(last, *refs):
    summed, density, source, diagonal = refs[:4]
    copies = None
    if last:
        out = refs[4]
        terms, here, load, scale, fresh, sems = refs[5:]
    else:
        right, out, spread, moment = refs[4:8]
        terms, here, load, scale, fresh, factor, narrow, short, sems = refs[8:]
    copies = Copies(sems)
    ins = [
        copies.start(summed, terms),
        copies.start(density, here),
        copies.start(source, load),
        copies.start(diagonal, scale),
    ]
    if not last:
        ins.append(copies.start(right, factor))
    for copy in ins:
        copy.wait()
    applied = jnp.sum(terms[...].astype(F32), axis=0)
    value = here[...] + (load[...] - applied) / scale[...]
    fresh[...] = value
    done = [copies.start(fresh, out)]
    if not last:
        rounded = value.astype(BF16)
        for k in range(narrow.shape[0]):
            narrow[k] = rounded
        done.append(copies.start(narrow, spread))
        short[...] = moments(rounded, factor).astype(BF16)
        done.append(copies.start(short, moment))
    for copy in done:
        copy.wait()


def update_call(summed, density, source, diagonal, right, last):
    outs = [jax.ShapeDtypeStruct(density.shape, F32)]
    ins = [summed, density, source, diagonal]
    scratch = [
        (summed.shape, BF16),
        (density.shape, F32),
        (density.shape, F32),
        (diagonal.shape, F32),
        (density.shape, F32),
    ]
    if not last:
        ins.append(right)
        outs += [
            jax.ShapeDtypeStruct(summed.shape, BF16),
            jax.ShapeDtypeStruct((density.shape[0], 128), BF16),
        ]
        scratch += [
            (right.shape, BF16),
            (summed.shape, BF16),
            ((density.shape[0], 128), BF16),
        ]
    return kernel_call(
        functools.partial(update_body, last),
        ins,
        outs,
        scratch,
        8,
        1 << 20,
        "update_last" if last else "update",
    )


def pick_body(joined, *refs):
    if joined:
        full, hot, values, moment, out = refs[:5]
        whole, mask, chosen, short, packed, sems = refs[5:]
    else:
        full, hot, out = refs[:3]
        whole, mask, packed, sems = refs[3:]
    copies = Copies(sems)
    ins = [copies.start(full, whole), copies.start(hot, mask)]
    if joined:
        ins += [copies.start(values, chosen), copies.start(moment, short)]
    for copy in ins:
        copy.wait()
    banks, lanes = packed.shape[0], packed.shape[2]
    picked = matmul(mask[...], whole[...], ((1,), (1,))).astype(BF16)
    picked = picked.reshape(banks, CAP, lanes)
    if joined:
        packed[:, :CAP] = chosen[...].reshape(banks, CAP, lanes)
        packed[:, CAP : 2 * CAP] = picked
        for bank in range(banks):
            packed[bank, 2 * CAP :] = short[...]
    else:
        packed[...] = picked
    copies.start(packed, out).wait()


def pick_call(full, hot, values, moment, banks):
    joined = values is not None
    rows = 2 * CAP + moment.shape[0] if joined else CAP
    lanes = full.shape[0]
    ins = [full, hot] + ([values, moment] if joined else [])
    scratch = [(x.shape, BF16) for x in ins] + [((banks, rows, lanes), BF16)]
    (out,) = kernel_call(
        functools.partial(pick_body, joined),
        ins,
        [jax.ShapeDtypeStruct((banks, rows, lanes), BF16)],
        scratch,
        5,
        2 * hot.size * lanes,
        "pick" if joined else "pick_first",
    )
    return out


def exchange(x, axis):
    return lax.all_to_all(x, axis, split_axis=0, concat_axis=0, tiled=True)


def swaps(x_first, x_second, axis):
    size = lax.axis_size(axis)
    inner = [(i, i ^ 1) for i in range(size)]
    outer = [(i, i + 1) if i % 2 else (i, i - 1) for i in range(1, size - 1)]
    return lax.ppermute(x_first, axis, inner), lax.ppermute(x_second, axis, outer)


def ordered(x, *others):
    return lax.optimization_barrier((x, others))[0]


def around(x, axis, shift):
    size = lax.axis_size(axis)
    return lax.ppermute(x, axis, [(i, (i + shift) % size) for i in range(size)])


def partner(x, axis):
    return lax.ppermute(x, axis, [(i, i ^ 1) for i in range(lax.axis_size(axis))])


def shards(
    fem_field,
    fem_source,
    reaction,
    bem_density,
    bem_source,
    bem_diagonal,
    near_blocks,
    near_pairs,
    low_left,
    low_right,
    centers,
    trace_cell,
    trace_bank,
    trace_row,
):
    fem_count = lax.axis_size("fem")
    bem_count = lax.axis_size("bem")
    fem_rank = lax.axis_index("fem")
    bem_rank = lax.axis_index("bem")
    excitations, local_rows = bem_density.shape
    share = excitations // fem_count
    per_dev, group, panel_rows, _ = near_blocks.shape
    panel_total, rank, _ = low_right.shape
    cells = reaction.size
    slots = trace_cell.shape[0]
    places = bem_count * CAP
    first_col = fem_rank * share
    own_first = bem_rank * per_dev

    parity = jnp.stack([fem_rank % 2, bem_rank % 2]).astype(jnp.int32)
    starts = jnp.stack([first_col, own_first]).astype(jnp.int32)
    sent, take, codes, *edges = setup_call(
        parity,
        starts,
        trace_bank.reshape(1, -1),
        trace_cell.reshape(1, -1),
        trace_row.reshape(1, -1),
        fem_field,
        bem_density,
        low_right,
        bem_count,
        share,
        per_dev,
    )
    cell_ids = jnp.arange(1, cells + 1, dtype=jnp.int32)
    spread = (cell_ids[:, None] == codes).astype(BF16)

    own_centers = lax.dynamic_slice_in_dim(centers, own_first, per_dev, 0)
    offsets = own_centers[:, None, :] - centers[None, :, :]
    kernel_rows = 1.0 / (1.0 + jnp.sum(offsets * offsets, axis=-1))
    panel_ids = jnp.arange(panel_total, dtype=jnp.int32)
    own_ids = own_first + jnp.arange(per_dev, dtype=jnp.int32)
    listed = jnp.any(near_pairs[:, :, None] == panel_ids[None, None, :], axis=1)
    listed = listed | (own_ids[:, None] == panel_ids[None, :])
    kernel_rows = jnp.where(listed, 0.0, kernel_rows)
    weights = jnp.repeat(kernel_rows.reshape(per_dev, bem_count, per_dev), rank, axis=2)
    weights = jnp.pad(weights.transpose(1, 0, 2), ((0, 0), (0, 0), (0, 128 - per_dev * rank)))
    factors = jnp.concatenate([low_left] * per_dev, axis=1)
    factors = jnp.pad(factors, ((0, 0), (0, 128 - per_dev * rank), (0, 0)))
    own_right = lax.dynamic_slice_in_dim(low_right, own_first, per_dev, 0)

    sources = lax.dynamic_slice_in_dim(near_pairs, fem_rank * group, group, 1)
    source_bank = sources // per_dev
    chip = jnp.mod(source_bank // 2 - bem_rank // 2 + 1, bem_count // 2)
    other = (source_bank + bem_rank) % 2
    table = ((chip * 2 + other) * per_dev + sources % per_dev).reshape(-1)
    table = jnp.concatenate([table, first_col[None]]).astype(jnp.int32)

    inverse = jnp.broadcast_to((1.0 / (6.0 + reaction))[..., None], fem_field.shape)
    density = lax.dynamic_slice_in_dim(bem_density, first_col, share, 0)
    source_part = lax.dynamic_slice_in_dim(bem_source, first_col, share, 0)
    diag_row = bem_diagonal[None, :]

    full = bem_density.astype(BF16)
    fem_state = fem_field
    received = exchange(sent, "bem")
    coded = received[:, CAP, 2 * CAP :].astype(F32)
    rows = (coded[:, :CAP] * 32.0 + coded[:, CAP:]).astype(jnp.int32).reshape(-1)
    hot = (rows[:, None] == jnp.arange(1, local_rows + 1, dtype=jnp.int32)).astype(BF16)
    for sweep in range(ITERS):
        last = sweep == ITERS - 1
        if sweep > 0:
            full = exchange(copies, "fem").reshape(excitations, local_rows)
            full = ordered(full, values)
        left = around(full, "bem", 2)
        right = around(full, "bem", -2)
        own = partner(full, "bem")
        parts = [left, partner(left, "bem"), full, own, right, partner(right, "bem")]
        if sweep > 0:
            sent = pick_call(full, hot, values, moment, bem_count)
            received = exchange(sent, "bem")
            returned = received
        if sweep == 0:
            halos = swaps(*edges[:2], "fem") + swaps(*edges[2:], "bem")
            table = ordered(table, halos, spread, inverse)
        partial = near_call(table, parts, near_blocks, received, hot, weights, factors)
        summed = exchange(partial.reshape(fem_count, share, local_rows), "fem")
        if sweep == 0:
            picked = pick_call(full, ordered(hot, partial), None, None, bem_count)
            returned = exchange(picked, "bem")
            summed = ordered(summed, picked)
        else:
            edges = ordered(tuple(edges), partial)
            halos = swaps(*edges[:2], "fem") + swaps(*edges[2:], "bem")
            summed = ordered(summed, halos)
        if last:
            density = update_call(summed, density, source_part, diag_row, own_right, last)[0]
            state = fem_state
        else:
            density, copies, moment = update_call(
                summed, density, source_part, diag_row, own_right, last
            )
            state = ordered(fem_state, copies)
        fem_state, *rest = fem_call(
            parity, state, fem_source, inverse, spread, returned, halos, take, last
        )
        if not last:
            values, *edges = rest
    return (fem_state, density)


def solution(mesh):
    return jax.shard_map(
        shards,
        mesh=mesh,
        in_specs=(
            P("fem", "bem", None, None),
            P("fem", "bem", None, None),
            P("fem", "bem", None),
            P(None, "bem"),
            P(None, "bem"),
            P("bem"),
            P("bem", "fem", None, None),
            P("bem", None),
            P("bem", None, None),
            P(),
            P(),
            P(("fem", "bem")),
            P(("fem", "bem"), None),
            P(("fem", "bem")),
        ),
        out_specs=(P("fem", "bem", None, None), P("fem", "bem")),
        check_vma=False,
    )
```

time: 260 us -> 203 us (0.78)
  the two profiles are of different devices: /device:TPU:99 before, /device:TPU:24 now
where the time goes in v1:
time: 203 us; the launch traced here: 201 us
  starting transfers between devices  99.6 us (49%)
  Pallas kernels  51.1 us (25%)
  waiting for transfers between devices  29.2 us (14%)
  other arithmetic  11.5 us (6%)
  local copies, waits for them, and re-layouts  8.33 us (4%)
    all_to_all x9, starting transfers between devices, exchange(): return lax.all_to_all(x, axis, split_axis=0, concat_axis=0, tiled=True)  56.7 us
    pallas_call x13, Pallas kernels, kernel_call(): pl.pallas_call(body, out_shape=outs, in_specs=[scalar] * len(smem) + [hbm...  51.1 us
    ppermute x6, starting transfers between devices, swaps(): lax.ppermute(x_second, axis, outer)  29.1 us
    all_to_all x9, waiting for transfers between devices, exchange(): return lax.all_to_all(x, axis, split_axis=0, concat_axis=0, tiled=True)  15 us
    ppermute x6, waiting for transfers between devices, swaps(): lax.ppermute(x_second, axis, outer)  11.3 us
    ppermute x6, starting transfers between devices, around(): return lax.ppermute(x, axis, [(i, (i + shift) % size) for i in range(size)])  11 us
  transfers between devices with their start and end apart: 36, of which 12 were waited for; matrix products, arithmetic and copies ran while one was open for 9% of the time, Pallas kernels for 15%

profile of v1, /device:TPU:24, one launch (start us, length us, event | category | flops | bytes accessed | tf_op | source)
XLA Modules:
  0.0 201.0 jit_solution(7328180562707905790)
XLA Ops:
  2.4 4.7 %collective-permute-start.7 = (bf16[128,1024]{1,0:T(8,128)(2,1)}, bf16[128,1024]{1,0:T(8,128)(2,1)}, u32[]{:S(2)}, u32[]{:S(2)}) collective-permute-start(bf16[128,1024]{1,0:T(8,128)(2,1)} %convert_element_type.23.refs_2_.refs_0_), channel_id=1, source_target_pairs={{0,14},{1,15},{2,0},{3,1},{4,2},{5,3},{6,4},{7,5},{8,6},{9,7},{10,... | collective-permute-start | bytes 786440 | tf_op jit(solution)/shard_map/ppermute | solution.py:487
  11.6 9.4 %all-to-all-start = ((bf16[16,48,128]{2,1,0:T(8,128)(2,1)}), bf16[16,48,128]{2,1,0:T(8,128)(2,1)S(1)}, u32[]{:S(2)}, u32[]{:S(2)}) async-start(bf16[16,48,128]{2,1,0:T(8,128)(2,1)} %get-tuple-element.50), calls=%async_computation | async-start | bytes 393216 | tf_op jit(solution)/shard_map/all_to_all | solution.py:471
  34.2 4.7 %collective-permute-start.3 = (bf16[8,32,128]{2,1,0:T(8,128)(2,1)S(1)}, bf16[8,32,128]{2,1,0:T(8,128)(2,1)S(1)}, u32[]{:S(2)}, u32[]{:S(2)}) collective-permute-start(bf16[8,32,128]{2,1,0:T(8,128)(2,1)S(1)} %copy-done.5), channel_id=1, source_target_pairs={{1,2},{2,1},{3,4},{4,3},{5,6},{6,5},{7,8},{8,7},{9,10},{10,9},{11,... | collective-permute-start | bytes 196616 | tf_op jit(solution)/shard_map/ppermute | solution.py:478
  47.8 5.6 %near.3 = bf16[128,1024]{1,0:T(8,128)(2,1)} custom-call(s32[13]{0:T(128)} %pad_add_fusion.1.table, bf16[128,1024]{1,0:T(8,128)(2,1)} %collective-permute-done.4.refs_0_, bf16[128,1024]{1,0:T(8,128)(2,1)} %collective-permute-done.5.refs_1_, bf16[128,1024]{1,0:T(8,128)(2,1)} %convert_element_type.23.refs_2_.refs_0_, ...), custom_call_target="tpu_custom_call" | custom-call | flops 805306368 | bytes 9388084 | tf_op jit(solution)/shard_map/near/pallas_call | solution.py:25
  53.4 5.5 %all-to-all-start.1 = ((bf16[8,16,1024]{2,1,0:T(8,128)(2,1)}), bf16[8,16,1024]{2,1,0:T(8,128)(2,1)}, u32[]{:S(2)}, u32[]{:S(2)}) async-start(bf16[8,16,1024]{2,1,0:T(8,128)(2,1)} %bitcast.20), calls=%async_computation.1 | async-start | bytes 524288 | tf_op jit(solution)/shard_map/all_to_all | solution.py:471
  65.4 4.9 %all-to-all-start.2 = ((bf16[16,32,128]{2,1,0:T(8,128)(2,1)}), bf16[16,32,128]{2,1,0:T(8,128)(2,1)}, u32[]{:S(2)}, u32[]{:S(2)}) async-start(bf16[16,32,128]{2,1,0:T(8,128)(2,1)} %pick_first.1), calls=%async_computation.2 | async-start | bytes 262144 | tf_op jit(solution)/shard_map/all_to_all | solution.py:471
  75.7 4.7 %all-to-all-start.3 = ((bf16[8,16,1024]{2,1,0:T(8,128)(2,1)}), bf16[8,16,1024]{2,1,0:T(8,128)(2,1)}, u32[]{:S(2)}, u32[]{:S(2)}) async-start(bf16[8,16,1024]{2,1,0:T(8,128)(2,1)} %get-tuple-element.53), calls=%async_computation.3 | async-start | bytes 524288 | tf_op jit(solution)/shard_map/all_to_all | solution.py:471
  80.4 6.3 %fem_step.2 = (f32[8,8,32,128]{3,2,1,0:T(8,128)}, bf16[512,128]{1,0:T(8,128)(2,1)}, bf16[8,32,128]{2,1,0:T(8,128)(2,1)}, bf16[8,32,128]{2,1,0:T(8,128)(2,1)}, bf...) custom-call(s32[2]{0:T(128)} %get-tuple-element.86.parity, f32[8,8,32,128]{3,2,1,0:T(8,128)} %refs_0_, ...), custom_call_target="tpu_custom_call" | custom-call | flops 536870912 | bytes 7733256 | tf_op jit(solution)/shard_map/fem_step/pallas_call | solution.py:25
  87.2 4.2 %collective-permute-start.12 = (bf16[128,1024]{1,0:T(8,128)(2,1)}, bf16[128,1024]{1,0:T(8,128)(2,1)}, u32[]{:S(2)}, u32[]{:S(2)}) collective-permute-start(bf16[128,1024]{1,0:T(8,128)(2,1)} %bitcast.12.refs_0_.refs_2_), channel_id=1, source_target_pairs={{0,14},{1,15},{2,0},{3,1},{4,2},{5,3},{6,4},{7,5},{8,6},{9,7},{10,... | collective-permute-start | bytes 786440 | tf_op jit(solution)/shard_map/ppermute | solution.py:487
  93.9 7.9 %all-to-all-start.4 = ((bf16[16,80,128]{2,1,0:T(8,128)(2,1)}), bf16[16,80,128]{2,1,0:T(8,128)(2,1)}, u32[]{:S(2)}, u32[]{:S(2)}) async-start(bf16[16,80,128]{2,1,0:T(8,128)(2,1)} %pick.2), calls=%async_computation.4 | async-start | bytes 655360 | tf_op jit(solution)/shard_map/all_to_all | solution.py:471
  103.7 5.7 %all-to-all-done.4.refs_7_.refs_4_ = bf16[16,80,128]{2,1,0:T(8,128)(2,1)} async-done(((bf16[16,80,128]{2,1,0:T(8,128)(2,1)}), bf16[16,80,128]{2,1,0:T(8,128)(2,1)}, u32[]{:S(2)}, u32[]{:S(2)}) %all-to-all-start.4) | async-done | bytes 327712 | tf_op jit(solution)/shard_map/all_to_all | solution.py:471
  109.3 5.5 %near.4 = bf16[128,1024]{1,0:T(8,128)(2,1)} custom-call(s32[13]{0:T(128)} %pad_add_fusion.1.table, bf16[128,1024]{1,0:T(8,128)(2,1)} %collective-permute-done.9.refs_0_, bf16[128,1024]{1,0:T(8,128)(2,1)} %collective-permute-done.10.refs_1_, bf16[128,1024]{1,0:T(8,128)(2,1)} %bitcast.12.refs_0_.refs_2_, bf16[128,1024]{1,0:T(8,128)(2,1)} %collective-permute-done.11.refs_3_, ...), custom_call_target="tpu_custom_call" | custom-call | flops 805306368 | bytes 9519156 | tf_op jit(solution)/shard_map/near/pallas_call | solution.py:25
  114.9 5.3 %all-to-all-start.5 = ((bf16[8,16,1024]{2,1,0:T(8,128)(2,1)}), bf16[8,16,1024]{2,1,0:T(8,128)(2,1)}, u32[]{:S(2)}, u32[]{:S(2)}) async-start(bf16[8,16,1024]{2,1,0:T(8,128)(2,1)} %bitcast.19), calls=%async_computation.5 | async-start | bytes 524288 | tf_op jit(solution)/shard_map/all_to_all | solution.py:471
  120.2 4.8 %collective-permute-start.15 = (bf16[8,32,128]{2,1,0:T(8,128)(2,1)}, bf16[8,32,128]{2,1,0:T(8,128)(2,1)}, u32[]{:S(2)}, u32[]{:S(2)}) collective-permute-start(bf16[8,32,128]{2,1,0:T(8,128)(2,1)} %get-tuple-element.65), channel_id=1, source_target_pairs={{16,32},{32,16},{48,64},{64,48},{80,96},{96,80},{17,33},{33,17},{4... | collective-permute-start | bytes 196616 | tf_op jit(solution)/shard_map/ppermute | solution.py:478
  125.1 5.4 %collective-permute-start.17 = (bf16[8,32,128]{2,1,0:T(8,128)(2,1)}, bf16[8,32,128]{2,1,0:T(8,128)(2,1)}, u32[]{:S(2)}, u32[]{:S(2)}) collective-permute-start(bf16[8,32,128]{2,1,0:T(8,128)(2,1)} %get-tuple-element.67), channel_id=1, source_target_pairs={{1,2},{2,1},{3,4},{4,3},{5,6},{6,5},{7,8},{8,7},{9,10},{10,9},{11,... | collective-permute-start | bytes 196616 | tf_op jit(solution)/shard_map/ppermute | solution.py:478
  136.5 5.4 %all-to-all-start.6 = ((bf16[8,16,1024]{2,1,0:T(8,128)(2,1)}), bf16[8,16,1024]{2,1,0:T(8,128)(2,1)}, u32[]{:S(2)}, u32[]{:S(2)}) async-start(bf16[8,16,1024]{2,1,0:T(8,128)(2,1)} %get-tuple-element.70), calls=%async_computation.6 | async-start | bytes 524288 | tf_op jit(solution)/shard_map/all_to_all | solution.py:471
  141.9 6.3 %fem_step.3 = (f32[8,8,32,128]{3,2,1,0:T(8,128)}, bf16[512,128]{1,0:T(8,128)(2,1)}, bf16[8,32,128]{2,1,0:T(8,128)(2,1)}, bf16[8,32,128]{2,1,0:T(8,128)(2,1)}, bf...) custom-call(s32[2]{0:T(128)} %get-tuple-element.86.parity, f32[8,8,32,128]{3,2,1,0:T(8,128)} %get-tuple-element.71.refs_0_, ...), custom_call_target="tpu_custom_call" | custom-call | flops 536870912 | bytes 7929864 | tf_op jit(solution)/shard_map/fem_step/pallas_call | solution.py:25
  152.8 7.9 %all-to-all-start.7 = ((bf16[16,80,128]{2,1,0:T(8,128)(2,1)}), bf16[16,80,128]{2,1,0:T(8,128)(2,1)}, u32[]{:S(2)}, u32[]{:S(2)}) async-start(bf16[16,80,128]{2,1,0:T(8,128)(2,1)} %pick.3), calls=%async_computation.7 | async-start | bytes 655360 | tf_op jit(solution)/shard_map/all_to_all | solution.py:471
  162.6 5.7 %all-to-all-done.7.refs_7_.refs_4_ = bf16[16,80,128]{2,1,0:T(8,128)(2,1)} async-done(((bf16[16,80,128]{2,1,0:T(8,128)(2,1)}), bf16[16,80,128]{2,1,0:T(8,128)(2,1)}, u32[]{:S(2)}, u32[]{:S(2)}) %all-to-all-start.7) | async-done | bytes 327712 | tf_op jit(solution)/shard_map/all_to_all | solution.py:471
  168.3 5.5 %near.5 = bf16[128,1024]{1,0:T(8,128)(2,1)} custom-call(s32[13]{0:T(128)} %pad_add_fusion.1.table, bf16[128,1024]{1,0:T(8,128)(2,1)} %collective-permute-done.18.refs_0_, bf16[128,1024]{1,0:T(8,128)(2,1)} %collective-permute-done.19.refs_1_, bf16[128,1024]{1,0:T(8,128)(2,1)} %bitcast.14.refs_0_.refs_2_, bf16[128,1024]{1,0:T(8,128)(2,1)} %collective-permute-done.20.refs_3_, ...), custom_call_target="tpu_custom_call" | custom-call | flops 805306368 | bytes 9519156 | tf_op jit(solution)/shard_map/near/pallas_call | solution.py:25
  173.8 5.7 %all-to-all-start.8 = ((bf16[8,16,1024]{2,1,0:T(8,128)(2,1)}), bf16[8,16,1024]{2,1,0:T(8,128)(2,1)}, u32[]{:S(2)}, u32[]{:S(2)}) async-start(bf16[8,16,1024]{2,1,0:T(8,128)(2,1)} %bitcast.18), calls=%async_computation.8 | async-start | bytes 524288 | tf_op jit(solution)/shard_map/all_to_all | solution.py:471
  179.6 4.8 %collective-permute-start.24 = (bf16[8,32,128]{2,1,0:T(8,128)(2,1)}, bf16[8,32,128]{2,1,0:T(8,128)(2,1)}, u32[]{:S(2)}, u32[]{:S(2)}) collective-permute-start(bf16[8,32,128]{2,1,0:T(8,128)(2,1)} %get-tuple-element.81), channel_id=1, source_target_pairs={{16,32},{32,16},{48,64},{64,48},{80,96},{96,80},{17,33},{33,17},{4... | collective-permute-start | bytes 196616 | tf_op jit(solution)/shard_map/ppermute | solution.py:478
  184.5 5.3 %collective-permute-start.26 = (bf16[8,32,128]{2,1,0:T(8,128)(2,1)}, bf16[8,32,128]{2,1,0:T(8,128)(2,1)}, u32[]{:S(2)}, u32[]{:S(2)}) collective-permute-start(bf16[8,32,128]{2,1,0:T(8,128)(2,1)} %get-tuple-element.83), channel_id=1, source_target_pairs={{1,2},{2,1},{3,4},{4,3},{5,6},{6,5},{7,8},{8,7},{9,10},{10,9},{11,... | collective-permute-start | bytes 196616 | tf_op jit(solution)/shard_map/ppermute | solution.py:478
  194.0 5.1 %fem_last.1 = f32[8,8,32,128]{3,2,1,0:T(8,128)} custom-call(s32[2]{0:T(128)} %get-tuple-element.86.parity, f32[8,8,32,128]{3,2,1,0:T(8,128)} %get-tuple-element.72.refs_0_, f32[8,8,32,128]{3,2,1,0:T(8,128)} %refs_1_.5, f32[8,8,32,128]{3,2,1,0:T(8,128)} %broadcast_in_dim.13.refs_2_, bf16[2048,512]{1,0:T(8,128)(2,1)} %compare_convert_fusion.refs_3_, ...), custom_call_target="tpu_custom_call" | custom-call | flops 536870912 | bytes 5832712 | tf_op jit(solution)/shard_map/fem_last/pallas_call | solution.py:25
  (104 shorter events, 63.5 us)
Async XLA Ops:
  2.4 43.1 %collective-permute-start.7 = (bf16[128,1024]{1,0:T(8,128)(2,1)}, bf16[128,1024]{1,0:T(8,128)(2,1)}, u32[]{:S(2)}, u32[]{:S(2)}) collective-permute-start(bf16[128,1024]{1,0:T(8,128)(2,1)} %convert_element_type.23.refs_2_.refs_0_), channel_id=1, source_target_pairs={{0,14},{1,15},{2,0},{3,1},{4,2},{5,3},{6,4},{7,5},{8,6},{9,7},{10,... | collective-permute-start | bytes 786440 | tf_op jit(solution)/shard_map/ppermute | solution.py:487
  7.1 38.5 %collective-permute-start.4 = (bf16[128,1024]{1,0:T(8,128)(2,1)}, bf16[128,1024]{1,0:T(8,128)(2,1)}, u32[]{:S(2)}, u32[]{:S(2)}) collective-permute-start(bf16[128,1024]{1,0:T(8,128)(2,1)} %convert_element_type.23.refs_2_.refs_0_), channel_id=1, source_target_pairs={{0,2},{1,3},{2,4},{3,5},{4,6},{5,7},{6,8},{7,9},{8,10},{9,11},{10,... | collective-permute-start | bytes 786440 | tf_op jit(solution)/shard_map/ppermute | solution.py:487
  11.6 33.1 %all-to-all-start = ((bf16[16,48,128]{2,1,0:T(8,128)(2,1)}), bf16[16,48,128]{2,1,0:T(8,128)(2,1)S(1)}, u32[]{:S(2)}, u32[]{:S(2)}) async-start(bf16[16,48,128]{2,1,0:T(8,128)(2,1)} %get-tuple-element.50), calls=%async_computation | async-start | bytes 393216 | tf_op jit(solution)/shard_map/all_to_all | solution.py:471
  21.0 13.2 %collective-permute-start = (bf16[8,32,128]{2,1,0:T(8,128)(2,1)}, bf16[8,32,128]{2,1,0:T(8,128)(2,1)S(1)}, u32[]{:S(2)}, u32[]{:S(2)}) collective-permute-start(bf16[8,32,128]{2,1,0:T(8,128)(2,1)} %get-tuple-element.44), channel_id=1, source_target_pairs={{0,16},{16,0},{32,48},{48,32},{64,80},{80,64},{96,112},{112,96},{1... | collective-permute-start | bytes 196616 | tf_op jit(solution)/shard_map/ppermute | solution.py:478
  21.7 18.5 %collective-permute-start.1 = (bf16[8,32,128]{2,1,0:T(8,128)(2,1)}, bf16[8,32,128]{2,1,0:T(8,128)(2,1)S(1)}, u32[]{:S(2)}, u32[]{:S(2)}) collective-permute-start(bf16[8,32,128]{2,1,0:T(8,128)(2,1)} %get-tuple-element.45), channel_id=1, source_target_pairs={{16,32},{32,16},{48,64},{64,48},{80,96},{96,80},{17,33},{33,17},{4... | collective-permute-start | bytes 196616 | tf_op jit(solution)/shard_map/ppermute | solution.py:478
  25.9 14.4 %collective-permute-start.2 = (bf16[8,32,128]{2,1,0:T(8,128)(2,1)}, bf16[8,32,128]{2,1,0:T(8,128)(2,1)S(1)}, u32[]{:S(2)}, u32[]{:S(2)}) collective-permute-start(bf16[8,32,128]{2,1,0:T(8,128)(2,1)} %get-tuple-element.46), channel_id=1, source_target_pairs={{0,1},{1,0},{2,3},{3,2},{4,5},{5,4},{6,7},{7,6},{8,9},{9,8},{10,11... | collective-permute-start | bytes 196616 | tf_op jit(solution)/shard_map/ppermute | solution.py:478
  53.4 12.0 %all-to-all-start.1 = ((bf16[8,16,1024]{2,1,0:T(8,128)(2,1)}), bf16[8,16,1024]{2,1,0:T(8,128)(2,1)}, u32[]{:S(2)}, u32[]{:S(2)}) async-start(bf16[8,16,1024]{2,1,0:T(8,128)(2,1)} %bitcast.20), calls=%async_computation.1 | async-start | bytes 524288 | tf_op jit(solution)/shard_map/all_to_all | solution.py:471
  65.4 10.3 %all-to-all-start.2 = ((bf16[16,32,128]{2,1,0:T(8,128)(2,1)}), bf16[16,32,128]{2,1,0:T(8,128)(2,1)}, u32[]{:S(2)}, u32[]{:S(2)}) async-start(bf16[16,32,128]{2,1,0:T(8,128)(2,1)} %pick_first.1), calls=%async_computation.2 | async-start | bytes 262144 | tf_op jit(solution)/shard_map/all_to_all | solution.py:471
  75.7 11.5 %all-to-all-start.3 = ((bf16[8,16,1024]{2,1,0:T(8,128)(2,1)}), bf16[8,16,1024]{2,1,0:T(8,128)(2,1)}, u32[]{:S(2)}, u32[]{:S(2)}) async-start(bf16[8,16,1024]{2,1,0:T(8,128)(2,1)} %get-tuple-element.53), calls=%async_computation.3 | async-start | bytes 524288 | tf_op jit(solution)/shard_map/all_to_all | solution.py:471
  87.2 14.8 %collective-permute-start.12 = (bf16[128,1024]{1,0:T(8,128)(2,1)}, bf16[128,1024]{1,0:T(8,128)(2,1)}, u32[]{:S(2)}, u32[]{:S(2)}) collective-permute-start(bf16[128,1024]{1,0:T(8,128)(2,1)} %bitcast.12.refs_0_.refs_2_), channel_id=1, source_target_pairs={{0,14},{1,15},{2,0},{3,1},{4,2},{5,3},{6,4},{7,5},{8,6},{9,7},{10,... | collective-permute-start | bytes 786440 | tf_op jit(solution)/shard_map/ppermute | solution.py:487
  91.4 11.3 %collective-permute-start.9 = (bf16[128,1024]{1,0:T(8,128)(2,1)}, bf16[128,1024]{1,0:T(8,128)(2,1)}, u32[]{:S(2)}, u32[]{:S(2)}) collective-permute-start(bf16[128,1024]{1,0:T(8,128)(2,1)} %bitcast.12.refs_0_.refs_2_), channel_id=1, source_target_pairs={{0,2},{1,3},{2,4},{3,5},{4,6},{5,7},{6,8},{7,9},{8,10},{9,11},{10,... | collective-permute-start | bytes 786440 | tf_op jit(solution)/shard_map/ppermute | solution.py:487
  93.9 15.4 %all-to-all-start.4 = ((bf16[16,80,128]{2,1,0:T(8,128)(2,1)}), bf16[16,80,128]{2,1,0:T(8,128)(2,1)}, u32[]{:S(2)}, u32[]{:S(2)}) async-start(bf16[16,80,128]{2,1,0:T(8,128)(2,1)} %pick.2), calls=%async_computation.4 | async-start | bytes 655360 | tf_op jit(solution)/shard_map/all_to_all | solution.py:471
  114.9 19.8 %all-to-all-start.5 = ((bf16[8,16,1024]{2,1,0:T(8,128)(2,1)}), bf16[8,16,1024]{2,1,0:T(8,128)(2,1)}, u32[]{:S(2)}, u32[]{:S(2)}) async-start(bf16[8,16,1024]{2,1,0:T(8,128)(2,1)} %bitcast.19), calls=%async_computation.5 | async-start | bytes 524288 | tf_op jit(solution)/shard_map/all_to_all | solution.py:471
  120.2 10.3 %collective-permute-start.14 = (bf16[8,32,128]{2,1,0:T(8,128)(2,1)}, bf16[8,32,128]{2,1,0:T(8,128)(2,1)}, u32[]{:S(2)}, u32[]{:S(2)}) collective-permute-start(bf16[8,32,128]{2,1,0:T(8,128)(2,1)} %get-tuple-element.64), channel_id=1, source_target_pairs={{0,16},{16,0},{32,48},{48,32},{64,80},{80,64},{96,112},{112,96},{1... | collective-permute-start | bytes 196616 | tf_op jit(solution)/shard_map/ppermute | solution.py:478
  120.2 10.3 %collective-permute-start.15 = (bf16[8,32,128]{2,1,0:T(8,128)(2,1)}, bf16[8,32,128]{2,1,0:T(8,128)(2,1)}, u32[]{:S(2)}, u32[]{:S(2)}) collective-permute-start(bf16[8,32,128]{2,1,0:T(8,128)(2,1)} %get-tuple-element.65), channel_id=1, source_target_pairs={{16,32},{32,16},{48,64},{64,48},{80,96},{96,80},{17,33},{33,17},{4... | collective-permute-start | bytes 196616 | tf_op jit(solution)/shard_map/ppermute | solution.py:478
  125.1 9.5 %collective-permute-start.17 = (bf16[8,32,128]{2,1,0:T(8,128)(2,1)}, bf16[8,32,128]{2,1,0:T(8,128)(2,1)}, u32[]{:S(2)}, u32[]{:S(2)}) collective-permute-start(bf16[8,32,128]{2,1,0:T(8,128)(2,1)} %get-tuple-element.67), channel_id=1, source_target_pairs={{1,2},{2,1},{3,4},{4,3},{5,6},{6,5},{7,8},{8,7},{9,10},{10,9},{11,... | collective-permute-start | bytes 196616 | tf_op jit(solution)/shard_map/ppermute | solution.py:478
  136.5 11.7 %all-to-all-start.6 = ((bf16[8,16,1024]{2,1,0:T(8,128)(2,1)}), bf16[8,16,1024]{2,1,0:T(8,128)(2,1)}, u32[]{:S(2)}, u32[]{:S(2)}) async-start(bf16[8,16,1024]{2,1,0:T(8,128)(2,1)} %get-tuple-element.70), calls=%async_computation.6 | async-start | bytes 524288 | tf_op jit(solution)/shard_map/all_to_all | solution.py:471
  148.2 12.6 %collective-permute-start.21 = (bf16[128,1024]{1,0:T(8,128)(2,1)}, bf16[128,1024]{1,0:T(8,128)(2,1)}, u32[]{:S(2)}, u32[]{:S(2)}) collective-permute-start(bf16[128,1024]{1,0:T(8,128)(2,1)} %bitcast.14.refs_0_.refs_2_), channel_id=1, source_target_pairs={{0,14},{1,15},{2,0},{3,1},{4,2},{5,3},{6,4},{7,5},{8,6},{9,7},{10,... | collective-permute-start | bytes 786440 | tf_op jit(solution)/shard_map/ppermute | solution.py:487
  148.3 12.9 %collective-permute-start.18 = (bf16[128,1024]{1,0:T(8,128)(2,1)}, bf16[128,1024]{1,0:T(8,128)(2,1)}, u32[]{:S(2)}, u32[]{:S(2)}) collective-permute-start(bf16[128,1024]{1,0:T(8,128)(2,1)} %bitcast.14.refs_0_.refs_2_), channel_id=1, source_target_pairs={{0,2},{1,3},{2,4},{3,5},{4,6},{5,7},{6,8},{7,9},{8,10},{9,11},{10,... | collective-permute-start | bytes 786440 | tf_op jit(solution)/shard_map/ppermute | solution.py:487
  152.8 15.4 %all-to-all-start.7 = ((bf16[16,80,128]{2,1,0:T(8,128)(2,1)}), bf16[16,80,128]{2,1,0:T(8,128)(2,1)}, u32[]{:S(2)}, u32[]{:S(2)}) async-start(bf16[16,80,128]{2,1,0:T(8,128)(2,1)} %pick.3), calls=%async_computation.7 | async-start | bytes 655360 | tf_op jit(solution)/shard_map/all_to_all | solution.py:471
  173.8 25.3 %all-to-all-start.8 = ((bf16[8,16,1024]{2,1,0:T(8,128)(2,1)}), bf16[8,16,1024]{2,1,0:T(8,128)(2,1)}, u32[]{:S(2)}, u32[]{:S(2)}) async-start(bf16[8,16,1024]{2,1,0:T(8,128)(2,1)} %bitcast.18), calls=%async_computation.8 | async-start | bytes 524288 | tf_op jit(solution)/shard_map/all_to_all | solution.py:471
  179.5 10.3 %collective-permute-start.23 = (bf16[8,32,128]{2,1,0:T(8,128)(2,1)}, bf16[8,32,128]{2,1,0:T(8,128)(2,1)}, u32[]{:S(2)}, u32[]{:S(2)}) collective-permute-start(bf16[8,32,128]{2,1,0:T(8,128)(2,1)} %get-tuple-element.80), channel_id=1, source_target_pairs={{0,16},{16,0},{32,48},{48,32},{64,80},{80,64},{96,112},{112,96},{1... | collective-permute-start | bytes 196616 | tf_op jit(solution)/shard_map/ppermute | solution.py:478
  179.6 10.2 %collective-permute-start.24 = (bf16[8,32,128]{2,1,0:T(8,128)(2,1)}, bf16[8,32,128]{2,1,0:T(8,128)(2,1)}, u32[]{:S(2)}, u32[]{:S(2)}) collective-permute-start(bf16[8,32,128]{2,1,0:T(8,128)(2,1)} %get-tuple-element.81), channel_id=1, source_target_pairs={{16,32},{32,16},{48,64},{64,48},{80,96},{96,80},{17,33},{33,17},{4... | collective-permute-start | bytes 196616 | tf_op jit(solution)/shard_map/ppermute | solution.py:478
  184.5 9.5 %collective-permute-start.26 = (bf16[8,32,128]{2,1,0:T(8,128)(2,1)}, bf16[8,32,128]{2,1,0:T(8,128)(2,1)}, u32[]{:S(2)}, u32[]{:S(2)}) collective-permute-start(bf16[8,32,128]{2,1,0:T(8,128)(2,1)} %get-tuple-element.83), channel_id=1, source_target_pairs={{1,2},{2,1},{3,4},{4,3},{5,6},{6,5},{7,8},{8,7},{9,10},{10,9},{11,... | collective-permute-start | bytes 196616 | tf_op jit(solution)/shard_map/ppermute | solution.py:478
  (18 other events, 108.3 us)

commit v2 on v1

v2 whole, which is shorter than its diff:
```python
import functools

import jax
import jax.numpy as jnp
from jax import lax
from jax.experimental import pallas as pl
from jax.experimental.pallas import tpu as pltpu
from jax.sharding import PartitionSpec as P

CAP = 32
ITERS = 3
COVER = 20_000_000_000
HIGHEST = lax.Precision.HIGHEST
BF16 = jnp.bfloat16
F32 = jnp.float32


def matmul(left, right, dims):
    return lax.dot_general(left, right, (dims, ((), ())), preferred_element_type=F32)


def kernel_call(body, args, outs, scratch, copies, flops, name, smem=()):
    hbm = pl.BlockSpec(memory_space=pltpu.HBM)
    scalar = pl.BlockSpec(memory_space=pltpu.SMEM)
    args = [*smem, *args]
    return pl.pallas_call(
        body,
        out_shape=outs,
        in_specs=[scalar] * len(smem) + [hbm] * (len(args) - len(smem)),
        out_specs=[hbm] * len(outs),
        scratch_shapes=[pltpu.VMEM(s, t) for s, t in scratch] + [pltpu.SemaphoreType.DMA((copies,))],
        compiler_params=pltpu.CompilerParams(vmem_limit_bytes=64 << 20),
        cost_estimate=pl.CostEstimate(
            flops=flops,
            bytes_accessed=sum(x.size * x.dtype.itemsize for x in args),
            transcendentals=0,
        ),
        name=name,
    )(*args)


class Copies:
    def __init__(self, sems):
        self.sems, self.count = sems, 0

    def start(self, source, target):
        copy = pltpu.make_async_copy(source, target, self.sems.at[self.count])
        self.count += 1
        copy.start()
        return copy


def whereabouts():
    bem = lax.axis_index("bem")
    core, odd = bem % 2, bem // 2 % 2
    inside = (bem > 0) & (bem < lax.axis_size("bem") - 1)
    return (lax.axis_index("fem") % 2, core, odd, (core + odd + 1) % 2, inside)


def near_body(pairs, *refs):
    parts = refs[:6]
    blocks, received, hot, weights, factors, out = refs[6:12]
    panels, held, got, mask, mix, factor, total, narrow, sems = refs[12:]
    per_dev, group, rows, _ = blocks.shape
    share = panels.shape[1] // lax.axis_size("fem")
    rank = factors.shape[1]
    copies = Copies(sems)
    small = [
        copies.start(received, got),
        copies.start(hot, mask),
        copies.start(weights, mix),
    ]
    for k in range(per_dev):
        small.append(copies.start(factors, factor.at[:, k * rank : (k + 1) * rank]))
    moved = []
    for place, ref in enumerate(parts):
        for half in range(per_dev):
            moved.append(
                copies.start(
                    ref.at[pl.ds(0, panels.shape[1]), half * rows : (half + 1) * rows],
                    panels.at[place * per_dev + half],
                )
            )
    loads = []
    for half in range(per_dev):
        for step in range(group):
            loads.append(copies.start(blocks.at[half, step], held.at[half * group + step]))
    factor[:, per_dev * rank :] = jnp.zeros_like(factor[:, per_dev * rank :])
    for copy in small:
        copy.wait()
    fem, bem, banks = lax.axis_index("fem"), lax.axis_index("bem"), lax.axis_size("bem")
    values = got[:, :CAP, :].reshape(-1, got.shape[2])
    traced = matmul(values, mask[...], ((0,), (0,)))
    start = pl.multiple_of(fem * share, share)
    for half in range(per_dev):
        mixed = jnp.zeros((share, got.shape[2]), F32)
        for bank in range(got.shape[0]):
            mixed = mixed + mix[bank, half : half + 1, :] * got[
                bank, got.shape[1] - share :, :
            ].astype(F32)
        upper = mixed.astype(BF16)
        lower = (mixed - upper.astype(F32)).astype(BF16)
        far = matmul(upper, factor[half], ((1,), (0,))) + matmul(lower, factor[half], ((1,), (0,)))
        total[half] = traced[:, half * rows : (half + 1) * rows]
        total[half, pl.ds(start, share), :] += far
    for copy in moved:
        copy.wait()
    done = []
    for half in range(per_dev):
        summed = total[half]
        for step in range(group):
            source = pairs[half, fem * group + step]
            bank = source // per_dev
            chip = (bank // 2 - bem // 2 + 1 + banks // 2) % (banks // 2)
            chip = jnp.where(bem // 2 % 2 == 1, chip, 2 - chip)
            place = (chip * 2 + (bank + bem) % 2) * per_dev + source % per_dev
            loads[half * group + step].wait()
            summed = summed + matmul(panels[place], held[half * group + step], ((1,), (0,)))
        narrow[half] = summed.astype(BF16)
        done.append(copies.start(narrow.at[half], out.at[:, half * rows : (half + 1) * rows]))
    for copy in done:
        copy.wait()


def near_call(pairs, parts, near_blocks, received, hot, weights, factors):
    per_dev, group, rows, _ = near_blocks.shape
    excitations = parts[2].shape[0]
    return kernel_call(
        near_body,
        [*parts, near_blocks, received, hot, weights, factors],
        [jax.ShapeDtypeStruct((excitations, per_dev * rows), BF16)],
        [
            ((6 * per_dev, excitations, rows), BF16),
            ((per_dev * group, rows, rows), BF16),
            (received.shape, BF16),
            (hot.shape, BF16),
            (weights.shape, F32),
            ((per_dev, weights.shape[2], rows), BF16),
            ((per_dev, excitations, rows), F32),
            ((per_dev, excitations, rows), BF16),
        ],
        3 + per_dev + 6 * per_dev + per_dev * group + per_dev,
        2 * excitations * near_blocks.size // rows * rows,
        "near",
        smem=[pairs],
    )[0]


def gate_call(kept, *arrived):
    hbm = pl.BlockSpec(memory_space=pltpu.HBM)
    return pl.pallas_call(
        lambda *refs: None,
        out_shape=jax.ShapeDtypeStruct(kept.shape, kept.dtype),
        in_specs=[hbm] * (1 + len(arrived)),
        out_specs=hbm,
        input_output_aliases={0: 0},
        compiler_params=pltpu.CompilerParams(vmem_limit_bytes=64 << 20),
        cost_estimate=pl.CostEstimate(flops=COVER, bytes_accessed=0, transcendentals=0),
        name="gate",
    )(kept, *arrived)


def write_edges(state, take, outs, chosen, rims, sides, marks, copies):
    values, first, second, rows, near = outs
    cx, cy, cz, lanes = state.shape
    rims[0] = state[0].astype(BF16)
    rims[1] = state[cx - 1].astype(BF16)
    for i in range(cx):
        sides[0, :, i * lanes : (i + 1) * lanes] = state[i, 0].astype(BF16)
        sides[1, :, i * lanes : (i + 1) * lanes] = state[i, cy - 1].astype(BF16)
    done = [
        copies.start(rims.at[1 - marks[0]], first),
        copies.start(rims.at[marks[0]], second),
        copies.start(sides, rows),
        copies.start(sides.at[1 - marks[1]], near),
    ]
    narrow = state[...].reshape(cx * cy * cz, lanes).astype(BF16)
    chosen[...] = matmul(take[...], narrow, ((1,), (0,))).astype(BF16)
    done.append(copies.start(chosen, values))
    return done


def edge_shapes(state, places):
    cx, cy, cz, lanes = state.shape
    return [
        jax.ShapeDtypeStruct((places, lanes), BF16),
        jax.ShapeDtypeStruct((cy, cz, lanes), BF16),
        jax.ShapeDtypeStruct((cy, cz, lanes), BF16),
        jax.ShapeDtypeStruct((2, cz, cx * lanes), BF16),
        jax.ShapeDtypeStruct((cz, cx * lanes), BF16),
    ]


def edge_scratch(state, places):
    cx, cy, cz, lanes = state.shape
    return [
        ((places, lanes), BF16),
        ((2, cy, cz, lanes), BF16),
        ((2, cz, cx * lanes), BF16),
    ]


def slot_places(bank_r):
    slots = bank_r.shape[1]
    down = lax.broadcasted_iota(jnp.int32, (slots, slots), 0)
    over = lax.broadcasted_iota(jnp.int32, (slots, slots), 1)

    def column(x):
        return jnp.sum(jnp.where(down == over, x, 0), axis=1, keepdims=True)

    bank_c = column(bank_r)
    same = bank_c == bank_r
    place_r = bank_r * CAP + jnp.sum(
        jnp.where(same & (down < over), 1, 0), axis=0, keepdims=True
    )
    return place_r, column(place_r), column


def index_body(bank, row, sent, banks_v, rows_v, packed, sems):
    copies = Copies(sems)
    for copy in [copies.start(bank, banks_v), copies.start(row, rows_v)]:
        copy.wait()
    banks, cap, lanes = packed.shape
    place_r, _, _ = slot_places(banks_v[...])
    hit = lax.broadcasted_iota(jnp.int32, (banks * cap, bank.shape[1]), 0) == place_r
    code = jnp.sum(jnp.where(hit, rows_v[...] + 1, 0), axis=1, keepdims=True)
    lane = lax.broadcasted_iota(jnp.int32, (banks * cap, lanes), 1)
    digits = jnp.where(lane == 0, code // 32, jnp.where(lane == 1, code % 32, 0))
    packed[...] = digits.astype(F32).astype(BF16).reshape(banks, cap, lanes)
    copies.start(packed, sent).wait()


def index_call(bank, row, banks, lanes):
    packed = (banks, CAP, lanes)
    return kernel_call(
        index_body,
        [bank, row],
        [jax.ShapeDtypeStruct(packed, BF16)],
        [(bank.shape, jnp.int32), (row.shape, jnp.int32), (packed, BF16)],
        3,
        1 << 20,
        "index",
    )[0]


def first_panel(part):
    return lax.axis_index("bem") * part.shape[0]


def setup_body(*refs):
    marks = whereabouts()
    bank, cell, state, density, right = refs[:5]
    take, codes, moment = refs[5:8]
    outs = refs[8:13]
    banks_v, cells_v, here, share_v, factor, picks, coded, short, chosen, rims, sides, sems = refs[13:]
    copies = Copies(sems)
    small = [copies.start(bank, banks_v), copies.start(cell, cells_v)]
    share = share_v.shape[0]
    start = pl.multiple_of(lax.axis_index("fem") * share, share)
    large = [
        copies.start(density.at[pl.ds(start, share)], share_v),
        copies.start(right.at[pl.ds(first_panel(factor), factor.shape[0])], factor),
        copies.start(state, here),
    ]
    for copy in small:
        copy.wait()
    slots = bank.shape[1]
    places, cells = take.shape
    cell_r = cells_v[...] + 1
    place_r, place_c, column = slot_places(banks_v[...])
    hit = lax.broadcasted_iota(jnp.int32, (places, slots), 0) == place_r
    cell_c = jnp.sum(jnp.where(hit, cell_r, 0), axis=1, keepdims=True)
    ids = lax.broadcasted_iota(jnp.int32, (places, cells), 1) + 1
    picks[...] = (cell_c == ids).astype(F32).astype(BF16)
    out = [copies.start(picks, take)]
    hit = lax.broadcasted_iota(jnp.int32, (slots, places), 1) == place_c
    coded[...] = jnp.sum(jnp.where(hit, column(cell_r), 0), axis=0, keepdims=True)
    out.append(copies.start(coded, codes))
    for copy in large:
        copy.wait()
    out += write_edges(here, picks, outs, chosen, rims, sides, marks, copies)
    short[...] = moments(share_v[...].astype(BF16), factor).astype(BF16)
    out.append(copies.start(short, moment))
    for copy in out:
        copy.wait()


def setup_call(bank, cell, state, density, right, banks, share, per_dev):
    cx, cy, cz, lanes = state.shape
    slots = bank.shape[1]
    places = banks * CAP
    take = jax.ShapeDtypeStruct((places, cx * cy * cz), BF16)
    return kernel_call(
        setup_body,
        [bank, cell, state, density, right],
        [
            take,
            jax.ShapeDtypeStruct((1, places), jnp.int32),
            jax.ShapeDtypeStruct((share, 128), BF16),
        ]
        + edge_shapes(state, places),
        [
            ((1, slots), jnp.int32),
            ((1, slots), jnp.int32),
            (state.shape, F32),
            ((share, density.shape[1]), F32),
            ((per_dev, *right.shape[1:]), BF16),
            (take.shape, BF16),
            ((1, places), jnp.int32),
            ((share, 128), BF16),
        ]
        + edge_scratch(state, places),
        13,
        2 * take.size * lanes,
        "setup",
    )


def moments(rounded, factor):
    per_dev, rank, rows = factor.shape
    sums = [
        matmul(rounded[:, q * rows : (q + 1) * rows], factor[q], ((1,), (1,)))
        for q in range(per_dev)
    ]
    sums.append(jnp.zeros((rounded.shape[0], 128 - per_dev * rank), F32))
    return jnp.concatenate(sums, axis=1)


def tables_body(
    codes, centers, pairs, reaction, spread, weights, inverse,
    codes_v, places, listed_v, scale, wide, mix, full, sems,
):
    copies = Copies(sems)
    ins = [
        copies.start(codes, codes_v),
        copies.start(centers, places),
        copies.start(pairs, listed_v),
        copies.start(reaction, scale),
    ]
    for copy in ins:
        copy.wait()
    cx, cy, cz, lanes = full.shape
    scale[...] = 1.0 / (6.0 + scale[...])
    down = lax.broadcasted_iota(jnp.int32, (cz, cz), 0)
    over = lax.broadcasted_iota(jnp.int32, (cz, cz), 1)

    def plane(m, carry):
        i, j = m // cy, m % cy
        along_lanes = scale[i, pl.ds(j, 1), :]
        factor = jnp.sum(jnp.where(down == over, along_lanes, 0.0), axis=1, keepdims=True)
        full[i, j] = jnp.broadcast_to(factor, (cz, lanes))
        return carry

    lax.fori_loop(0, cx * cy, plane, 0, unroll=8)
    wanted = codes_v[...]
    rows = 256
    done = []
    for k in range(wide.shape[0] // rows):
        ids = lax.broadcasted_iota(jnp.int32, (rows, wanted.shape[1]), 0) + (k * rows + 1)
        wide[k * rows : (k + 1) * rows] = (ids == wanted).astype(F32).astype(BF16)
    done += [copies.start(wide, spread), copies.start(full, inverse)]
    banks, per_dev, lanes = mix.shape
    panels = places.shape[1]
    rank = lanes // 2 // per_dev
    near = listed_v[...]
    ids = lax.broadcasted_iota(jnp.int32, (panels, near.shape[1]), 0)
    own = lax.broadcasted_iota(jnp.int32, (panels, 1), 0)
    panel = lax.broadcasted_iota(jnp.int32, (panels, lanes), 0)
    lane = lax.broadcasted_iota(jnp.int32, (panels, lanes), 1)
    spots = places[...]
    square = [lax.broadcasted_iota(jnp.int32, (panels, panels), d) for d in (0, 1)]
    which = lax.broadcasted_iota(jnp.int32, spots.shape, 1)
    own_first = lax.axis_index("bem") * per_dev
    for p in range(per_dev):
        here = jnp.sum(jnp.where(which == own_first + p, spots, 0.0), axis=1, keepdims=True)
        offset = here - spots
        apart = jnp.sum(offset * offset, axis=0, keepdims=True)
        apart = jnp.where(square[0] == square[1], apart, 0.0)
        kernel = 1.0 / (1.0 + jnp.sum(apart, axis=1, keepdims=True))
        hits = jnp.sum(jnp.where(ids == near[p : p + 1], 1, 0), axis=1, keepdims=True)
        kernel = jnp.where((hits > 0) | (own == own_first + p), 0.0, kernel)
        for k in range(banks):
            there = (panel == per_dev * k + lane // rank) & (lane < per_dev * rank)
            mix[k, p : p + 1] = jnp.sum(jnp.where(there, kernel, 0.0), axis=0, keepdims=True)
    done.append(copies.start(mix, weights))
    for copy in done:
        copy.wait()


def tables_call(codes, centers, pairs, reaction, lanes, banks):
    cells = reaction.size
    inverse = jax.ShapeDtypeStruct((*reaction.shape, lanes), F32)
    spread = jax.ShapeDtypeStruct((cells, codes.shape[1]), BF16)
    weights = jax.ShapeDtypeStruct((banks, pairs.shape[0], 128), F32)
    return kernel_call(
        tables_body,
        [codes, centers, pairs, reaction],
        [spread, weights, inverse],
        [
            (codes.shape, jnp.int32),
            (centers.shape, F32),
            (pairs.shape, jnp.int32),
            (reaction.shape, F32),
            (spread.shape, BF16),
            (weights.shape, F32),
            (inverse.shape, F32),
        ],
        7,
        1 << 20,
        "tables",
    )


def fem_body(last, *refs):
    marks = whereabouts()
    state, source, inverse, spread, returned = refs[:5]
    first, second, near, inner, outer = refs[5:10]
    if last:
        out = refs[10]
        padded, load, scale, wide, back, rim, side, coupled, fresh, sems = refs[11:]
    else:
        take, out = refs[10:12]
        outs = refs[12:17]
        padded, load, scale, wide, back, rim, side, coupled, fresh = refs[17:26]
        picks, chosen, rims, sides, sems = refs[26:]
    cx, cy, cz, lanes = state.shape
    rows = inner.shape[0] - cz
    copies = Copies(sems)
    early = [copies.start(spread, wide), copies.start(returned.at[:, pl.ds(CAP, CAP)], back)]
    late = [
        copies.start(first, rim.at[1 - marks[0]]),
        copies.start(second, rim.at[marks[0]]),
        copies.start(near, side.at[2]),
        copies.start(inner.at[pl.ds(rows, cz)], side.at[0]),
        copies.start(outer.at[pl.ds(rows, cz)], side.at[1]),
        copies.start(state, padded.at[pl.ds(1, cx), pl.ds(1, cy)]),
        copies.start(source, load),
        copies.start(inverse, scale),
    ]
    if not last:
        picking = copies.start(take, picks)
    for copy in early:
        copy.wait()
    coupled[...] = matmul(wide[...], back[...].reshape(-1, lanes), ((1,), (0,)))
    for copy in late:
        copy.wait()
    padded[0, 1 : cy + 1] = rim[0].astype(F32)
    padded[cx + 1, 1 : cy + 1] = rim[1].astype(F32)
    far, close = marks[1] * (cy + 1), (1 - marks[1]) * (cy + 1)
    held = jnp.full((cz, lanes), marks[4].astype(jnp.int32), jnp.int32) > 0
    for i in range(cx):
        part = side[marks[3], :, i * lanes : (i + 1) * lanes].astype(F32)
        padded[i + 1, far] = jnp.where(held, part, 0.0)
        padded[i + 1, close] = side[2, :, i * lanes : (i + 1) * lanes].astype(F32)
    depth = lax.broadcasted_iota(jnp.int32, (cz, lanes), 0)

    def plane(m, carry):
        i, j = m // cy, m % cy
        here = padded[i + 1, j + 1]
        beside = padded[i + 2, j + 1] + padded[i, j + 1]
        beside = beside + padded[i + 1, j + 2] + padded[i + 1, j]
        beside = beside + jnp.where(depth == cz - 1, 0.0, pltpu.roll(here, cz - 1, 0))
        beside = beside + jnp.where(depth == 0, 0.0, pltpu.roll(here, 1, 0))
        start = pl.multiple_of(m * cz, cz)
        value = load[i, j] + beside - coupled[pl.ds(start, cz), :]
        fresh[i, j] = value * scale[i, j]
        return carry

    lax.fori_loop(0, cx * cy, plane, 0, unroll=4)
    done = [copies.start(fresh, out)]
    if not last:
        picking.wait()
        done += write_edges(fresh, picks, outs, chosen, rims, sides, marks, copies)
    for copy in done:
        copy.wait()


def fem_call(state, source, inverse, spread, returned, halos, take, last):
    cx, cy, cz, lanes = state.shape
    outs = [jax.ShapeDtypeStruct(state.shape, F32)]
    ins = [state, source, inverse, spread, returned, *halos]
    scratch = [
        ((cx + 2, cy + 2, cz, lanes), F32),
        (state.shape, F32),
        (state.shape, F32),
        (spread.shape, BF16),
        ((returned.shape[0], CAP, lanes), BF16),
        ((2, cy, cz, lanes), BF16),
        ((3, cz, cx * lanes), BF16),
        ((cx * cy * cz, lanes), F32),
        (state.shape, F32),
    ]
    if not last:
        ins.append(take)
        outs += edge_shapes(state, take.shape[0])
        scratch += [(take.shape, BF16)] + edge_scratch(state, take.shape[0])
    return kernel_call(
        functools.partial(fem_body, last),
        ins,
        outs,
        scratch,
        17,
        4 * spread.size * lanes,
        "fem_last" if last else "fem_step",
    )


def share_of(whole, part, start):
    return whole if whole.shape == part.shape else whole.at[pl.ds(start, part.shape[0])]


def update_body(last, *refs):
    summed, density, source, diagonal = refs[:4]
    copies = None
    if last:
        out = refs[4]
        terms, here, load, scale, fresh, sems = refs[5:]
    else:
        right, out, spread, moment = refs[4:8]
        terms, here, load, scale, fresh, factor, narrow, short, sems = refs[8:]
    copies = Copies(sems)
    ins = [
        copies.start(summed, terms),
        copies.start(share_of(density, here, pl.multiple_of(lax.axis_index("fem") * here.shape[0], here.shape[0])), here),
        copies.start(share_of(source, load, pl.multiple_of(lax.axis_index("fem") * load.shape[0], load.shape[0])), load),
        copies.start(diagonal, scale),
    ]
    if not last:
        ins.append(copies.start(share_of(right, factor, first_panel(factor)), factor))
    for copy in ins:
        copy.wait()
    applied = jnp.sum(terms[...].astype(F32), axis=0)
    value = here[...] + (load[...] - applied) / scale[...]
    fresh[...] = value
    done = [copies.start(fresh, out)]
    if not last:
        rounded = value.astype(BF16)
        for k in range(narrow.shape[0]):
            narrow[k] = rounded
        done.append(copies.start(narrow, spread))
        short[...] = moments(rounded, factor).astype(BF16)
        done.append(copies.start(short, moment))
    for copy in done:
        copy.wait()


def update_call(summed, density, source, diagonal, right, per_dev, last):
    shape = summed.shape[1:]
    outs = [jax.ShapeDtypeStruct(shape, F32)]
    ins = [summed, density, source, diagonal]
    scratch = [
        (summed.shape, BF16),
        (shape, F32),
        (shape, F32),
        (diagonal.shape, F32),
        (shape, F32),
    ]
    if not last:
        ins.append(right)
        outs += [
            jax.ShapeDtypeStruct(summed.shape, BF16),
            jax.ShapeDtypeStruct((shape[0], 128), BF16),
        ]
        scratch += [
            ((per_dev, *right.shape[1:]), BF16),
            (summed.shape, BF16),
            ((shape[0], 128), BF16),
        ]
    return kernel_call(
        functools.partial(update_body, last),
        ins,
        outs,
        scratch,
        8,
        1 << 20,
        "update_last" if last else "update",
    )


def pick_body(first, *refs):
    marks = whereabouts()
    full, hot, values, moment, rows, sent, inner, outer = refs[:8]
    if first:
        out, whole, mask, chosen, short, sides, packed, coded, sems = refs[8:]
    else:
        whole, mask, chosen, short, sides, packed, sems = refs[8:]
    copies = Copies(sems)
    get = copies.start(hot, coded if first else mask)
    ins = [
        copies.start(full, whole),
        copies.start(rows, sides),
        copies.start(values, chosen),
        copies.start(moment, short),
    ]
    get.wait()
    done = []
    if first:
        digits = coded[...].reshape(mask.shape[0], -1).astype(F32)
        code = (digits[:, :1] * 32.0 + digits[:, 1:2]).astype(jnp.int32)
        ids = lax.broadcasted_iota(jnp.int32, mask.shape, 1) + 1
        mask[...] = (code == ids).astype(F32).astype(BF16)
        done.append(copies.start(mask, out))
    for copy in ins:
        copy.wait()
    height = whole.shape[0]
    cz = sides.shape[1]
    for target, which in ((inner, 1 - marks[2]), (outer, marks[2])):
        done.append(copies.start(whole, target.at[pl.ds(0, height)]))
        done.append(copies.start(sides.at[which], target.at[pl.ds(height, cz)]))
    banks, lanes = packed.shape[0], packed.shape[2]
    picked = matmul(mask[...], whole[...], ((1,), (1,))).astype(BF16)
    packed[:, :CAP] = chosen[...].reshape(banks, CAP, lanes)
    packed[:, CAP : 2 * CAP] = picked.reshape(banks, CAP, lanes)
    for bank in range(banks):
        packed[bank, 2 * CAP :] = short[...]
    done.append(copies.start(packed, sent))
    for copy in done:
        copy.wait()


def pick_call(full, hot, values, moment, rows, banks):
    first = hot.ndim == 3
    lanes, width = full.shape
    mask = jax.ShapeDtypeStruct((values.shape[0], width), BF16)
    sent = jax.ShapeDtypeStruct((banks, 2 * CAP + moment.shape[0], lanes), BF16)
    swap = jax.ShapeDtypeStruct((lanes + rows.shape[1], width), BF16)
    scratch = [(full.shape, BF16), (mask.shape, BF16), (values.shape, BF16)]
    scratch += [(moment.shape, BF16), (rows.shape, BF16), (sent.shape, BF16)]
    if first:
        scratch.append((hot.shape, BF16))
    return kernel_call(
        functools.partial(pick_body, first),
        [full, hot, values, moment, rows],
        [sent, swap, swap] + [mask] * first,
        scratch,
        11,
        2 * mask.size * lanes,
        "pick_first" if first else "pick",
    )


def exchange(x, axis):
    return lax.all_to_all(x, axis, split_axis=0, concat_axis=0, tiled=True)


def swaps(x_first, x_second, axis):
    size = lax.axis_size(axis)
    inner = [(i, i ^ 1) for i in range(size)]
    outer = [(i, i + 1) if i % 2 else (i, i - 1) for i in range(1, size - 1)]
    return lax.ppermute(x_first, axis, inner), lax.ppermute(x_second, axis, outer)


def chip_swaps(x_inner, x_outer, axis):
    size = lax.axis_size(axis)
    inner = [(i, i ^ 2) for i in range(size)]
    outer = [(i, (i + 2 if i // 2 % 2 else i - 2) % size) for i in range(size)]
    return lax.ppermute(x_inner, axis, inner), lax.ppermute(x_outer, axis, outer)


def ordered(x, *others):
    return lax.optimization_barrier((x, others))[0]


def partner(x, axis):
    return lax.ppermute(x, axis, [(i, i ^ 1) for i in range(lax.axis_size(axis))])


def shards(
    fem_field,
    fem_source,
    reaction,
    bem_density,
    bem_source,
    bem_diagonal,
    near_blocks,
    near_pairs,
    low_left,
    low_right,
    centers,
    trace_cell,
    trace_bank,
    trace_row,
):
    fem_count = lax.axis_size("fem")
    bem_count = lax.axis_size("bem")
    excitations, local_rows = bem_density.shape
    share = excitations // fem_count
    per_dev, group, panel_rows, _ = near_blocks.shape
    bank = trace_bank.reshape(1, -1)
    asked = exchange(index_call(bank, trace_row.reshape(1, -1), bem_count, excitations), "bem")
    take, codes, moment, values, *edges = setup_call(
        bank,
        trace_cell.reshape(1, -1),
        fem_field,
        bem_density,
        low_right,
        bem_count,
        share,
        per_dev,
    )
    spread, weights, inverse = tables_call(
        codes, centers.T, near_pairs, reaction, excitations, bem_count
    )

    diag_row = bem_diagonal[None, :]

    full = bem_density.astype(BF16)
    fem_state, density, hot = fem_field, bem_density, asked
    for sweep in range(ITERS):
        last = sweep == ITERS - 1
        if sweep > 0:
            full = exchange(copies, "fem").reshape(excitations, local_rows)
        first, second, rows, near = edges
        sent, inner, outer, *mask = pick_call(full, hot, values, moment, rows, bem_count)
        if mask:
            (hot,) = mask
        inner, outer = chip_swaps(inner, outer, "bem")
        received = exchange(sent, "bem")
        other_inner, other_outer = partner(inner, "bem"), partner(outer, "bem")
        parts = [inner, other_inner, full, partner(full, "bem"), outer, other_outer]
        first, second, near = ordered((first, second, near), sent)
        halos = swaps(first, second, "fem") + (partner(near, "bem"),)
        weights = gate_call(weights, received, *halos, *([spread] if sweep == 0 else []))
        partial = near_call(near_pairs, parts, near_blocks, received, hot, weights, low_left)
        summed = exchange(partial.reshape(fem_count, share, local_rows), "fem")
        fem_state, *rest = fem_call(
            ordered(fem_state, partial),
            fem_source,
            inverse,
            spread,
            received,
            (*halos, other_inner, other_outer),
            take,
            last,
        )
        density, *more = update_call(
            ordered(summed, fem_state),
            density,
            bem_source,
            diag_row,
            low_right,
            per_dev,
            last,
        )
        if not last:
            copies, moment = more
            values, *edges = rest
    return (fem_state, density)


def solution(mesh):
    return jax.shard_map(
        shards,
        mesh=mesh,
        in_specs=(
            P("fem", "bem", None, None),
            P("fem", "bem", None, None),
            P("fem", "bem", None),
            P(None, "bem"),
            P(None, "bem"),
            P("bem"),
            P("bem", "fem", None, None),
            P("bem", None),
            P("bem", None, None),
            P(),
            P(),
            P(("fem", "bem")),
            P(("fem", "bem"), None),
            P(("fem", "bem")),
        ),
        out_specs=(P("fem", "bem", None, None), P("fem", "bem")),
        check_vma=False,
    )
```

time: 203 us -> 170 us (0.84)
  starting transfers between devices: 99.6 us -> 68.5 us
  blocking collectives: 0 us -> 22.1 us
  other arithmetic: 11.5 us -> 1.78 us
  waiting for transfers between devices: 29.2 us -> 19.8 us
  local copies, waits for them, and re-layouts: 8.33 us -> 0 us
  Pallas kernels: 51.1 us -> 55 us
    all_to_all x0 -> x2, blocking collectives: none -> 22.1 us  [exchange(): return lax.all_to_all(x, axis, split_axis=0, concat_axis=0, tiled=True)]
    ppermute x6 -> x3, starting transfers between devices: 29.1 us -> 10.2 us  [swaps(): lax.ppermute(x_second, axis, outer)]
    all_to_all x9 -> x7, starting transfers between devices: 56.7 us -> 41.6 us  [exchange(): return lax.all_to_all(x, axis, split_axis=0, concat_axis=0, tiled=True)]
    ppermute x6 -> x3, waiting for transfers between devices: 11.3 us -> 0.01 us  [swaps(): lax.ppermute(x_second, axis, outer)]
    all_to_all x9 -> x7, waiting for transfers between devices: 15 us -> 4.5 us  [exchange(): return lax.all_to_all(x, axis, split_axis=0, concat_axis=0, tiled=True)]
    ppermute x6 -> x3, waiting for transfers between devices: 0.02 us -> 9 us  [swaps(): lax.ppermute(x_first, axis, inner)]
    dynamic_slice x4 -> x0, local copies, waits for them, and re-layouts: 5.15 us -> none  [the longest x1 1.48 us: shards(): density = lax.dynamic_slice_in_dim(bem_density, first_col, share, 0)]
    pallas_call x13 -> x15, Pallas kernels: 51.1 us -> 55 us  [kernel_call(): pl.pallas_call(body, out_shape=outs, in_specs=[scalar] * len(smem) + [hbm...]
  transfers between devices with their start and end apart: 36 -> 31, of which waited for: 12 -> 15; matrix products, arithmetic and copies ran while one was open for 9% -> 1% of each run, Pallas kernels for 15% -> 14%
where the time goes in v2:
time: 170 us; the launch traced here: 168 us
  starting transfers between devices  68.5 us (40%)
  Pallas kernels  55 us (32%)
  blocking collectives  22.1 us (13%)
  waiting for transfers between devices  19.8 us (12%)
  other arithmetic  1.78 us (1%)
    pallas_call x15, Pallas kernels, kernel_call(): pl.pallas_call(body, out_shape=outs, in_specs=[scalar] * len(smem) + [hbm...  55 us
    all_to_all x7, starting transfers between devices, exchange(): return lax.all_to_all(x, axis, split_axis=0, concat_axis=0, tiled=True)  41.6 us
    all_to_all x2, blocking collectives, exchange(): return lax.all_to_all(x, axis, split_axis=0, concat_axis=0, tiled=True)  22.1 us
    ppermute x3, starting transfers between devices, swaps(): lax.ppermute(x_second, axis, outer)  10.2 us
    ppermute x3, waiting for transfers between devices, swaps(): lax.ppermute(x_first, axis, inner)  9 us
    ppermute x3, starting transfers between devices, chip_swaps(): lax.ppermute(x_outer, axis, outer)  7.54 us
    ppermute x12, waiting for transfers between devices, partner(): lax.ppermute(x, axis, [(i, i ^ 1) for i in range(lax.axis_size(axis))])  6.29 us
    all_to_all x7, waiting for transfers between devices, exchange(): return lax.all_to_all(x, axis, split_axis=0, concat_axis=0, tiled=True)  4.5 us
  transfers between devices with their start and end apart: 31, of which 15 were waited for; matrix products, arithmetic and copies ran while one was open for 1% of the time, Pallas kernels for 14%

profile of v2, /device:TPU:24, one launch (start us, length us, event | category | flops | bytes accessed | tf_op | source)
XLA Modules:
  0.0 168.2 jit_solution(14685997547922453341)
XLA Ops:
  2.5 8.3 %all-to-all-start = ((bf16[16,32,128]{2,1,0:T(8,128)(2,1)}), bf16[16,32,128]{2,1,0:T(8,128)(2,1)}, u32[]{:S(2)}, u32[]{:S(2)}) async-start(bf16[16,32,128]{2,1,0:T(8,128)(2,1)} %index.1), calls=%async_computation | async-start | bytes 262144 | tf_op jit(solution)/shard_map/all_to_all | solution.py:643
  12.6 3.1 %setup.1 = (bf16[512,2048]{1,0:T(8,128)(2,1)}, s32[1,512]{1,0:T(1,128)}, bf16[16,128]{1,0:T(8,128)(2,1)}, bf16[512,128]{1,0:T(8,128)(2,1)}, bf16[8,32,128]{2,1,0...) custom-call(s32[1,256]{1,0:T(1,128)} %bitcast.23, ...), custom_call_target="tpu_custom_call" | custom-call | flops 268435456 | bytes 2623488 | tf_op jit(solution)/shard_map/setup/pallas_call | solution.py:26
  19.9 2.8 %collective-permute-start.3 = (bf16[160,1024]{1,0:T(8,128)(2,1)}, bf16[160,1024]{1,0:T(8,128)(2,1)}, u32[]{:S(2)}, u32[]{:S(2)}) collective-permute-start(bf16[160,1024]{1,0:T(8,128)(2,1)} %get-tuple-element.60), channel_id=1, source_target_pairs={{0,14},{1,15},{2,4},{3,5},{4,2},{5,3},{6,8},{7,9},{8,6},{9,7},{10,... | collective-permute-start | bytes 983048 | tf_op jit(solution)/shard_map/ppermute | solution.py:657
  22.8 6.2 %all-to-all-start.1 = ((bf16[16,80,128]{2,1,0:T(8,128)(2,1)}), bf16[16,80,128]{2,1,0:T(8,128)(2,1)}, u32[]{:S(2)}, u32[]{:S(2)}) async-start(bf16[16,80,128]{2,1,0:T(8,128)(2,1)} %get-tuple-element.61), calls=%async_computation.1 | async-start | bytes 655360 | tf_op jit(solution)/shard_map/all_to_all | solution.py:643
  29.7 4.1 %collective-permute-start.6 = (bf16[8,32,128]{2,1,0:T(8,128)(2,1)}, bf16[8,32,128]{2,1,0:T(8,128)(2,1)}, u32[]{:S(2)}, u32[]{:S(2)}) collective-permute-start(bf16[8,32,128]{2,1,0:T(8,128)(2,1)} %get-tuple-element.69), channel_id=1, source_target_pairs={{16,32},{32,16},{48,64},{64,48},{80,96},{96,80},{17,33},{33,17},{4... | collective-permute-start | bytes 196616 | tf_op jit(solution)/shard_map/ppermute | solution.py:650
  33.9 4.4 %tables.1 = (bf16[2048,512]{1,0:T(8,128)(2,1)}, f32[16,2,128]{2,1,0:T(2,128)}, f32[8,8,32,128]{3,2,1,0:T(8,128)}) custom-call(s32[1,512]{1,0:T(1,128)} %get-tuple-element.63.codes, f32[3,32]{1,0:T(4,128)} %bitcast.24, s32[2,48]{1,0:T(2,128)} %pairs.7, f32[8,8,32]{2,1,0:T(8,128)} %reaction.1), custom_call_target="tpu_custom_call" | custom-call | flops 1048576 | bytes 11008 | tf_op jit(solution)/shard_map/tables/pallas_call | solution.py:26
  41.3 5.5 %near.3 = bf16[128,1024]{1,0:T(8,128)(2,1)} custom-call(s32[2,48]{1,0:T(2,128)} %pairs.7, bf16[160,1024]{1,0:T(8,128)(2,1)} %collective-permute-done.refs_0_, bf16[160,1024]{1,0:T(8,128)(2,1)} %collective-permute-done.1.refs_1_.refs_8_, bf16[128,1024]{1,0:T(8,128)(2,1)} %convert_element_type.3.refs_0_.refs_2_, ...), custom_call_target="tpu_custom_call" | custom-call | flops 805306368 | bytes 9585024 | tf_op jit(solution)/shard_map/near/pallas_call | solution.py:26
  46.9 5.5 %all-to-all-start.2 = ((bf16[8,16,1024]{2,1,0:T(8,128)(2,1)}), bf16[8,16,1024]{2,1,0:T(8,128)(2,1)}, u32[]{:S(2)}, u32[]{:S(2)}) async-start(bf16[8,16,1024]{2,1,0:T(8,128)(2,1)} %bitcast.16), calls=%async_computation.2 | async-start | bytes 524288 | tf_op jit(solution)/shard_map/all_to_all | solution.py:643
  52.4 5.7 %fem_step.2 = (f32[8,8,32,128]{3,2,1,0:T(8,128)}, bf16[512,128]{1,0:T(8,128)(2,1)}, bf16[8,32,128]{2,1,0:T(8,128)(2,1)}, bf16[8,32,128]{2,1,0:T(8,128)(2,1)}, bf...) custom-call(f32[8,8,32,128]{3,2,1,0:T(8,128)} %refs_0_, f32[8,8,32,128]{3,2,1,0:T(8,128)} %refs_1_.7, ...), custom_call_target="tpu_custom_call" | custom-call | flops 536870912 | bytes 8519680 | tf_op jit(solution)/shard_map/fem_step/pallas_call | solution.py:26
  61.0 11.0 %all_to_all.45 = bf16[8,16,1024]{2,1,0:T(8,128)(2,1)} all-to-all(bf16[8,16,1024]{2,1,0:T(8,128)(2,1)} %get-tuple-element.77), channel_id=1, replica_groups=mesh['fem'=8,'bem'=16] {'fem'}, dimensions={0} | all-to-all | bytes 524288 | tf_op jit(solution)/shard_map/all_to_all | solution.py:643
  78.2 6.9 %all-to-all-start.4 = ((bf16[16,80,128]{2,1,0:T(8,128)(2,1)}), bf16[16,80,128]{2,1,0:T(8,128)(2,1)}, u32[]{:S(2)}, u32[]{:S(2)}) async-start(bf16[16,80,128]{2,1,0:T(8,128)(2,1)} %get-tuple-element.83), calls=%async_computation.4 | async-start | bytes 655360 | tf_op jit(solution)/shard_map/all_to_all | solution.py:643
  86.1 3.0 %collective-permute-start.14 = (bf16[8,32,128]{2,1,0:T(8,128)(2,1)}, bf16[8,32,128]{2,1,0:T(8,128)(2,1)}, u32[]{:S(2)}, u32[]{:S(2)}) collective-permute-start(bf16[8,32,128]{2,1,0:T(8,128)(2,1)} %get-tuple-element.88), channel_id=1, source_target_pairs={{16,32},{32,16},{48,64},{64,48},{80,96},{96,80},{17,33},{33,17},{4... | collective-permute-start | bytes 196616 | tf_op jit(solution)/shard_map/ppermute | solution.py:650
  89.2 4.6 %collective-permute-done.13.refs_2_.refs_5_ = bf16[8,32,128]{2,1,0:T(8,128)(2,1)} collective-permute-done((bf16[8,32,128]{2,1,0:T(8,128)(2,1)}, bf16[8,32,128]{2,1,0:T(8,128)(2,1)}, u32[]{:S(2)}, u32[]{:S(2)}) %collective-permute-start.13) | collective-permute-done | bytes 65568 | tf_op jit(solution)/shard_map/ppermute | solution.py:650
  96.6 5.5 %near.4 = bf16[128,1024]{1,0:T(8,128)(2,1)} custom-call(s32[2,48]{1,0:T(2,128)} %pairs.7, bf16[160,1024]{1,0:T(8,128)(2,1)} %collective-permute-done.8.refs_0_, bf16[160,1024]{1,0:T(8,128)(2,1)} %collective-permute-done.9.refs_1_.refs_8_, bf16[128,1024]{1,0:T(8,128)(2,1)} %bitcast.15, bf16[128,1024]{1,0:T(8,128)(2,1)} %collective-permute-done.10.refs_3_, ...), custom_call_target="tpu_custom_call" | custom-call | flops 805306368 | bytes 9585024 | tf_op jit(solution)/shard_map/near/pallas_call | solution.py:26
  102.1 4.1 %all-to-all-start.5 = ((bf16[8,16,1024]{2,1,0:T(8,128)(2,1)}), bf16[8,16,1024]{2,1,0:T(8,128)(2,1)}, u32[]{:S(2)}, u32[]{:S(2)}) async-start(bf16[8,16,1024]{2,1,0:T(8,128)(2,1)} %bitcast.17), calls=%async_computation.5 | async-start | bytes 524288 | tf_op jit(solution)/shard_map/all_to_all | solution.py:643
  106.2 5.6 %fem_step.3 = (f32[8,8,32,128]{3,2,1,0:T(8,128)}, bf16[512,128]{1,0:T(8,128)(2,1)}, bf16[8,32,128]{2,1,0:T(8,128)(2,1)}, bf16[8,32,128]{2,1,0:T(8,128)(2,1)}, bf...) custom-call(f32[8,8,32,128]{3,2,1,0:T(8,128)} %get-tuple-element.90.refs_0_, f32[8,8,32,128]{3,2,1,0:T(8,128)} %refs_1_.7, ...), custom_call_target="tpu_custom_call" | custom-call | flops 536870912 | bytes 8519680 | tf_op jit(solution)/shard_map/fem_step/pallas_call | solution.py:26
  114.6 11.1 %all_to_all.46 = bf16[8,16,1024]{2,1,0:T(8,128)(2,1)} all-to-all(bf16[8,16,1024]{2,1,0:T(8,128)(2,1)} %get-tuple-element.94), channel_id=1, replica_groups=mesh['fem'=8,'bem'=16] {'fem'}, dimensions={0} | all-to-all | bytes 524288 | tf_op jit(solution)/shard_map/all_to_all | solution.py:643
  129.8 2.6 %collective-permute-start.19 = (bf16[160,1024]{1,0:T(8,128)(2,1)}, bf16[160,1024]{1,0:T(8,128)(2,1)}, u32[]{:S(2)}, u32[]{:S(2)}) collective-permute-start(bf16[160,1024]{1,0:T(8,128)(2,1)} %get-tuple-element.99), channel_id=1, source_target_pairs={{0,14},{1,15},{2,4},{3,5},{4,2},{5,3},{6,8},{7,9},{8,6},{9,7},{10,... | collective-permute-start | bytes 983048 | tf_op jit(solution)/shard_map/ppermute | solution.py:657
  132.5 6.4 %all-to-all-start.7 = ((bf16[16,80,128]{2,1,0:T(8,128)(2,1)}), bf16[16,80,128]{2,1,0:T(8,128)(2,1)}, u32[]{:S(2)}, u32[]{:S(2)}) async-start(bf16[16,80,128]{2,1,0:T(8,128)(2,1)} %get-tuple-element.100), calls=%async_computation.7 | async-start | bytes 655360 | tf_op jit(solution)/shard_map/all_to_all | solution.py:643
  139.7 3.1 %collective-permute-start.22 = (bf16[8,32,128]{2,1,0:T(8,128)(2,1)}, bf16[8,32,128]{2,1,0:T(8,128)(2,1)}, u32[]{:S(2)}, u32[]{:S(2)}) collective-permute-start(bf16[8,32,128]{2,1,0:T(8,128)(2,1)} %get-tuple-element.105), channel_id=1, source_target_pairs={{16,32},{32,16},{48,64},{64,48},{80,96},{96,80},{17,33},{33,17},{4... | collective-permute-start | bytes 196616 | tf_op jit(solution)/shard_map/ppermute | solution.py:650
  142.9 4.4 %collective-permute-done.21.refs_2_.refs_5_ = bf16[8,32,128]{2,1,0:T(8,128)(2,1)} collective-permute-done((bf16[8,32,128]{2,1,0:T(8,128)(2,1)}, bf16[8,32,128]{2,1,0:T(8,128)(2,1)}, u32[]{:S(2)}, u32[]{:S(2)}) %collective-permute-start.21) | collective-permute-done | bytes 65568 | tf_op jit(solution)/shard_map/ppermute | solution.py:650
  150.1 5.5 %near.5 = bf16[128,1024]{1,0:T(8,128)(2,1)} custom-call(s32[2,48]{1,0:T(2,128)} %pairs.7, bf16[160,1024]{1,0:T(8,128)(2,1)} %collective-permute-done.16.refs_0_, bf16[160,1024]{1,0:T(8,128)(2,1)} %collective-permute-done.17.refs_1_.refs_8_, bf16[128,1024]{1,0:T(8,128)(2,1)} %bitcast.12, bf16[128,1024]{1,0:T(8,128)(2,1)} %collective-permute-done.18.refs_3_, ...), custom_call_target="tpu_custom_call" | custom-call | flops 805306368 | bytes 9585024 | tf_op jit(solution)/shard_map/near/pallas_call | solution.py:26
  155.7 4.2 %all-to-all-start.8 = ((bf16[8,16,1024]{2,1,0:T(8,128)(2,1)}), bf16[8,16,1024]{2,1,0:T(8,128)(2,1)}, u32[]{:S(2)}, u32[]{:S(2)}) async-start(bf16[8,16,1024]{2,1,0:T(8,128)(2,1)} %bitcast.18), calls=%async_computation.8 | async-start | bytes 524288 | tf_op jit(solution)/shard_map/all_to_all | solution.py:643
  159.8 4.5 %fem_last.1 = f32[8,8,32,128]{3,2,1,0:T(8,128)} custom-call(f32[8,8,32,128]{3,2,1,0:T(8,128)} %get-tuple-element.107.refs_0_, f32[8,8,32,128]{3,2,1,0:T(8,128)} %refs_1_.7, f32[8,8,32,128]{3,2,1,0:T(8,128)} %get-tuple-element.73.refs_2_, bf16[2048,512]{1,0:T(8,128)(2,1)} %get-tuple-element.71.refs_5_.refs_3_, ...), custom_call_target="tpu_custom_call" | custom-call | flops 536870912 | bytes 6422528 | tf_op jit(solution)/shard_map/fem_last/pallas_call | solution.py:26
  (59 shorter events, 39.0 us)
Async XLA Ops:
  2.5 13.7 %all-to-all-start = ((bf16[16,32,128]{2,1,0:T(8,128)(2,1)}), bf16[16,32,128]{2,1,0:T(8,128)(2,1)}, u32[]{:S(2)}, u32[]{:S(2)}) async-start(bf16[16,32,128]{2,1,0:T(8,128)(2,1)} %index.1), calls=%async_computation | async-start | bytes 262144 | tf_op jit(solution)/shard_map/all_to_all | solution.py:643
  18.9 20.0 %collective-permute-start = (bf16[160,1024]{1,0:T(8,128)(2,1)}, bf16[160,1024]{1,0:T(8,128)(2,1)}, u32[]{:S(2)}, u32[]{:S(2)}) collective-permute-start(bf16[160,1024]{1,0:T(8,128)(2,1)} %get-tuple-element.59), channel_id=1, source_target_pairs={{0,2},{1,3},{2,0},{3,1},{4,6},{5,7},{6,4},{7,5},{8,10},{9,11},{10,... | collective-permute-start | bytes 983048 | tf_op jit(solution)/shard_map/ppermute | solution.py:657
  19.9 19.1 %collective-permute-start.3 = (bf16[160,1024]{1,0:T(8,128)(2,1)}, bf16[160,1024]{1,0:T(8,128)(2,1)}, u32[]{:S(2)}, u32[]{:S(2)}) collective-permute-start(bf16[160,1024]{1,0:T(8,128)(2,1)} %get-tuple-element.60), channel_id=1, source_target_pairs={{0,14},{1,15},{2,4},{3,5},{4,2},{5,3},{6,8},{7,9},{8,6},{9,7},{10,... | collective-permute-start | bytes 983048 | tf_op jit(solution)/shard_map/ppermute | solution.py:657
  22.8 16.7 %all-to-all-start.1 = ((bf16[16,80,128]{2,1,0:T(8,128)(2,1)}), bf16[16,80,128]{2,1,0:T(8,128)(2,1)}, u32[]{:S(2)}, u32[]{:S(2)}) async-start(bf16[16,80,128]{2,1,0:T(8,128)(2,1)} %get-tuple-element.61), calls=%async_computation.1 | async-start | bytes 655360 | tf_op jit(solution)/shard_map/all_to_all | solution.py:643
  29.0 9.3 %collective-permute-start.5 = (bf16[8,32,128]{2,1,0:T(8,128)(2,1)}, bf16[8,32,128]{2,1,0:T(8,128)(2,1)}, u32[]{:S(2)}, u32[]{:S(2)}) collective-permute-start(bf16[8,32,128]{2,1,0:T(8,128)(2,1)} %get-tuple-element.68), channel_id=1, source_target_pairs={{0,16},{16,0},{32,48},{48,32},{64,80},{80,64},{96,112},{112,96},{1... | collective-permute-start | bytes 196616 | tf_op jit(solution)/shard_map/ppermute | solution.py:650
  29.7 9.7 %collective-permute-start.6 = (bf16[8,32,128]{2,1,0:T(8,128)(2,1)}, bf16[8,32,128]{2,1,0:T(8,128)(2,1)}, u32[]{:S(2)}, u32[]{:S(2)}) collective-permute-start(bf16[8,32,128]{2,1,0:T(8,128)(2,1)} %get-tuple-element.69), channel_id=1, source_target_pairs={{16,32},{32,16},{48,64},{64,48},{80,96},{96,80},{17,33},{33,17},{4... | collective-permute-start | bytes 196616 | tf_op jit(solution)/shard_map/ppermute | solution.py:650
  33.8 5.6 %collective-permute-start.7 = (bf16[32,1024]{1,0:T(8,128)(2,1)}, bf16[32,1024]{1,0:T(8,128)(2,1)}, u32[]{:S(2)}, u32[]{:S(2)}) collective-permute-start(bf16[32,1024]{1,0:T(8,128)(2,1)} %get-tuple-element.70), channel_id=1, source_target_pairs={{0,1},{1,0},{2,3},{3,2},{4,5},{5,4},{6,7},{7,6},{8,9},{9,8},{10,11... | collective-permute-start | bytes 196616 | tf_op jit(solution)/shard_map/ppermute | solution.py:665
  46.9 12.2 %all-to-all-start.2 = ((bf16[8,16,1024]{2,1,0:T(8,128)(2,1)}), bf16[8,16,1024]{2,1,0:T(8,128)(2,1)}, u32[]{:S(2)}, u32[]{:S(2)}) async-start(bf16[8,16,1024]{2,1,0:T(8,128)(2,1)} %bitcast.16), calls=%async_computation.2 | async-start | bytes 524288 | tf_op jit(solution)/shard_map/all_to_all | solution.py:643
  74.6 19.1 %collective-permute-start.8 = (bf16[160,1024]{1,0:T(8,128)(2,1)}, bf16[160,1024]{1,0:T(8,128)(2,1)}, u32[]{:S(2)}, u32[]{:S(2)}) collective-permute-start(bf16[160,1024]{1,0:T(8,128)(2,1)} %get-tuple-element.81), channel_id=1, source_target_pairs={{0,2},{1,3},{2,0},{3,1},{4,6},{5,7},{6,4},{7,5},{8,10},{9,11},{10,... | collective-permute-start | bytes 983048 | tf_op jit(solution)/shard_map/ppermute | solution.py:657
  76.1 18.1 %collective-permute-start.11 = (bf16[160,1024]{1,0:T(8,128)(2,1)}, bf16[160,1024]{1,0:T(8,128)(2,1)}, u32[]{:S(2)}, u32[]{:S(2)}) collective-permute-start(bf16[160,1024]{1,0:T(8,128)(2,1)} %get-tuple-element.82), channel_id=1, source_target_pairs={{0,14},{1,15},{2,4},{3,5},{4,2},{5,3},{6,8},{7,9},{8,6},{9,7},{10,... | collective-permute-start | bytes 983048 | tf_op jit(solution)/shard_map/ppermute | solution.py:657
  78.2 16.1 %all-to-all-start.4 = ((bf16[16,80,128]{2,1,0:T(8,128)(2,1)}), bf16[16,80,128]{2,1,0:T(8,128)(2,1)}, u32[]{:S(2)}, u32[]{:S(2)}) async-start(bf16[16,80,128]{2,1,0:T(8,128)(2,1)} %get-tuple-element.83), calls=%async_computation.4 | async-start | bytes 655360 | tf_op jit(solution)/shard_map/all_to_all | solution.py:643
  85.2 8.6 %collective-permute-start.13 = (bf16[8,32,128]{2,1,0:T(8,128)(2,1)}, bf16[8,32,128]{2,1,0:T(8,128)(2,1)}, u32[]{:S(2)}, u32[]{:S(2)}) collective-permute-start(bf16[8,32,128]{2,1,0:T(8,128)(2,1)} %get-tuple-element.87), channel_id=1, source_target_pairs={{0,16},{16,0},{32,48},{48,32},{64,80},{80,64},{96,112},{112,96},{1... | collective-permute-start | bytes 196616 | tf_op jit(solution)/shard_map/ppermute | solution.py:650
  86.1 8.2 %collective-permute-start.14 = (bf16[8,32,128]{2,1,0:T(8,128)(2,1)}, bf16[8,32,128]{2,1,0:T(8,128)(2,1)}, u32[]{:S(2)}, u32[]{:S(2)}) collective-permute-start(bf16[8,32,128]{2,1,0:T(8,128)(2,1)} %get-tuple-element.88), channel_id=1, source_target_pairs={{16,32},{32,16},{48,64},{64,48},{80,96},{96,80},{17,33},{33,17},{4... | collective-permute-start | bytes 196616 | tf_op jit(solution)/shard_map/ppermute | solution.py:650
  89.1 5.3 %collective-permute-start.15 = (bf16[32,1024]{1,0:T(8,128)(2,1)}, bf16[32,1024]{1,0:T(8,128)(2,1)}, u32[]{:S(2)}, u32[]{:S(2)}) collective-permute-start(bf16[32,1024]{1,0:T(8,128)(2,1)} %get-tuple-element.89), channel_id=1, source_target_pairs={{0,1},{1,0},{2,3},{3,2},{4,5},{5,4},{6,7},{7,6},{8,9},{9,8},{10,11... | collective-permute-start | bytes 196616 | tf_op jit(solution)/shard_map/ppermute | solution.py:665
  93.7 2.3 %collective-permute-start.9 = (bf16[160,1024]{1,0:T(8,128)(2,1)}, bf16[160,1024]{1,0:T(8,128)(2,1)}, u32[]{:S(2)}, u32[]{:S(2)}) collective-permute-start(bf16[160,1024]{1,0:T(8,128)(2,1)} %collective-permute-done.8.refs_0_), channel_id=1, source_target_pairs={{0,1},{1,0},{2,3},{3,2},{4,5},{5,4},{6,7},{7,6},{8,9},{9,8},{10,11... | collective-permute-start | bytes 983048 | tf_op jit(solution)/shard_map/ppermute | solution.py:665
  102.1 10.6 %all-to-all-start.5 = ((bf16[8,16,1024]{2,1,0:T(8,128)(2,1)}), bf16[8,16,1024]{2,1,0:T(8,128)(2,1)}, u32[]{:S(2)}, u32[]{:S(2)}) async-start(bf16[8,16,1024]{2,1,0:T(8,128)(2,1)} %bitcast.17), calls=%async_computation.5 | async-start | bytes 524288 | tf_op jit(solution)/shard_map/all_to_all | solution.py:643
  128.3 19.1 %collective-permute-start.16 = (bf16[160,1024]{1,0:T(8,128)(2,1)}, bf16[160,1024]{1,0:T(8,128)(2,1)}, u32[]{:S(2)}, u32[]{:S(2)}) collective-permute-start(bf16[160,1024]{1,0:T(8,128)(2,1)} %get-tuple-element.98), channel_id=1, source_target_pairs={{0,2},{1,3},{2,0},{3,1},{4,6},{5,7},{6,4},{7,5},{8,10},{9,11},{10,... | collective-permute-start | bytes 983048 | tf_op jit(solution)/shard_map/ppermute | solution.py:657
  129.8 18.0 %collective-permute-start.19 = (bf16[160,1024]{1,0:T(8,128)(2,1)}, bf16[160,1024]{1,0:T(8,128)(2,1)}, u32[]{:S(2)}, u32[]{:S(2)}) collective-permute-start(bf16[160,1024]{1,0:T(8,128)(2,1)} %get-tuple-element.99), channel_id=1, source_target_pairs={{0,14},{1,15},{2,4},{3,5},{4,2},{5,3},{6,8},{7,9},{8,6},{9,7},{10,... | collective-permute-start | bytes 983048 | tf_op jit(solution)/shard_map/ppermute | solution.py:657
  132.5 15.5 %all-to-all-start.7 = ((bf16[16,80,128]{2,1,0:T(8,128)(2,1)}), bf16[16,80,128]{2,1,0:T(8,128)(2,1)}, u32[]{:S(2)}, u32[]{:S(2)}) async-start(bf16[16,80,128]{2,1,0:T(8,128)(2,1)} %get-tuple-element.100), calls=%async_computation.7 | async-start | bytes 655360 | tf_op jit(solution)/shard_map/all_to_all | solution.py:643
  138.8 8.5 %collective-permute-start.21 = (bf16[8,32,128]{2,1,0:T(8,128)(2,1)}, bf16[8,32,128]{2,1,0:T(8,128)(2,1)}, u32[]{:S(2)}, u32[]{:S(2)}) collective-permute-start(bf16[8,32,128]{2,1,0:T(8,128)(2,1)} %get-tuple-element.104), channel_id=1, source_target_pairs={{0,16},{16,0},{32,48},{48,32},{64,80},{80,64},{96,112},{112,96},{1... | collective-permute-start | bytes 196616 | tf_op jit(solution)/shard_map/ppermute | solution.py:650
  139.7 8.2 %collective-permute-start.22 = (bf16[8,32,128]{2,1,0:T(8,128)(2,1)}, bf16[8,32,128]{2,1,0:T(8,128)(2,1)}, u32[]{:S(2)}, u32[]{:S(2)}) collective-permute-start(bf16[8,32,128]{2,1,0:T(8,128)(2,1)} %get-tuple-element.105), channel_id=1, source_target_pairs={{16,32},{32,16},{48,64},{64,48},{80,96},{96,80},{17,33},{33,17},{4... | collective-permute-start | bytes 196616 | tf_op jit(solution)/shard_map/ppermute | solution.py:650
  142.8 5.1 %collective-permute-start.23 = (bf16[32,1024]{1,0:T(8,128)(2,1)}, bf16[32,1024]{1,0:T(8,128)(2,1)}, u32[]{:S(2)}, u32[]{:S(2)}) collective-permute-start(bf16[32,1024]{1,0:T(8,128)(2,1)} %get-tuple-element.106), channel_id=1, source_target_pairs={{0,1},{1,0},{2,3},{3,2},{4,5},{5,4},{6,7},{7,6},{8,9},{9,8},{10,11... | collective-permute-start | bytes 196616 | tf_op jit(solution)/shard_map/ppermute | solution.py:665
  147.3 2.3 %collective-permute-start.17 = (bf16[160,1024]{1,0:T(8,128)(2,1)}, bf16[160,1024]{1,0:T(8,128)(2,1)}, u32[]{:S(2)}, u32[]{:S(2)}) collective-permute-start(bf16[160,1024]{1,0:T(8,128)(2,1)} %collective-permute-done.16.refs_0_), channel_id=1, source_target_pairs={{0,1},{1,0},{2,3},{3,2},{4,5},{5,4},{6,7},{7,6},{8,9},{9,8},{10,11... | collective-permute-start | bytes 983048 | tf_op jit(solution)/shard_map/ppermute | solution.py:665
  155.7 10.7 %all-to-all-start.8 = ((bf16[8,16,1024]{2,1,0:T(8,128)(2,1)}), bf16[8,16,1024]{2,1,0:T(8,128)(2,1)}, u32[]{:S(2)}, u32[]{:S(2)}) async-start(bf16[8,16,1024]{2,1,0:T(8,128)(2,1)} %bitcast.18), calls=%async_computation.8 | async-start | bytes 524288 | tf_op jit(solution)/shard_map/all_to_all | solution.py:643
  (7 other events, 14.7 us)

commit v3 on v2

--- a/solution.py
+++ b/solution.py
@@ -176,7 +176,8 @@
     ]
     narrow = state[...].reshape(cx * cy * cz, lanes).astype(BF16)
     chosen[...] = matmul(take[...], narrow, ((1,), (0,))).astype(BF16)
-    done.append(copies.start(chosen, values))
+    if values is not None:
+        done.append(copies.start(chosen, values))
     return done
 
 
@@ -216,45 +217,19 @@
     return place_r, column(place_r), column
 
 
-def index_body(bank, row, sent, banks_v, rows_v, packed, sems):
-    copies = Copies(sems)
-    for copy in [copies.start(bank, banks_v), copies.start(row, rows_v)]:
-        copy.wait()
-    banks, cap, lanes = packed.shape
-    place_r, _, _ = slot_places(banks_v[...])
-    hit = lax.broadcasted_iota(jnp.int32, (banks * cap, bank.shape[1]), 0) == place_r
-    code = jnp.sum(jnp.where(hit, rows_v[...] + 1, 0), axis=1, keepdims=True)
-    lane = lax.broadcasted_iota(jnp.int32, (banks * cap, lanes), 1)
-    digits = jnp.where(lane == 0, code // 32, jnp.where(lane == 1, code % 32, 0))
-    packed[...] = digits.astype(F32).astype(BF16).reshape(banks, cap, lanes)
-    copies.start(packed, sent).wait()
-
-
-def index_call(bank, row, banks, lanes):
-    packed = (banks, CAP, lanes)
-    return kernel_call(
-        index_body,
-        [bank, row],
-        [jax.ShapeDtypeStruct(packed, BF16)],
-        [(bank.shape, jnp.int32), (row.shape, jnp.int32), (packed, BF16)],
-        3,
-        1 << 20,
-        "index",
-    )[0]
-
-
 def first_panel(part):
     return lax.axis_index("bem") * part.shape[0]
 
 
 def setup_body(*refs):
     marks = whereabouts()
-    bank, cell, state, density, right = refs[:5]
-    take, codes, moment = refs[5:8]
-    outs = refs[8:13]
-    banks_v, cells_v, here, share_v, factor, picks, coded, short, chosen, rims, sides, sems = refs[13:]
+    bank, cell, row, state, density, right = refs[:6]
+    take, codes, sent = refs[6:9]
+    outs = refs[9:13]
+    banks_v, cells_v, rows_v, here, share_v, factor, picks, coded, packed = refs[13:22]
+    chosen, rims, sides, sems = refs[22:]
     copies = Copies(sems)
-    small = [copies.start(bank, banks_v), copies.start(cell, cells_v)]
+    small = [copies.start(bank, banks_v), copies.start(cell, cells_v), copies.start(row, rows_v)]
     share = share_v.shape[0]
     start = pl.multiple_of(lax.axis_index("fem") * share, share)
     large = [
@@ -266,10 +241,15 @@
         copy.wait()
     slots = bank.shape[1]
     places, cells = take.shape
+    banks, _, lanes = packed.shape
     cell_r = cells_v[...] + 1
     place_r, place_c, column = slot_places(banks_v[...])
     hit = lax.broadcasted_iota(jnp.int32, (places, slots), 0) == place_r
     cell_c = jnp.sum(jnp.where(hit, cell_r, 0), axis=1, keepdims=True)
+    code = jnp.sum(jnp.where(hit, rows_v[...] + 1, 0), axis=1, keepdims=True)
+    lane = lax.broadcasted_iota(jnp.int32, (places, lanes), 1)
+    digits = jnp.where(lane == 0, code // 32, jnp.where(lane == 1, code % 32, 0))
+    packed[:, CAP : 2 * CAP] = digits.astype(F32).astype(BF16).reshape(banks, CAP, lanes)
     ids = lax.broadcasted_iota(jnp.int32, (places, cells), 1) + 1
     picks[...] = (cell_c == ids).astype(F32).astype(BF16)
     out = [copies.start(picks, take)]
@@ -278,36 +258,39 @@
     out.append(copies.start(coded, codes))
     for copy in large:
         copy.wait()
-    out += write_edges(here, picks, outs, chosen, rims, sides, marks, copies)
-    short[...] = moments(share_v[...].astype(BF16), factor).astype(BF16)
-    out.append(copies.start(short, moment))
+    out += write_edges(here, picks, (None, *outs), chosen, rims, sides, marks, copies)
+    packed[:, :CAP] = chosen[...].reshape(banks, CAP, lanes)
+    short = moments(share_v[...].astype(BF16), factor).astype(BF16)
+    for k in range(banks):
+        packed[k, 2 * CAP :] = short
+    out.append(copies.start(packed, sent))
     for copy in out:
         copy.wait()
 
 
-def setup_call(bank, cell, state, density, right, banks, share, per_dev):
+def setup_call(bank, cell, row, state, density, right, banks, share, per_dev):
     cx, cy, cz, lanes = state.shape
     slots = bank.shape[1]
     places = banks * CAP
     take = jax.ShapeDtypeStruct((places, cx * cy * cz), BF16)
+    sent = (banks, 2 * CAP + share, lanes)
     return kernel_call(
         setup_body,
-        [bank, cell, state, density, right],
+        [bank, cell, row, state, density, right],
         [
             take,
             jax.ShapeDtypeStruct((1, places), jnp.int32),
-            jax.ShapeDtypeStruct((share, 128), BF16),
+            jax.ShapeDtypeStruct(sent, BF16),
         ]
-        + edge_shapes(state, places),
-        [
-            ((1, slots), jnp.int32),
-            ((1, slots), jnp.int32),
+        + edge_shapes(state, places)[1:],
+        [((1, slots), jnp.int32)] * 3
+        + [
             (state.shape, F32),
             ((share, density.shape[1]), F32),
             ((per_dev, *right.shape[1:]), BF16),
             (take.shape, BF16),
             ((1, places), jnp.int32),
-            ((share, 128), BF16),
+            (sent, BF16),
         ]
         + edge_scratch(state, places),
         13,
@@ -326,19 +309,16 @@
     return jnp.concatenate(sums, axis=1)
 
 
-def tables_body(
-    codes, centers, pairs, reaction, spread, weights, inverse,
-    codes_v, places, listed_v, scale, wide, mix, full, sems,
-):
+def tables_body(codes, reaction, spread, inverse, codes_v, scale, wide, full, sems):
     copies = Copies(sems)
-    ins = [
-        copies.start(codes, codes_v),
-        copies.start(centers, places),
-        copies.start(pairs, listed_v),
-        copies.start(reaction, scale),
-    ]
-    for copy in ins:
-        copy.wait()
+    for copy in [copies.start(codes, codes_v), copies.start(reaction, scale)]:
+        copy.wait()
+    wanted = codes_v[...]
+    rows = 256
+    for k in range(wide.shape[0] // rows):
+        ids = lax.broadcasted_iota(jnp.int32, (rows, wanted.shape[1]), 0) + (k * rows + 1)
+        wide[k * rows : (k + 1) * rows] = (ids == wanted).astype(F32).astype(BF16)
+    done = [copies.start(wide, spread)]
     cx, cy, cz, lanes = full.shape
     scale[...] = 1.0 / (6.0 + scale[...])
     down = lax.broadcasted_iota(jnp.int32, (cz, cz), 0)
@@ -352,13 +332,34 @@
         return carry
 
     lax.fori_loop(0, cx * cy, plane, 0, unroll=8)
-    wanted = codes_v[...]
-    rows = 256
-    done = []
-    for k in range(wide.shape[0] // rows):
-        ids = lax.broadcasted_iota(jnp.int32, (rows, wanted.shape[1]), 0) + (k * rows + 1)
-        wide[k * rows : (k + 1) * rows] = (ids == wanted).astype(F32).astype(BF16)
-    done += [copies.start(wide, spread), copies.start(full, inverse)]
+    done.append(copies.start(full, inverse))
+    for copy in done:
+        copy.wait()
+
+
+def tables_call(codes, reaction, lanes):
+    spread = jax.ShapeDtypeStruct((reaction.size, codes.shape[1]), BF16)
+    inverse = jax.ShapeDtypeStruct((*reaction.shape, lanes), F32)
+    return kernel_call(
+        tables_body,
+        [codes, reaction],
+        [spread, inverse],
+        [
+            (codes.shape, jnp.int32),
+            (reaction.shape, F32),
+            (spread.shape, BF16),
+            (inverse.shape, F32),
+        ],
+        4,
+        1 << 20,
+        "tables",
+    )
+
+
+def weights_body(centers, pairs, weights, places, listed_v, mix, sems):
+    copies = Copies(sems)
+    for copy in [copies.start(centers, places), copies.start(pairs, listed_v)]:
+        copy.wait()
     banks, per_dev, lanes = mix.shape
     panels = places.shape[1]
     rank = lanes // 2 // per_dev
@@ -382,33 +383,20 @@
         for k in range(banks):
             there = (panel == per_dev * k + lane // rank) & (lane < per_dev * rank)
             mix[k, p : p + 1] = jnp.sum(jnp.where(there, kernel, 0.0), axis=0, keepdims=True)
-    done.append(copies.start(mix, weights))
-    for copy in done:
-        copy.wait()
-
-
-def tables_call(codes, centers, pairs, reaction, lanes, banks):
-    cells = reaction.size
-    inverse = jax.ShapeDtypeStruct((*reaction.shape, lanes), F32)
-    spread = jax.ShapeDtypeStruct((cells, codes.shape[1]), BF16)
+    copies.start(mix, weights).wait()
+
+
+def weights_call(centers, pairs, banks):
     weights = jax.ShapeDtypeStruct((banks, pairs.shape[0], 128), F32)
     return kernel_call(
-        tables_body,
-        [codes, centers, pairs, reaction],
-        [spread, weights, inverse],
-        [
-            (codes.shape, jnp.int32),
-            (centers.shape, F32),
-            (pairs.shape, jnp.int32),
-            (reaction.shape, F32),
-            (spread.shape, BF16),
-            (weights.shape, F32),
-            (inverse.shape, F32),
-        ],
-        7,
+        weights_body,
+        [centers, pairs],
+        [weights],
+        [(centers.shape, F32), (pairs.shape, jnp.int32), (weights.shape, F32)],
+        3,
         1 << 20,
-        "tables",
-    )
+        "weights",
+    )[0]
 
 
 def fem_body(last, *refs):
@@ -425,8 +413,9 @@
         picks, chosen, rims, sides, sems = refs[26:]
     cx, cy, cz, lanes = state.shape
     rows = inner.shape[0] - cz
+    skip = CAP if returned.shape[1] > CAP else 0
     copies = Copies(sems)
-    early = [copies.start(spread, wide), copies.start(returned.at[:, pl.ds(CAP, CAP)], back)]
+    early = [copies.start(spread, wide), copies.start(returned.at[:, pl.ds(skip, CAP)], back)]
     late = [
         copies.start(first, rim.at[1 - marks[0]]),
         copies.start(second, rim.at[marks[0]]),
@@ -577,65 +566,112 @@
     )
 
 
-def pick_body(first, *refs):
-    marks = whereabouts()
-    full, hot, values, moment, rows, sent, inner, outer = refs[:8]
-    if first:
-        out, whole, mask, chosen, short, sides, packed, coded, sems = refs[8:]
-    else:
-        whole, mask, chosen, short, sides, packed, sems = refs[8:]
+def send_swaps(whole, sides, inner, outer, copies):
+    height, cz = whole.shape[0], sides.shape[1]
+    odd = whereabouts()[2]
+    done = []
+    for target, which in ((inner, 1 - odd), (outer, odd)):
+        done.append(copies.start(whole, target.at[pl.ds(0, height)]))
+        done.append(copies.start(sides.at[which], target.at[pl.ds(height, cz)]))
+    return done
+
+
+def load_body(density, rows, full, inner, outer, wide, whole, sides, sems):
     copies = Copies(sems)
-    get = copies.start(hot, coded if first else mask)
+    for copy in [copies.start(density, wide), copies.start(rows, sides)]:
+        copy.wait()
+    whole[...] = wide[...].astype(BF16)
+    done = send_swaps(whole, sides, inner, outer, copies)
+    done.append(copies.start(whole, full))
+    for copy in done:
+        copy.wait()
+
+
+def load_call(density, rows):
+    lanes, width = density.shape
+    swap = jax.ShapeDtypeStruct((lanes + rows.shape[1], width), BF16)
+    return kernel_call(
+        load_body,
+        [density, rows],
+        [jax.ShapeDtypeStruct(density.shape, BF16), swap, swap],
+        [(density.shape, F32), (density.shape, BF16), (rows.shape, BF16)],
+        7,
+        1 << 20,
+        "load",
+    )
+
+
+def choose_body(received, full, hot, sent, coded, mask, whole, packed, sems):
+    copies = Copies(sems)
+    get = copies.start(received.at[:, pl.ds(CAP, CAP)], coded)
+    load = copies.start(full, whole)
+    get.wait()
+    digits = coded[...].reshape(mask.shape[0], -1).astype(F32)
+    code = (digits[:, :1] * 32.0 + digits[:, 1:2]).astype(jnp.int32)
+    ids = lax.broadcasted_iota(jnp.int32, mask.shape, 1) + 1
+    mask[...] = (code == ids).astype(F32).astype(BF16)
+    done = [copies.start(mask, hot)]
+    load.wait()
+    picked = matmul(mask[...], whole[...], ((1,), (1,))).astype(BF16)
+    packed[...] = picked.reshape(packed.shape)
+    done.append(copies.start(packed, sent))
+    for copy in done:
+        copy.wait()
+
+
+def choose_call(received, full):
+    banks, _, lanes = received.shape
+    mask = jax.ShapeDtypeStruct((banks * CAP, full.shape[1]), BF16)
+    sent = jax.ShapeDtypeStruct((banks, CAP, lanes), BF16)
+    return kernel_call(
+        choose_body,
+        [received, full],
+        [mask, sent],
+        [(sent.shape, BF16), (mask.shape, BF16), (full.shape, BF16), (sent.shape, BF16)],
+        4,
+        2 * mask.size * lanes,
+        "choose",
+    )
+
+
+def pick_body(full, hot, values, moment, rows, sent, inner, outer, *refs):
+    whole, mask, chosen, short, sides, packed, sems = refs
+    copies = Copies(sems)
     ins = [
         copies.start(full, whole),
         copies.start(rows, sides),
         copies.start(values, chosen),
         copies.start(moment, short),
     ]
-    get.wait()
-    done = []
-    if first:
-        digits = coded[...].reshape(mask.shape[0], -1).astype(F32)
-        code = (digits[:, :1] * 32.0 + digits[:, 1:2]).astype(jnp.int32)
-        ids = lax.broadcasted_iota(jnp.int32, mask.shape, 1) + 1
-        mask[...] = (code == ids).astype(F32).astype(BF16)
-        done.append(copies.start(mask, out))
+    get = copies.start(hot, mask)
     for copy in ins:
         copy.wait()
-    height = whole.shape[0]
-    cz = sides.shape[1]
-    for target, which in ((inner, 1 - marks[2]), (outer, marks[2])):
-        done.append(copies.start(whole, target.at[pl.ds(0, height)]))
-        done.append(copies.start(sides.at[which], target.at[pl.ds(height, cz)]))
+    done = send_swaps(whole, sides, inner, outer, copies)
     banks, lanes = packed.shape[0], packed.shape[2]
-    picked = matmul(mask[...], whole[...], ((1,), (1,))).astype(BF16)
     packed[:, :CAP] = chosen[...].reshape(banks, CAP, lanes)
-    packed[:, CAP : 2 * CAP] = picked.reshape(banks, CAP, lanes)
     for bank in range(banks):
         packed[bank, 2 * CAP :] = short[...]
+    get.wait()
+    picked = matmul(mask[...], whole[...], ((1,), (1,))).astype(BF16)
+    packed[:, CAP : 2 * CAP] = picked.reshape(banks, CAP, lanes)
     done.append(copies.start(packed, sent))
     for copy in done:
         copy.wait()
 
 
 def pick_call(full, hot, values, moment, rows, banks):
-    first = hot.ndim == 3
     lanes, width = full.shape
-    mask = jax.ShapeDtypeStruct((values.shape[0], width), BF16)
     sent = jax.ShapeDtypeStruct((banks, 2 * CAP + moment.shape[0], lanes), BF16)
     swap = jax.ShapeDtypeStruct((lanes + rows.shape[1], width), BF16)
-    scratch = [(full.shape, BF16), (mask.shape, BF16), (values.shape, BF16)]
-    scratch += [(moment.shape, BF16), (rows.shape, BF16), (sent.shape, BF16)]
-    if first:
-        scratch.append((hot.shape, BF16))
+    ins = [full, hot, values, moment, rows]
     return kernel_call(
-        functools.partial(pick_body, first),
-        [full, hot, values, moment, rows],
-        [sent, swap, swap] + [mask] * first,
-        scratch,
-        11,
-        2 * mask.size * lanes,
-        "pick_first" if first else "pick",
+        pick_body,
+        ins,
+        [sent, swap, swap],
+        [(x.shape, BF16) for x in (*ins, sent)],
+        10,
+        2 * hot.size * lanes,
+        "pick",
     )
 
 
@@ -687,10 +723,10 @@
     share = excitations // fem_count
     per_dev, group, panel_rows, _ = near_blocks.shape
     bank = trace_bank.reshape(1, -1)
-    asked = exchange(index_call(bank, trace_row.reshape(1, -1), bem_count, excitations), "bem")
-    take, codes, moment, values, *edges = setup_call(
+    take, codes, sent, *edges = setup_call(
         bank,
         trace_cell.reshape(1, -1),
+        trace_row.reshape(1, -1),
         fem_field,
         bem_density,
         low_right,
@@ -698,52 +734,62 @@
         share,
         per_dev,
     )
-    spread, weights, inverse = tables_call(
-        codes, centers.T, near_pairs, reaction, excitations, bem_count
-    )
-
+    weights = weights_call(centers.T, near_pairs, bem_count)
     diag_row = bem_diagonal[None, :]
 
-    full = bem_density.astype(BF16)
-    fem_state, density, hot = fem_field, bem_density, asked
+    fem_state, density = fem_field, bem_density
     for sweep in range(ITERS):
-        last = sweep == ITERS - 1
-        if sweep > 0:
+        initial, last = sweep == 0, sweep == ITERS - 1
+        first, second, rows, near = edges
+        if initial:
+            full, inner, outer = load_call(bem_density, rows)
+            first, second, near = ordered((first, second, near), full)
+        else:
             full = exchange(copies, "fem").reshape(excitations, local_rows)
-        first, second, rows, near = edges
-        sent, inner, outer, *mask = pick_call(full, hot, values, moment, rows, bem_count)
-        if mask:
-            (hot,) = mask
+            full = ordered(full, values)
+            sent, inner, outer = pick_call(full, hot, values, moment, rows, bem_count)
+            first, second, near = ordered((first, second, near), sent)
         inner, outer = chip_swaps(inner, outer, "bem")
-        received = exchange(sent, "bem")
-        other_inner, other_outer = partner(inner, "bem"), partner(outer, "bem")
-        parts = [inner, other_inner, full, partner(full, "bem"), outer, other_outer]
-        first, second, near = ordered((first, second, near), sent)
+        received = returned = exchange(sent, "bem")
+        if initial:
+            hot, picked = choose_call(received, full)
+        others = [partner(x, "bem") for x in (inner, full, outer)]
+        parts = [inner, others[0], full, others[1], outer, others[2]]
+        if initial:
+            returned = exchange(picked, "bem")
         halos = swaps(first, second, "fem") + (partner(near, "bem"),)
-        weights = gate_call(weights, received, *halos, *([spread] if sweep == 0 else []))
+        weights = gate_call(weights, received, *halos)
         partial = near_call(near_pairs, parts, near_blocks, received, hot, weights, low_left)
+        if initial:
+            partial = ordered(partial, returned)
         summed = exchange(partial.reshape(fem_count, share, local_rows), "fem")
-        fem_state, *rest = fem_call(
-            ordered(fem_state, partial),
-            fem_source,
-            inverse,
-            spread,
-            received,
-            (*halos, other_inner, other_outer),
-            take,
-            last,
-        )
+
+        def fem_step(after):
+            return fem_call(
+                ordered(fem_state, after),
+                fem_source,
+                inverse,
+                spread,
+                returned,
+                (*halos, others[0], others[2]),
+                take,
+                last,
+            )
+
+        if initial:
+            spread, inverse = tables_call(ordered(codes, partial), reaction, excitations)
+            summed = ordered(summed, spread)
+        else:
+            fem_state, *rest = fem_step(partial)
+            summed = ordered(summed, fem_state)
         density, *more = update_call(
-            ordered(summed, fem_state),
-            density,
-            bem_source,
-            diag_row,
-            low_right,
-            per_dev,
-            last,
+            summed, density, bem_source, diag_row, low_right, per_dev, last
         )
         if not last:
             copies, moment = more
+        if initial:
+            fem_state, *rest = fem_step(copies)
+        if not last:
             values, *edges = rest
     return (fem_state, density)
 

time: 170 us -> 169 us (level)
  blocking collectives: 22.1 us -> 11.1 us
  starting transfers between devices: 68.5 us -> 75.3 us
  waiting for transfers between devices: 19.8 us -> 23.2 us
  other arithmetic: 1.78 us -> 0 us
    all_to_all x2 -> x1, blocking collectives: 22.1 us -> 11.1 us  [exchange(): return lax.all_to_all(x, axis, split_axis=0, concat_axis=0, tiled=True)]
    all_to_all x7 -> x8, starting transfers between devices: 41.6 us -> 46.9 us  [exchange(): return lax.all_to_all(x, axis, split_axis=0, concat_axis=0, tiled=True)]
    all_to_all x7 -> x8, waiting for transfers between devices: 4.5 us -> 8.26 us  [exchange(): return lax.all_to_all(x, axis, split_axis=0, concat_axis=0, tiled=True)]
    convert_element_type x1 -> x0, other arithmetic: 1.78 us -> none  [shards(): full = bem_density.astype(BF16)]
    pallas_call x15 -> x16, Pallas kernels: 55 us -> 56 us  [kernel_call(): pl.pallas_call(body, out_shape=outs, in_specs=[scalar] * len(smem) + [hbm...]
  transfers between devices with their start and end apart: 31 -> 32, of which waited for: 15 -> 16; matrix products, arithmetic and copies ran while one was open for 1% -> 0% of each run, Pallas kernels for 14% -> 17%
where the time goes in v3:
time: 169 us; the launch traced here: 167 us
  starting transfers between devices  75.3 us (45%)
  Pallas kernels  56 us (33%)
  waiting for transfers between devices  23.2 us (14%)
  blocking collectives  11.1 us (7%)
    pallas_call x16, Pallas kernels, kernel_call(): pl.pallas_call(body, out_shape=outs, in_specs=[scalar] * len(smem) + [hbm...  56 us
    all_to_all x8, starting transfers between devices, exchange(): return lax.all_to_all(x, axis, split_axis=0, concat_axis=0, tiled=True)  46.9 us
    all_to_all x1, blocking collectives, exchange(): return lax.all_to_all(x, axis, split_axis=0, concat_axis=0, tiled=True)  11.1 us
    ppermute x3, starting transfers between devices, swaps(): lax.ppermute(x_second, axis, outer)  10.6 us
    ppermute x3, waiting for transfers between devices, swaps(): lax.ppermute(x_first, axis, inner)  8.53 us
    all_to_all x8, waiting for transfers between devices, exchange(): return lax.all_to_all(x, axis, split_axis=0, concat_axis=0, tiled=True)  8.26 us
    ppermute x3, starting transfers between devices, chip_swaps(): lax.ppermute(x_outer, axis, outer)  7.88 us
    ppermute x12, waiting for transfers between devices, partner(): lax.ppermute(x, axis, [(i, i ^ 1) for i in range(lax.axis_size(axis))])  6.34 us
  transfers between devices with their start and end apart: 32, of which 16 were waited for; matrix products, arithmetic and copies ran while one was open for 0% of the time, Pallas kernels for 17%

profile of v3, /device:TPU:24, one launch (start us, length us, event | category | flops | bytes accessed | tf_op | source)
XLA Modules:
  0.0 166.5 jit_solution(2830420193141127234)
XLA Ops:
  0.6 3.6 %setup.1 = (bf16[512,2048]{1,0:T(8,128)(2,1)}, s32[1,512]{1,0:T(1,128)}, bf16[16,80,128]{2,1,0:T(8,128)(2,1)}, bf16[8,32,128]{2,1,0:T(8,128)(2,1)}, bf16[8,32,12...) custom-call(s32[1,256]{1,0:T(1,128)} %bitcast.20, s32[1,256]{1,0:T(1,128)} %bitcast.21, ...), custom_call_target="tpu_custom_call" | custom-call | flops 268435456 | bytes 2624512 | tf_op jit(solution)/shard_map/setup/pallas_call | solution.py:26
  8.3 3.2 %collective-permute-start.3 = (bf16[160,1024]{1,0:T(8,128)(2,1)}, bf16[160,1024]{1,0:T(8,128)(2,1)}, u32[]{:S(2)}, u32[]{:S(2)}) collective-permute-start(bf16[160,1024]{1,0:T(8,128)(2,1)} %get-tuple-element.62), channel_id=1, source_target_pairs={{0,14},{1,15},{2,4},{3,5},{4,2},{5,3},{6,8},{7,9},{8,6},{9,7},{10,... | collective-permute-start | bytes 983048 | tf_op jit(solution)/shard_map/ppermute | solution.py:693
  11.5 6.3 %all-to-all-start = ((bf16[16,80,128]{2,1,0:T(8,128)(2,1)}), bf16[16,80,128]{2,1,0:T(8,128)(2,1)}, u32[]{:S(2)}, u32[]{:S(2)}) async-start(bf16[16,80,128]{2,1,0:T(8,128)(2,1)} %get-tuple-element.63), calls=%async_computation | async-start | bytes 655360 | tf_op jit(solution)/shard_map/all_to_all | solution.py:679
  18.6 4.1 %collective-permute-start.6 = (bf16[8,32,128]{2,1,0:T(8,128)(2,1)}, bf16[8,32,128]{2,1,0:T(8,128)(2,1)}, u32[]{:S(2)}, u32[]{:S(2)}) collective-permute-start(bf16[8,32,128]{2,1,0:T(8,128)(2,1)} %get-tuple-element.69), channel_id=1, source_target_pairs={{16,32},{32,16},{48,64},{64,48},{80,96},{96,80},{17,33},{33,17},{4... | collective-permute-start | bytes 196616 | tf_op jit(solution)/shard_map/ppermute | solution.py:686
  28.1 7.0 %all-to-all-start.1 = ((bf16[16,32,128]{2,1,0:T(8,128)(2,1)}), bf16[16,32,128]{2,1,0:T(8,128)(2,1)}, u32[]{:S(2)}, u32[]{:S(2)}) async-start(bf16[16,32,128]{2,1,0:T(8,128)(2,1)} %get-tuple-element.71), calls=%async_computation.1 | async-start | bytes 262144 | tf_op jit(solution)/shard_map/all_to_all | solution.py:679
  38.0 5.5 %near.3 = bf16[128,1024]{1,0:T(8,128)(2,1)} custom-call(s32[2,48]{1,0:T(2,128)} %pairs.7, bf16[160,1024]{1,0:T(8,128)(2,1)} %collective-permute-done.refs_0_, bf16[160,1024]{1,0:T(8,128)(2,1)} %collective-permute-done.1.refs_1_.refs_8_, bf16[128,1024]{1,0:T(8,128)(2,1)} %get-tuple-element.61.full.refs_2_, bf16[128,1024]{1,0:T(8,128)(2,1)} %collective-permute-done.2.refs_3_, ...), custom_call_target="tpu_custom_call" | custom-call | flops 805306368 | bytes 9585024 | tf_op jit(solution)/shard_map/near/pallas_call | solution.py:26
  43.5 6.4 %all-to-all-start.2 = ((bf16[8,16,1024]{2,1,0:T(8,128)(2,1)}), bf16[8,16,1024]{2,1,0:T(8,128)(2,1)}, u32[]{:S(2)}, u32[]{:S(2)}) async-start(bf16[8,16,1024]{2,1,0:T(8,128)(2,1)} %bitcast.15), calls=%async_computation.2 | async-start | bytes 524288 | tf_op jit(solution)/shard_map/all_to_all | solution.py:679
  49.9 3.1 %tables.1 = (bf16[2048,512]{1,0:T(8,128)(2,1)}, f32[8,8,32,128]{3,2,1,0:T(8,128)}) custom-call(s32[1,512]{1,0:T(1,128)} %get-tuple-element.74.codes, f32[8,8,32]{2,1,0:T(8,128)} %reaction.1), custom_call_target="tpu_custom_call" | custom-call | flops 1048576 | bytes 10240 | tf_op jit(solution)/shard_map/tables/pallas_call | solution.py:26
  53.0 3.4 %all-to-all-done.2.refs_0_ = bf16[8,16,1024]{2,1,0:T(8,128)(2,1)} async-done(((bf16[8,16,1024]{2,1,0:T(8,128)(2,1)}), bf16[8,16,1024]{2,1,0:T(8,128)(2,1)}, u32[]{:S(2)}, u32[]{:S(2)}) %all-to-all-start.2) | async-done | bytes 262176 | tf_op jit(solution)/shard_map/all_to_all | solution.py:679
  58.3 4.8 %all-to-all-start.3 = ((bf16[8,16,1024]{2,1,0:T(8,128)(2,1)}), bf16[8,16,1024]{2,1,0:T(8,128)(2,1)}, u32[]{:S(2)}, u32[]{:S(2)}) async-start(bf16[8,16,1024]{2,1,0:T(8,128)(2,1)} %get-tuple-element.77), calls=%async_computation.3 | async-start | bytes 524288 | tf_op jit(solution)/shard_map/all_to_all | solution.py:679
  63.1 5.7 %fem_step.2 = (f32[8,8,32,128]{3,2,1,0:T(8,128)}, bf16[512,128]{1,0:T(8,128)(2,1)}, bf16[8,32,128]{2,1,0:T(8,128)(2,1)}, bf16[8,32,128]{2,1,0:T(8,128)(2,1)}, bf...) custom-call(f32[8,8,32,128]{3,2,1,0:T(8,128)} %refs_0_, f32[8,8,32,128]{3,2,1,0:T(8,128)} %refs_1_.7, ...), custom_call_target="tpu_custom_call" | custom-call | flops 536870912 | bytes 8323072 | tf_op jit(solution)/shard_map/fem_step/pallas_call | solution.py:26
  75.7 7.0 %all-to-all-start.4 = ((bf16[16,80,128]{2,1,0:T(8,128)(2,1)}), bf16[16,80,128]{2,1,0:T(8,128)(2,1)}, u32[]{:S(2)}, u32[]{:S(2)}) async-start(bf16[16,80,128]{2,1,0:T(8,128)(2,1)} %get-tuple-element.88), calls=%async_computation.4 | async-start | bytes 655360 | tf_op jit(solution)/shard_map/all_to_all | solution.py:679
  83.5 3.4 %collective-permute-start.14 = (bf16[8,32,128]{2,1,0:T(8,128)(2,1)}, bf16[8,32,128]{2,1,0:T(8,128)(2,1)}, u32[]{:S(2)}, u32[]{:S(2)}) collective-permute-start(bf16[8,32,128]{2,1,0:T(8,128)(2,1)} %get-tuple-element.93), channel_id=1, source_target_pairs={{16,32},{32,16},{48,64},{64,48},{80,96},{96,80},{17,33},{33,17},{4... | collective-permute-start | bytes 196616 | tf_op jit(solution)/shard_map/ppermute | solution.py:686
  87.0 4.1 %collective-permute-done.13.refs_2_.refs_5_ = bf16[8,32,128]{2,1,0:T(8,128)(2,1)} collective-permute-done((bf16[8,32,128]{2,1,0:T(8,128)(2,1)}, bf16[8,32,128]{2,1,0:T(8,128)(2,1)}, u32[]{:S(2)}, u32[]{:S(2)}) %collective-permute-start.13) | collective-permute-done | bytes 65568 | tf_op jit(solution)/shard_map/ppermute | solution.py:686
  93.9 5.5 %near.4 = bf16[128,1024]{1,0:T(8,128)(2,1)} custom-call(s32[2,48]{1,0:T(2,128)} %pairs.7, bf16[160,1024]{1,0:T(8,128)(2,1)} %collective-permute-done.8.refs_0_, bf16[160,1024]{1,0:T(8,128)(2,1)} %collective-permute-done.9.refs_1_.refs_8_, bf16[128,1024]{1,0:T(8,128)(2,1)} %bitcast.6.full.refs_2_, bf16[128,1024]{1,0:T(8,128)(2,1)} %collective-permute-done.10.refs_3_, ...), custom_call_target="tpu_custom_call" | custom-call | flops 805306368 | bytes 9585024 | tf_op jit(solution)/shard_map/near/pallas_call | solution.py:26
  99.4 4.9 %all-to-all-start.5 = ((bf16[8,16,1024]{2,1,0:T(8,128)(2,1)}), bf16[8,16,1024]{2,1,0:T(8,128)(2,1)}, u32[]{:S(2)}, u32[]{:S(2)}) async-start(bf16[8,16,1024]{2,1,0:T(8,128)(2,1)} %bitcast.13), calls=%async_computation.5 | async-start | bytes 524288 | tf_op jit(solution)/shard_map/all_to_all | solution.py:679
  104.3 5.6 %fem_step.3 = (f32[8,8,32,128]{3,2,1,0:T(8,128)}, bf16[512,128]{1,0:T(8,128)(2,1)}, bf16[8,32,128]{2,1,0:T(8,128)(2,1)}, bf16[8,32,128]{2,1,0:T(8,128)(2,1)}, bf...) custom-call(f32[8,8,32,128]{3,2,1,0:T(8,128)} %get-tuple-element.95.refs_0_, f32[8,8,32,128]{3,2,1,0:T(8,128)} %refs_1_.7, ...), custom_call_target="tpu_custom_call" | custom-call | flops 536870912 | bytes 8519680 | tf_op jit(solution)/shard_map/fem_step/pallas_call | solution.py:26
  112.7 11.1 %all_to_all.45 = bf16[8,16,1024]{2,1,0:T(8,128)(2,1)} all-to-all(bf16[8,16,1024]{2,1,0:T(8,128)(2,1)} %get-tuple-element.99), channel_id=1, replica_groups=mesh['fem'=8,'bem'=16] {'fem'}, dimensions={0} | all-to-all | bytes 524288 | tf_op jit(solution)/shard_map/all_to_all | solution.py:679
  130.7 6.4 %all-to-all-start.7 = ((bf16[16,80,128]{2,1,0:T(8,128)(2,1)}), bf16[16,80,128]{2,1,0:T(8,128)(2,1)}, u32[]{:S(2)}, u32[]{:S(2)}) async-start(bf16[16,80,128]{2,1,0:T(8,128)(2,1)} %get-tuple-element.106), calls=%async_computation.7 | async-start | bytes 655360 | tf_op jit(solution)/shard_map/all_to_all | solution.py:679
  138.0 3.1 %collective-permute-start.22 = (bf16[8,32,128]{2,1,0:T(8,128)(2,1)}, bf16[8,32,128]{2,1,0:T(8,128)(2,1)}, u32[]{:S(2)}, u32[]{:S(2)}) collective-permute-start(bf16[8,32,128]{2,1,0:T(8,128)(2,1)} %get-tuple-element.111), channel_id=1, source_target_pairs={{16,32},{32,16},{48,64},{64,48},{80,96},{96,80},{17,33},{33,17},{4... | collective-permute-start | bytes 196616 | tf_op jit(solution)/shard_map/ppermute | solution.py:686
  141.1 4.4 %collective-permute-done.21.refs_2_.refs_5_ = bf16[8,32,128]{2,1,0:T(8,128)(2,1)} collective-permute-done((bf16[8,32,128]{2,1,0:T(8,128)(2,1)}, bf16[8,32,128]{2,1,0:T(8,128)(2,1)}, u32[]{:S(2)}, u32[]{:S(2)}) %collective-permute-start.21) | collective-permute-done | bytes 65568 | tf_op jit(solution)/shard_map/ppermute | solution.py:686
  148.4 5.5 %near.5 = bf16[128,1024]{1,0:T(8,128)(2,1)} custom-call(s32[2,48]{1,0:T(2,128)} %pairs.7, bf16[160,1024]{1,0:T(8,128)(2,1)} %collective-permute-done.16.refs_0_, bf16[160,1024]{1,0:T(8,128)(2,1)} %collective-permute-done.17.refs_1_.refs_8_, bf16[128,1024]{1,0:T(8,128)(2,1)} %bitcast.12, bf16[128,1024]{1,0:T(8,128)(2,1)} %collective-permute-done.18.refs_3_, ...), custom_call_target="tpu_custom_call" | custom-call | flops 805306368 | bytes 9585024 | tf_op jit(solution)/shard_map/near/pallas_call | solution.py:26
  154.0 4.2 %all-to-all-start.8 = ((bf16[8,16,1024]{2,1,0:T(8,128)(2,1)}), bf16[8,16,1024]{2,1,0:T(8,128)(2,1)}, u32[]{:S(2)}, u32[]{:S(2)}) async-start(bf16[8,16,1024]{2,1,0:T(8,128)(2,1)} %bitcast.14), calls=%async_computation.8 | async-start | bytes 524288 | tf_op jit(solution)/shard_map/all_to_all | solution.py:679
  158.1 4.5 %fem_last.1 = f32[8,8,32,128]{3,2,1,0:T(8,128)} custom-call(f32[8,8,32,128]{3,2,1,0:T(8,128)} %get-tuple-element.113.refs_0_, f32[8,8,32,128]{3,2,1,0:T(8,128)} %refs_1_.7, f32[8,8,32,128]{3,2,1,0:T(8,128)} %get-tuple-element.79.refs_2_, bf16[2048,512]{1,0:T(8,128)(2,1)} %get-tuple-element.75.refs_3_, ...), custom_call_target="tpu_custom_call" | custom-call | flops 536870912 | bytes 6422528 | tf_op jit(solution)/shard_map/fem_last/pallas_call | solution.py:26
  (60 shorter events, 42.6 us)
Async XLA Ops:
  6.3 29.0 %collective-permute-start = (bf16[160,1024]{1,0:T(8,128)(2,1)}, bf16[160,1024]{1,0:T(8,128)(2,1)}, u32[]{:S(2)}, u32[]{:S(2)}) collective-permute-start(bf16[160,1024]{1,0:T(8,128)(2,1)} %get-tuple-element.60), channel_id=1, source_target_pairs={{0,2},{1,3},{2,0},{3,1},{4,6},{5,7},{6,4},{7,5},{8,10},{9,11},{10,... | collective-permute-start | bytes 983048 | tf_op jit(solution)/shard_map/ppermute | solution.py:693
  8.3 27.3 %collective-permute-start.3 = (bf16[160,1024]{1,0:T(8,128)(2,1)}, bf16[160,1024]{1,0:T(8,128)(2,1)}, u32[]{:S(2)}, u32[]{:S(2)}) collective-permute-start(bf16[160,1024]{1,0:T(8,128)(2,1)} %get-tuple-element.62), channel_id=1, source_target_pairs={{0,14},{1,15},{2,4},{3,5},{4,2},{5,3},{6,8},{7,9},{8,6},{9,7},{10,... | collective-permute-start | bytes 983048 | tf_op jit(solution)/shard_map/ppermute | solution.py:693
  11.5 14.2 %all-to-all-start = ((bf16[16,80,128]{2,1,0:T(8,128)(2,1)}), bf16[16,80,128]{2,1,0:T(8,128)(2,1)}, u32[]{:S(2)}, u32[]{:S(2)}) async-start(bf16[16,80,128]{2,1,0:T(8,128)(2,1)} %get-tuple-element.63), calls=%async_computation | async-start | bytes 655360 | tf_op jit(solution)/shard_map/all_to_all | solution.py:679
  17.8 17.3 %collective-permute-start.5 = (bf16[8,32,128]{2,1,0:T(8,128)(2,1)}, bf16[8,32,128]{2,1,0:T(8,128)(2,1)}, u32[]{:S(2)}, u32[]{:S(2)}) collective-permute-start(bf16[8,32,128]{2,1,0:T(8,128)(2,1)} %get-tuple-element.68), channel_id=1, source_target_pairs={{0,16},{16,0},{32,48},{48,32},{64,80},{80,64},{96,112},{112,96},{1... | collective-permute-start | bytes 196616 | tf_op jit(solution)/shard_map/ppermute | solution.py:686
  18.6 17.3 %collective-permute-start.6 = (bf16[8,32,128]{2,1,0:T(8,128)(2,1)}, bf16[8,32,128]{2,1,0:T(8,128)(2,1)}, u32[]{:S(2)}, u32[]{:S(2)}) collective-permute-start(bf16[8,32,128]{2,1,0:T(8,128)(2,1)} %get-tuple-element.69), channel_id=1, source_target_pairs={{16,32},{32,16},{48,64},{64,48},{80,96},{96,80},{17,33},{33,17},{4... | collective-permute-start | bytes 196616 | tf_op jit(solution)/shard_map/ppermute | solution.py:686
  22.7 13.2 %collective-permute-start.7 = (bf16[32,1024]{1,0:T(8,128)(2,1)}, bf16[32,1024]{1,0:T(8,128)(2,1)}, u32[]{:S(2)}, u32[]{:S(2)}) collective-permute-start(bf16[32,1024]{1,0:T(8,128)(2,1)} %get-tuple-element.70), channel_id=1, source_target_pairs={{0,1},{1,0},{2,3},{3,2},{4,5},{5,4},{6,7},{7,6},{8,9},{9,8},{10,11... | collective-permute-start | bytes 196616 | tf_op jit(solution)/shard_map/ppermute | solution.py:701
  28.1 15.4 %all-to-all-start.1 = ((bf16[16,32,128]{2,1,0:T(8,128)(2,1)}), bf16[16,32,128]{2,1,0:T(8,128)(2,1)}, u32[]{:S(2)}, u32[]{:S(2)}) async-start(bf16[16,32,128]{2,1,0:T(8,128)(2,1)} %get-tuple-element.71), calls=%async_computation.1 | async-start | bytes 262144 | tf_op jit(solution)/shard_map/all_to_all | solution.py:679
  43.5 12.9 %all-to-all-start.2 = ((bf16[8,16,1024]{2,1,0:T(8,128)(2,1)}), bf16[8,16,1024]{2,1,0:T(8,128)(2,1)}, u32[]{:S(2)}, u32[]{:S(2)}) async-start(bf16[8,16,1024]{2,1,0:T(8,128)(2,1)} %bitcast.15), calls=%async_computation.2 | async-start | bytes 524288 | tf_op jit(solution)/shard_map/all_to_all | solution.py:679
  58.3 11.0 %all-to-all-start.3 = ((bf16[8,16,1024]{2,1,0:T(8,128)(2,1)}), bf16[8,16,1024]{2,1,0:T(8,128)(2,1)}, u32[]{:S(2)}, u32[]{:S(2)}) async-start(bf16[8,16,1024]{2,1,0:T(8,128)(2,1)} %get-tuple-element.77), calls=%async_computation.3 | async-start | bytes 524288 | tf_op jit(solution)/shard_map/all_to_all | solution.py:679
  72.1 19.0 %collective-permute-start.8 = (bf16[160,1024]{1,0:T(8,128)(2,1)}, bf16[160,1024]{1,0:T(8,128)(2,1)}, u32[]{:S(2)}, u32[]{:S(2)}) collective-permute-start(bf16[160,1024]{1,0:T(8,128)(2,1)} %get-tuple-element.86), channel_id=1, source_target_pairs={{0,2},{1,3},{2,0},{3,1},{4,6},{5,7},{6,4},{7,5},{8,10},{9,11},{10,... | collective-permute-start | bytes 983048 | tf_op jit(solution)/shard_map/ppermute | solution.py:693
  73.6 18.0 %collective-permute-start.11 = (bf16[160,1024]{1,0:T(8,128)(2,1)}, bf16[160,1024]{1,0:T(8,128)(2,1)}, u32[]{:S(2)}, u32[]{:S(2)}) collective-permute-start(bf16[160,1024]{1,0:T(8,128)(2,1)} %get-tuple-element.87), channel_id=1, source_target_pairs={{0,14},{1,15},{2,4},{3,5},{4,2},{5,3},{6,8},{7,9},{8,6},{9,7},{10,... | collective-permute-start | bytes 983048 | tf_op jit(solution)/shard_map/ppermute | solution.py:693
  75.7 16.2 %all-to-all-start.4 = ((bf16[16,80,128]{2,1,0:T(8,128)(2,1)}), bf16[16,80,128]{2,1,0:T(8,128)(2,1)}, u32[]{:S(2)}, u32[]{:S(2)}) async-start(bf16[16,80,128]{2,1,0:T(8,128)(2,1)} %get-tuple-element.88), calls=%async_computation.4 | async-start | bytes 655360 | tf_op jit(solution)/shard_map/all_to_all | solution.py:679
  82.6 8.5 %collective-permute-start.13 = (bf16[8,32,128]{2,1,0:T(8,128)(2,1)}, bf16[8,32,128]{2,1,0:T(8,128)(2,1)}, u32[]{:S(2)}, u32[]{:S(2)}) collective-permute-start(bf16[8,32,128]{2,1,0:T(8,128)(2,1)} %get-tuple-element.92), channel_id=1, source_target_pairs={{0,16},{16,0},{32,48},{48,32},{64,80},{80,64},{96,112},{112,96},{1... | collective-permute-start | bytes 196616 | tf_op jit(solution)/shard_map/ppermute | solution.py:686
  83.5 8.4 %collective-permute-start.14 = (bf16[8,32,128]{2,1,0:T(8,128)(2,1)}, bf16[8,32,128]{2,1,0:T(8,128)(2,1)}, u32[]{:S(2)}, u32[]{:S(2)}) collective-permute-start(bf16[8,32,128]{2,1,0:T(8,128)(2,1)} %get-tuple-element.93), channel_id=1, source_target_pairs={{16,32},{32,16},{48,64},{64,48},{80,96},{96,80},{17,33},{33,17},{4... | collective-permute-start | bytes 196616 | tf_op jit(solution)/shard_map/ppermute | solution.py:686
  86.9 5.0 %collective-permute-start.15 = (bf16[32,1024]{1,0:T(8,128)(2,1)}, bf16[32,1024]{1,0:T(8,128)(2,1)}, u32[]{:S(2)}, u32[]{:S(2)}) collective-permute-start(bf16[32,1024]{1,0:T(8,128)(2,1)} %get-tuple-element.94), channel_id=1, source_target_pairs={{0,1},{1,0},{2,3},{3,2},{4,5},{5,4},{6,7},{7,6},{8,9},{9,8},{10,11... | collective-permute-start | bytes 196616 | tf_op jit(solution)/shard_map/ppermute | solution.py:701
  91.1 2.3 %collective-permute-start.9 = (bf16[160,1024]{1,0:T(8,128)(2,1)}, bf16[160,1024]{1,0:T(8,128)(2,1)}, u32[]{:S(2)}, u32[]{:S(2)}) collective-permute-start(bf16[160,1024]{1,0:T(8,128)(2,1)} %collective-permute-done.8.refs_0_), channel_id=1, source_target_pairs={{0,1},{1,0},{2,3},{3,2},{4,5},{5,4},{6,7},{7,6},{8,9},{9,8},{10,11... | collective-permute-start | bytes 983048 | tf_op jit(solution)/shard_map/ppermute | solution.py:701
  99.4 11.4 %all-to-all-start.5 = ((bf16[8,16,1024]{2,1,0:T(8,128)(2,1)}), bf16[8,16,1024]{2,1,0:T(8,128)(2,1)}, u32[]{:S(2)}, u32[]{:S(2)}) async-start(bf16[8,16,1024]{2,1,0:T(8,128)(2,1)} %bitcast.13), calls=%async_computation.5 | async-start | bytes 524288 | tf_op jit(solution)/shard_map/all_to_all | solution.py:679
  126.5 19.1 %collective-permute-start.16 = (bf16[160,1024]{1,0:T(8,128)(2,1)}, bf16[160,1024]{1,0:T(8,128)(2,1)}, u32[]{:S(2)}, u32[]{:S(2)}) collective-permute-start(bf16[160,1024]{1,0:T(8,128)(2,1)} %get-tuple-element.104), channel_id=1, source_target_pairs={{0,2},{1,3},{2,0},{3,1},{4,6},{5,7},{6,4},{7,5},{8,10},{9,11},{10,... | collective-permute-start | bytes 983048 | tf_op jit(solution)/shard_map/ppermute | solution.py:693
  128.1 18.0 %collective-permute-start.19 = (bf16[160,1024]{1,0:T(8,128)(2,1)}, bf16[160,1024]{1,0:T(8,128)(2,1)}, u32[]{:S(2)}, u32[]{:S(2)}) collective-permute-start(bf16[160,1024]{1,0:T(8,128)(2,1)} %get-tuple-element.105), channel_id=1, source_target_pairs={{0,14},{1,15},{2,4},{3,5},{4,2},{5,3},{6,8},{7,9},{8,6},{9,7},{10,... | collective-permute-start | bytes 983048 | tf_op jit(solution)/shard_map/ppermute | solution.py:693
  130.7 15.5 %all-to-all-start.7 = ((bf16[16,80,128]{2,1,0:T(8,128)(2,1)}), bf16[16,80,128]{2,1,0:T(8,128)(2,1)}, u32[]{:S(2)}, u32[]{:S(2)}) async-start(bf16[16,80,128]{2,1,0:T(8,128)(2,1)} %get-tuple-element.106), calls=%async_computation.7 | async-start | bytes 655360 | tf_op jit(solution)/shard_map/all_to_all | solution.py:679
  137.1 8.5 %collective-permute-start.21 = (bf16[8,32,128]{2,1,0:T(8,128)(2,1)}, bf16[8,32,128]{2,1,0:T(8,128)(2,1)}, u32[]{:S(2)}, u32[]{:S(2)}) collective-permute-start(bf16[8,32,128]{2,1,0:T(8,128)(2,1)} %get-tuple-element.110), channel_id=1, source_target_pairs={{0,16},{16,0},{32,48},{48,32},{64,80},{80,64},{96,112},{112,96},{1... | collective-permute-start | bytes 196616 | tf_op jit(solution)/shard_map/ppermute | solution.py:686
  138.0 8.2 %collective-permute-start.22 = (bf16[8,32,128]{2,1,0:T(8,128)(2,1)}, bf16[8,32,128]{2,1,0:T(8,128)(2,1)}, u32[]{:S(2)}, u32[]{:S(2)}) collective-permute-start(bf16[8,32,128]{2,1,0:T(8,128)(2,1)} %get-tuple-element.111), channel_id=1, source_target_pairs={{16,32},{32,16},{48,64},{64,48},{80,96},{96,80},{17,33},{33,17},{4... | collective-permute-start | bytes 196616 | tf_op jit(solution)/shard_map/ppermute | solution.py:686
  141.0 5.1 %collective-permute-start.23 = (bf16[32,1024]{1,0:T(8,128)(2,1)}, bf16[32,1024]{1,0:T(8,128)(2,1)}, u32[]{:S(2)}, u32[]{:S(2)}) collective-permute-start(bf16[32,1024]{1,0:T(8,128)(2,1)} %get-tuple-element.112), channel_id=1, source_target_pairs={{0,1},{1,0},{2,3},{3,2},{4,5},{5,4},{6,7},{7,6},{8,9},{9,8},{10,11... | collective-permute-start | bytes 196616 | tf_op jit(solution)/shard_map/ppermute | solution.py:701
  154.0 10.7 %all-to-all-start.8 = ((bf16[8,16,1024]{2,1,0:T(8,128)(2,1)}), bf16[8,16,1024]{2,1,0:T(8,128)(2,1)}, u32[]{:S(2)}, u32[]{:S(2)}) async-start(bf16[8,16,1024]{2,1,0:T(8,128)(2,1)} %bitcast.14), calls=%async_computation.8 | async-start | bytes 524288 | tf_op jit(solution)/shard_map/all_to_all | solution.py:679
  (8 other events, 17.1 us)

commit v4 on v3

--- a/solution.py
+++ b/solution.py
@@ -596,7 +596,7 @@
         [jax.ShapeDtypeStruct(density.shape, BF16), swap, swap],
         [(density.shape, F32), (density.shape, BF16), (rows.shape, BF16)],
         7,
-        1 << 20,
+        COVER,
         "load",
     )
 
@@ -734,7 +734,6 @@
         share,
         per_dev,
     )
-    weights = weights_call(centers.T, near_pairs, bem_count)
     diag_row = bem_diagonal[None, :]
 
     fem_state, density = fem_field, bem_density
@@ -743,7 +742,6 @@
         first, second, rows, near = edges
         if initial:
             full, inner, outer = load_call(bem_density, rows)
-            first, second, near = ordered((first, second, near), full)
         else:
             full = exchange(copies, "fem").reshape(excitations, local_rows)
             full = ordered(full, values)
@@ -753,6 +751,8 @@
         received = returned = exchange(sent, "bem")
         if initial:
             hot, picked = choose_call(received, full)
+            first, second, near = ordered((first, second, near), picked)
+            weights = weights_call(ordered(centers.T, picked), near_pairs, bem_count)
         others = [partner(x, "bem") for x in (inner, full, outer)]
         parts = [inner, others[0], full, others[1], outer, others[2]]
         if initial:

time: 169 us -> 169 us (level)
  transfers between devices with their start and end apart: 32 -> 32, of which waited for: 16 -> 16; matrix products, arithmetic and copies ran while one was open for 0% -> 0% of each run, Pallas kernels for 17% -> 18%
where the time goes in v4:
time: 169 us; the launch traced here: 167 us
  starting transfers between devices  74.8 us (44%)
  Pallas kernels  56 us (33%)
  waiting for transfers between devices  23.6 us (14%)
  blocking collectives  11.1 us (7%)
    pallas_call x16, Pallas kernels, kernel_call(): pl.pallas_call(body, out_shape=outs, in_specs=[scalar] * len(smem) + [hbm...  56 us
    all_to_all x8, starting transfers between devices, exchange(): return lax.all_to_all(x, axis, split_axis=0, concat_axis=0, tiled=True)  48 us
    all_to_all x1, blocking collectives, exchange(): return lax.all_to_all(x, axis, split_axis=0, concat_axis=0, tiled=True)  11.1 us
    ppermute x3, starting transfers between devices, swaps(): lax.ppermute(x_second, axis, outer)  10.6 us
    all_to_all x8, waiting for transfers between devices, exchange(): return lax.all_to_all(x, axis, split_axis=0, concat_axis=0, tiled=True)  8.71 us
    ppermute x3, waiting for transfers between devices, swaps(): lax.ppermute(x_first, axis, inner)  8.53 us
    ppermute x3, starting transfers between devices, chip_swaps(): lax.ppermute(x_outer, axis, outer)  6.72 us
    ppermute x12, waiting for transfers between devices, partner(): lax.ppermute(x, axis, [(i, i ^ 1) for i in range(lax.axis_size(axis))])  6.34 us
  transfers between devices with their start and end apart: 32, of which 16 were waited for; matrix products, arithmetic and copies ran while one was open for 0% of the time, Pallas kernels for 18%

profile of v4, /device:TPU:24, one launch (start us, length us, event | category | flops | bytes accessed | tf_op | source)
XLA Modules:
  0.0 166.5 jit_solution(391734042393441124)
XLA Ops:
  0.6 3.6 %setup.1 = (bf16[512,2048]{1,0:T(8,128)(2,1)}, s32[1,512]{1,0:T(1,128)}, bf16[16,80,128]{2,1,0:T(8,128)(2,1)}, bf16[8,32,128]{2,1,0:T(8,128)(2,1)}, bf16[8,32,12...) custom-call(s32[1,256]{1,0:T(1,128)} %bitcast.20, s32[1,256]{1,0:T(1,128)} %bitcast.21, ...), custom_call_target="tpu_custom_call" | custom-call | flops 268435456 | bytes 2624512 | tf_op jit(solution)/shard_map/setup/pallas_call | solution.py:26
  4.2 8.3 %all-to-all-start = ((bf16[16,80,128]{2,1,0:T(8,128)(2,1)}), bf16[16,80,128]{2,1,0:T(8,128)(2,1)}, u32[]{:S(2)}, u32[]{:S(2)}) async-start(bf16[16,80,128]{2,1,0:T(8,128)(2,1)} %get-tuple-element.64), calls=%async_computation | async-start | bytes 655360 | tf_op jit(solution)/shard_map/all_to_all | solution.py:679
  23.3 4.1 %collective-permute-start.6 = (bf16[8,32,128]{2,1,0:T(8,128)(2,1)}, bf16[8,32,128]{2,1,0:T(8,128)(2,1)}, u32[]{:S(2)}, u32[]{:S(2)}) collective-permute-start(bf16[8,32,128]{2,1,0:T(8,128)(2,1)} %get-tuple-element.72), channel_id=1, source_target_pairs={{16,32},{32,16},{48,64},{64,48},{80,96},{96,80},{17,33},{33,17},{4... | collective-permute-start | bytes 196616 | tf_op jit(solution)/shard_map/ppermute | solution.py:686
  27.5 6.9 %all-to-all-start.1 = ((bf16[16,32,128]{2,1,0:T(8,128)(2,1)}), bf16[16,32,128]{2,1,0:T(8,128)(2,1)}, u32[]{:S(2)}, u32[]{:S(2)}) async-start(bf16[16,32,128]{2,1,0:T(8,128)(2,1)} %get-tuple-element.66), calls=%async_computation.1 | async-start | bytes 262144 | tf_op jit(solution)/shard_map/all_to_all | solution.py:679
  38.9 5.5 %near.3 = bf16[128,1024]{1,0:T(8,128)(2,1)} custom-call(s32[2,48]{1,0:T(2,128)} %pairs.7, bf16[160,1024]{1,0:T(8,128)(2,1)} %collective-permute-done.refs_0_, bf16[160,1024]{1,0:T(8,128)(2,1)} %collective-permute-done.1.refs_1_.refs_8_, bf16[128,1024]{1,0:T(8,128)(2,1)} %get-tuple-element.62.full.refs_2_, bf16[128,1024]{1,0:T(8,128)(2,1)} %collective-permute-done.2.refs_3_, ...), custom_call_target="tpu_custom_call" | custom-call | flops 805306368 | bytes 9585024 | tf_op jit(solution)/shard_map/near/pallas_call | solution.py:26
  44.4 5.5 %all-to-all-start.2 = ((bf16[8,16,1024]{2,1,0:T(8,128)(2,1)}), bf16[8,16,1024]{2,1,0:T(8,128)(2,1)}, u32[]{:S(2)}, u32[]{:S(2)}) async-start(bf16[8,16,1024]{2,1,0:T(8,128)(2,1)} %bitcast.15), calls=%async_computation.2 | async-start | bytes 524288 | tf_op jit(solution)/shard_map/all_to_all | solution.py:679
  49.9 3.1 %tables.1 = (bf16[2048,512]{1,0:T(8,128)(2,1)}, f32[8,8,32,128]{3,2,1,0:T(8,128)}) custom-call(s32[1,512]{1,0:T(1,128)} %get-tuple-element.76.codes, f32[8,8,32]{2,1,0:T(8,128)} %reaction.1), custom_call_target="tpu_custom_call" | custom-call | flops 1048576 | bytes 10240 | tf_op jit(solution)/shard_map/tables/pallas_call | solution.py:26
  53.0 3.4 %all-to-all-done.2.refs_0_ = bf16[8,16,1024]{2,1,0:T(8,128)(2,1)} async-done(((bf16[8,16,1024]{2,1,0:T(8,128)(2,1)}), bf16[8,16,1024]{2,1,0:T(8,128)(2,1)}, u32[]{:S(2)}, u32[]{:S(2)}) %all-to-all-start.2) | async-done | bytes 262176 | tf_op jit(solution)/shard_map/all_to_all | solution.py:679
  58.3 4.8 %all-to-all-start.3 = ((bf16[8,16,1024]{2,1,0:T(8,128)(2,1)}), bf16[8,16,1024]{2,1,0:T(8,128)(2,1)}, u32[]{:S(2)}, u32[]{:S(2)}) async-start(bf16[8,16,1024]{2,1,0:T(8,128)(2,1)} %get-tuple-element.79), calls=%async_computation.3 | async-start | bytes 524288 | tf_op jit(solution)/shard_map/all_to_all | solution.py:679
  63.1 5.7 %fem_step.2 = (f32[8,8,32,128]{3,2,1,0:T(8,128)}, bf16[512,128]{1,0:T(8,128)(2,1)}, bf16[8,32,128]{2,1,0:T(8,128)(2,1)}, bf16[8,32,128]{2,1,0:T(8,128)(2,1)}, bf...) custom-call(f32[8,8,32,128]{3,2,1,0:T(8,128)} %refs_0_, f32[8,8,32,128]{3,2,1,0:T(8,128)} %refs_1_.7, ...), custom_call_target="tpu_custom_call" | custom-call | flops 536870912 | bytes 8323072 | tf_op jit(solution)/shard_map/fem_step/pallas_call | solution.py:26
  75.6 7.0 %all-to-all-start.4 = ((bf16[16,80,128]{2,1,0:T(8,128)(2,1)}), bf16[16,80,128]{2,1,0:T(8,128)(2,1)}, u32[]{:S(2)}, u32[]{:S(2)}) async-start(bf16[16,80,128]{2,1,0:T(8,128)(2,1)} %get-tuple-element.90), calls=%async_computation.4 | async-start | bytes 655360 | tf_op jit(solution)/shard_map/all_to_all | solution.py:679
  83.5 3.4 %collective-permute-start.14 = (bf16[8,32,128]{2,1,0:T(8,128)(2,1)}, bf16[8,32,128]{2,1,0:T(8,128)(2,1)}, u32[]{:S(2)}, u32[]{:S(2)}) collective-permute-start(bf16[8,32,128]{2,1,0:T(8,128)(2,1)} %get-tuple-element.95), channel_id=1, source_target_pairs={{16,32},{32,16},{48,64},{64,48},{80,96},{96,80},{17,33},{33,17},{4... | collective-permute-start | bytes 196616 | tf_op jit(solution)/shard_map/ppermute | solution.py:686
  87.0 4.1 %collective-permute-done.13.refs_2_.refs_5_ = bf16[8,32,128]{2,1,0:T(8,128)(2,1)} collective-permute-done((bf16[8,32,128]{2,1,0:T(8,128)(2,1)}, bf16[8,32,128]{2,1,0:T(8,128)(2,1)}, u32[]{:S(2)}, u32[]{:S(2)}) %collective-permute-start.13) | collective-permute-done | bytes 65568 | tf_op jit(solution)/shard_map/ppermute | solution.py:686
  93.9 5.5 %near.4 = bf16[128,1024]{1,0:T(8,128)(2,1)} custom-call(s32[2,48]{1,0:T(2,128)} %pairs.7, bf16[160,1024]{1,0:T(8,128)(2,1)} %collective-permute-done.8.refs_0_, bf16[160,1024]{1,0:T(8,128)(2,1)} %collective-permute-done.9.refs_1_.refs_8_, bf16[128,1024]{1,0:T(8,128)(2,1)} %bitcast.6.full.refs_2_, bf16[128,1024]{1,0:T(8,128)(2,1)} %collective-permute-done.10.refs_3_, ...), custom_call_target="tpu_custom_call" | custom-call | flops 805306368 | bytes 9585024 | tf_op jit(solution)/shard_map/near/pallas_call | solution.py:26
  99.4 4.9 %all-to-all-start.5 = ((bf16[8,16,1024]{2,1,0:T(8,128)(2,1)}), bf16[8,16,1024]{2,1,0:T(8,128)(2,1)}, u32[]{:S(2)}, u32[]{:S(2)}) async-start(bf16[8,16,1024]{2,1,0:T(8,128)(2,1)} %bitcast.13), calls=%async_computation.5 | async-start | bytes 524288 | tf_op jit(solution)/shard_map/all_to_all | solution.py:679
  104.4 5.6 %fem_step.3 = (f32[8,8,32,128]{3,2,1,0:T(8,128)}, bf16[512,128]{1,0:T(8,128)(2,1)}, bf16[8,32,128]{2,1,0:T(8,128)(2,1)}, bf16[8,32,128]{2,1,0:T(8,128)(2,1)}, bf...) custom-call(f32[8,8,32,128]{3,2,1,0:T(8,128)} %get-tuple-element.97.refs_0_, f32[8,8,32,128]{3,2,1,0:T(8,128)} %refs_1_.7, ...), custom_call_target="tpu_custom_call" | custom-call | flops 536870912 | bytes 8519680 | tf_op jit(solution)/shard_map/fem_step/pallas_call | solution.py:26
  112.7 11.1 %all_to_all.45 = bf16[8,16,1024]{2,1,0:T(8,128)(2,1)} all-to-all(bf16[8,16,1024]{2,1,0:T(8,128)(2,1)} %get-tuple-element.101), channel_id=1, replica_groups=mesh['fem'=8,'bem'=16] {'fem'}, dimensions={0} | all-to-all | bytes 524288 | tf_op jit(solution)/shard_map/all_to_all | solution.py:679
  123.8 2.7 %pick.3 = (bf16[16,80,128]{2,1,0:T(8,128)(2,1)}, bf16[160,1024]{1,0:T(8,128)(2,1)}, bf16[160,1024]{1,0:T(8,128)(2,1)}) custom-call(bf16[128,1024]{1,0:T(8,128)(2,1)} %bitcast.10, bf16[512,1024]{1,0:T(8,128)(2,1)} %get-tuple-element.65.refs_8_.hot, bf16[512,128]{1,0:T(8,128)(2,1)} %get-tuple-element.102.values, bf16[16,128]{1,0:T(8,128)(2,1)} %get-tuple-element.104.moment, ...), custom_call_target="tpu_custom_call" | custom-call | flops 134217728 | bytes 1576960 | tf_op jit(solution)/shard_map/pick/pallas_call | solution.py:26
  130.7 6.4 %all-to-all-start.7 = ((bf16[16,80,128]{2,1,0:T(8,128)(2,1)}), bf16[16,80,128]{2,1,0:T(8,128)(2,1)}, u32[]{:S(2)}, u32[]{:S(2)}) async-start(bf16[16,80,128]{2,1,0:T(8,128)(2,1)} %get-tuple-element.108), calls=%async_computation.7 | async-start | bytes 655360 | tf_op jit(solution)/shard_map/all_to_all | solution.py:679
  138.0 3.1 %collective-permute-start.22 = (bf16[8,32,128]{2,1,0:T(8,128)(2,1)}, bf16[8,32,128]{2,1,0:T(8,128)(2,1)}, u32[]{:S(2)}, u32[]{:S(2)}) collective-permute-start(bf16[8,32,128]{2,1,0:T(8,128)(2,1)} %get-tuple-element.113), channel_id=1, source_target_pairs={{16,32},{32,16},{48,64},{64,48},{80,96},{96,80},{17,33},{33,17},{4... | collective-permute-start | bytes 196616 | tf_op jit(solution)/shard_map/ppermute | solution.py:686
  141.2 4.4 %collective-permute-done.21.refs_2_.refs_5_ = bf16[8,32,128]{2,1,0:T(8,128)(2,1)} collective-permute-done((bf16[8,32,128]{2,1,0:T(8,128)(2,1)}, bf16[8,32,128]{2,1,0:T(8,128)(2,1)}, u32[]{:S(2)}, u32[]{:S(2)}) %collective-permute-start.21) | collective-permute-done | bytes 65568 | tf_op jit(solution)/shard_map/ppermute | solution.py:686
  148.4 5.5 %near.5 = bf16[128,1024]{1,0:T(8,128)(2,1)} custom-call(s32[2,48]{1,0:T(2,128)} %pairs.7, bf16[160,1024]{1,0:T(8,128)(2,1)} %collective-permute-done.16.refs_0_, bf16[160,1024]{1,0:T(8,128)(2,1)} %collective-permute-done.17.refs_1_.refs_8_, bf16[128,1024]{1,0:T(8,128)(2,1)} %bitcast.12, bf16[128,1024]{1,0:T(8,128)(2,1)} %collective-permute-done.18.refs_3_, ...), custom_call_target="tpu_custom_call" | custom-call | flops 805306368 | bytes 9585024 | tf_op jit(solution)/shard_map/near/pallas_call | solution.py:26
  154.0 4.2 %all-to-all-start.8 = ((bf16[8,16,1024]{2,1,0:T(8,128)(2,1)}), bf16[8,16,1024]{2,1,0:T(8,128)(2,1)}, u32[]{:S(2)}, u32[]{:S(2)}) async-start(bf16[8,16,1024]{2,1,0:T(8,128)(2,1)} %bitcast.14), calls=%async_computation.8 | async-start | bytes 524288 | tf_op jit(solution)/shard_map/all_to_all | solution.py:679
  158.1 4.5 %fem_last.1 = f32[8,8,32,128]{3,2,1,0:T(8,128)} custom-call(f32[8,8,32,128]{3,2,1,0:T(8,128)} %get-tuple-element.115.refs_0_, f32[8,8,32,128]{3,2,1,0:T(8,128)} %refs_1_.7, f32[8,8,32,128]{3,2,1,0:T(8,128)} %get-tuple-element.81.refs_2_, bf16[2048,512]{1,0:T(8,128)(2,1)} %get-tuple-element.77.refs_3_, ...), custom_call_target="tpu_custom_call" | custom-call | flops 536870912 | bytes 6422528 | tf_op jit(solution)/shard_map/fem_last/pallas_call | solution.py:26
  (60 shorter events, 42.1 us)
Async XLA Ops:
  4.2 15.9 %all-to-all-start = ((bf16[16,80,128]{2,1,0:T(8,128)(2,1)}), bf16[16,80,128]{2,1,0:T(8,128)(2,1)}, u32[]{:S(2)}, u32[]{:S(2)}) async-start(bf16[16,80,128]{2,1,0:T(8,128)(2,1)} %get-tuple-element.64), calls=%async_computation | async-start | bytes 655360 | tf_op jit(solution)/shard_map/all_to_all | solution.py:679
  14.6 21.3 %collective-permute-start = (bf16[160,1024]{1,0:T(8,128)(2,1)}, bf16[160,1024]{1,0:T(8,128)(2,1)}, u32[]{:S(2)}, u32[]{:S(2)}) collective-permute-start(bf16[160,1024]{1,0:T(8,128)(2,1)} %get-tuple-element.61), channel_id=1, source_target_pairs={{0,2},{1,3},{2,0},{3,1},{4,6},{5,7},{6,4},{7,5},{8,10},{9,11},{10,... | collective-permute-start | bytes 983048 | tf_op jit(solution)/shard_map/ppermute | solution.py:693
  16.2 20.0 %collective-permute-start.3 = (bf16[160,1024]{1,0:T(8,128)(2,1)}, bf16[160,1024]{1,0:T(8,128)(2,1)}, u32[]{:S(2)}, u32[]{:S(2)}) collective-permute-start(bf16[160,1024]{1,0:T(8,128)(2,1)} %get-tuple-element.63), channel_id=1, source_target_pairs={{0,14},{1,15},{2,4},{3,5},{4,2},{5,3},{6,8},{7,9},{8,6},{9,7},{10,... | collective-permute-start | bytes 983048 | tf_op jit(solution)/shard_map/ppermute | solution.py:693
  22.4 14.1 %collective-permute-start.5 = (bf16[8,32,128]{2,1,0:T(8,128)(2,1)}, bf16[8,32,128]{2,1,0:T(8,128)(2,1)}, u32[]{:S(2)}, u32[]{:S(2)}) collective-permute-start(bf16[8,32,128]{2,1,0:T(8,128)(2,1)} %get-tuple-element.71), channel_id=1, source_target_pairs={{0,16},{16,0},{32,48},{48,32},{64,80},{80,64},{96,112},{112,96},{1... | collective-permute-start | bytes 196616 | tf_op jit(solution)/shard_map/ppermute | solution.py:686
  23.3 13.5 %collective-permute-start.6 = (bf16[8,32,128]{2,1,0:T(8,128)(2,1)}, bf16[8,32,128]{2,1,0:T(8,128)(2,1)}, u32[]{:S(2)}, u32[]{:S(2)}) collective-permute-start(bf16[8,32,128]{2,1,0:T(8,128)(2,1)} %get-tuple-element.72), channel_id=1, source_target_pairs={{16,32},{32,16},{48,64},{64,48},{80,96},{96,80},{17,33},{33,17},{4... | collective-permute-start | bytes 196616 | tf_op jit(solution)/shard_map/ppermute | solution.py:686
  27.4 9.3 %collective-permute-start.7 = (bf16[32,1024]{1,0:T(8,128)(2,1)}, bf16[32,1024]{1,0:T(8,128)(2,1)}, u32[]{:S(2)}, u32[]{:S(2)}) collective-permute-start(bf16[32,1024]{1,0:T(8,128)(2,1)} %get-tuple-element.73), channel_id=1, source_target_pairs={{0,1},{1,0},{2,3},{3,2},{4,5},{5,4},{6,7},{7,6},{8,9},{9,8},{10,11... | collective-permute-start | bytes 196616 | tf_op jit(solution)/shard_map/ppermute | solution.py:701
  27.5 16.9 %all-to-all-start.1 = ((bf16[16,32,128]{2,1,0:T(8,128)(2,1)}), bf16[16,32,128]{2,1,0:T(8,128)(2,1)}, u32[]{:S(2)}, u32[]{:S(2)}) async-start(bf16[16,32,128]{2,1,0:T(8,128)(2,1)} %get-tuple-element.66), calls=%async_computation.1 | async-start | bytes 262144 | tf_op jit(solution)/shard_map/all_to_all | solution.py:679
  44.4 12.0 %all-to-all-start.2 = ((bf16[8,16,1024]{2,1,0:T(8,128)(2,1)}), bf16[8,16,1024]{2,1,0:T(8,128)(2,1)}, u32[]{:S(2)}, u32[]{:S(2)}) async-start(bf16[8,16,1024]{2,1,0:T(8,128)(2,1)} %bitcast.15), calls=%async_computation.2 | async-start | bytes 524288 | tf_op jit(solution)/shard_map/all_to_all | solution.py:679
  58.3 11.0 %all-to-all-start.3 = ((bf16[8,16,1024]{2,1,0:T(8,128)(2,1)}), bf16[8,16,1024]{2,1,0:T(8,128)(2,1)}, u32[]{:S(2)}, u32[]{:S(2)}) async-start(bf16[8,16,1024]{2,1,0:T(8,128)(2,1)} %get-tuple-element.79), calls=%async_computation.3 | async-start | bytes 524288 | tf_op jit(solution)/shard_map/all_to_all | solution.py:679
  72.0 19.1 %collective-permute-start.8 = (bf16[160,1024]{1,0:T(8,128)(2,1)}, bf16[160,1024]{1,0:T(8,128)(2,1)}, u32[]{:S(2)}, u32[]{:S(2)}) collective-permute-start(bf16[160,1024]{1,0:T(8,128)(2,1)} %get-tuple-element.88), channel_id=1, source_target_pairs={{0,2},{1,3},{2,0},{3,1},{4,6},{5,7},{6,4},{7,5},{8,10},{9,11},{10,... | collective-permute-start | bytes 983048 | tf_op jit(solution)/shard_map/ppermute | solution.py:693
  73.6 18.0 %collective-permute-start.11 = (bf16[160,1024]{1,0:T(8,128)(2,1)}, bf16[160,1024]{1,0:T(8,128)(2,1)}, u32[]{:S(2)}, u32[]{:S(2)}) collective-permute-start(bf16[160,1024]{1,0:T(8,128)(2,1)} %get-tuple-element.89), channel_id=1, source_target_pairs={{0,14},{1,15},{2,4},{3,5},{4,2},{5,3},{6,8},{7,9},{8,6},{9,7},{10,... | collective-permute-start | bytes 983048 | tf_op jit(solution)/shard_map/ppermute | solution.py:693
  75.6 16.3 %all-to-all-start.4 = ((bf16[16,80,128]{2,1,0:T(8,128)(2,1)}), bf16[16,80,128]{2,1,0:T(8,128)(2,1)}, u32[]{:S(2)}, u32[]{:S(2)}) async-start(bf16[16,80,128]{2,1,0:T(8,128)(2,1)} %get-tuple-element.90), calls=%async_computation.4 | async-start | bytes 655360 | tf_op jit(solution)/shard_map/all_to_all | solution.py:679
  82.6 8.5 %collective-permute-start.13 = (bf16[8,32,128]{2,1,0:T(8,128)(2,1)}, bf16[8,32,128]{2,1,0:T(8,128)(2,1)}, u32[]{:S(2)}, u32[]{:S(2)}) collective-permute-start(bf16[8,32,128]{2,1,0:T(8,128)(2,1)} %get-tuple-element.94), channel_id=1, source_target_pairs={{0,16},{16,0},{32,48},{48,32},{64,80},{80,64},{96,112},{112,96},{1... | collective-permute-start | bytes 196616 | tf_op jit(solution)/shard_map/ppermute | solution.py:686
  83.5 8.4 %collective-permute-start.14 = (bf16[8,32,128]{2,1,0:T(8,128)(2,1)}, bf16[8,32,128]{2,1,0:T(8,128)(2,1)}, u32[]{:S(2)}, u32[]{:S(2)}) collective-permute-start(bf16[8,32,128]{2,1,0:T(8,128)(2,1)} %get-tuple-element.95), channel_id=1, source_target_pairs={{16,32},{32,16},{48,64},{64,48},{80,96},{96,80},{17,33},{33,17},{4... | collective-permute-start | bytes 196616 | tf_op jit(solution)/shard_map/ppermute | solution.py:686
  86.9 5.0 %collective-permute-start.15 = (bf16[32,1024]{1,0:T(8,128)(2,1)}, bf16[32,1024]{1,0:T(8,128)(2,1)}, u32[]{:S(2)}, u32[]{:S(2)}) collective-permute-start(bf16[32,1024]{1,0:T(8,128)(2,1)} %get-tuple-element.96), channel_id=1, source_target_pairs={{0,1},{1,0},{2,3},{3,2},{4,5},{5,4},{6,7},{7,6},{8,9},{9,8},{10,11... | collective-permute-start | bytes 196616 | tf_op jit(solution)/shard_map/ppermute | solution.py:701
  91.1 2.3 %collective-permute-start.9 = (bf16[160,1024]{1,0:T(8,128)(2,1)}, bf16[160,1024]{1,0:T(8,128)(2,1)}, u32[]{:S(2)}, u32[]{:S(2)}) collective-permute-start(bf16[160,1024]{1,0:T(8,128)(2,1)} %collective-permute-done.8.refs_0_), channel_id=1, source_target_pairs={{0,1},{1,0},{2,3},{3,2},{4,5},{5,4},{6,7},{7,6},{8,9},{9,8},{10,11... | collective-permute-start | bytes 983048 | tf_op jit(solution)/shard_map/ppermute | solution.py:701
  99.4 11.4 %all-to-all-start.5 = ((bf16[8,16,1024]{2,1,0:T(8,128)(2,1)}), bf16[8,16,1024]{2,1,0:T(8,128)(2,1)}, u32[]{:S(2)}, u32[]{:S(2)}) async-start(bf16[8,16,1024]{2,1,0:T(8,128)(2,1)} %bitcast.13), calls=%async_computation.5 | async-start | bytes 524288 | tf_op jit(solution)/shard_map/all_to_all | solution.py:679
  126.5 19.1 %collective-permute-start.16 = (bf16[160,1024]{1,0:T(8,128)(2,1)}, bf16[160,1024]{1,0:T(8,128)(2,1)}, u32[]{:S(2)}, u32[]{:S(2)}) collective-permute-start(bf16[160,1024]{1,0:T(8,128)(2,1)} %get-tuple-element.106), channel_id=1, source_target_pairs={{0,2},{1,3},{2,0},{3,1},{4,6},{5,7},{6,4},{7,5},{8,10},{9,11},{10,... | collective-permute-start | bytes 983048 | tf_op jit(solution)/shard_map/ppermute | solution.py:693
  128.1 18.0 %collective-permute-start.19 = (bf16[160,1024]{1,0:T(8,128)(2,1)}, bf16[160,1024]{1,0:T(8,128)(2,1)}, u32[]{:S(2)}, u32[]{:S(2)}) collective-permute-start(bf16[160,1024]{1,0:T(8,128)(2,1)} %get-tuple-element.107), channel_id=1, source_target_pairs={{0,14},{1,15},{2,4},{3,5},{4,2},{5,3},{6,8},{7,9},{8,6},{9,7},{10,... | collective-permute-start | bytes 983048 | tf_op jit(solution)/shard_map/ppermute | solution.py:693
  130.7 15.5 %all-to-all-start.7 = ((bf16[16,80,128]{2,1,0:T(8,128)(2,1)}), bf16[16,80,128]{2,1,0:T(8,128)(2,1)}, u32[]{:S(2)}, u32[]{:S(2)}) async-start(bf16[16,80,128]{2,1,0:T(8,128)(2,1)} %get-tuple-element.108), calls=%async_computation.7 | async-start | bytes 655360 | tf_op jit(solution)/shard_map/all_to_all | solution.py:679
  137.1 8.5 %collective-permute-start.21 = (bf16[8,32,128]{2,1,0:T(8,128)(2,1)}, bf16[8,32,128]{2,1,0:T(8,128)(2,1)}, u32[]{:S(2)}, u32[]{:S(2)}) collective-permute-start(bf16[8,32,128]{2,1,0:T(8,128)(2,1)} %get-tuple-element.112), channel_id=1, source_target_pairs={{0,16},{16,0},{32,48},{48,32},{64,80},{80,64},{96,112},{112,96},{1... | collective-permute-start | bytes 196616 | tf_op jit(solution)/shard_map/ppermute | solution.py:686
  138.0 8.2 %collective-permute-start.22 = (bf16[8,32,128]{2,1,0:T(8,128)(2,1)}, bf16[8,32,128]{2,1,0:T(8,128)(2,1)}, u32[]{:S(2)}, u32[]{:S(2)}) collective-permute-start(bf16[8,32,128]{2,1,0:T(8,128)(2,1)} %get-tuple-element.113), channel_id=1, source_target_pairs={{16,32},{32,16},{48,64},{64,48},{80,96},{96,80},{17,33},{33,17},{4... | collective-permute-start | bytes 196616 | tf_op jit(solution)/shard_map/ppermute | solution.py:686
  141.1 5.1 %collective-permute-start.23 = (bf16[32,1024]{1,0:T(8,128)(2,1)}, bf16[32,1024]{1,0:T(8,128)(2,1)}, u32[]{:S(2)}, u32[]{:S(2)}) collective-permute-start(bf16[32,1024]{1,0:T(8,128)(2,1)} %get-tuple-element.114), channel_id=1, source_target_pairs={{0,1},{1,0},{2,3},{3,2},{4,5},{5,4},{6,7},{7,6},{8,9},{9,8},{10,11... | collective-permute-start | bytes 196616 | tf_op jit(solution)/shard_map/ppermute | solution.py:701
  154.0 10.7 %all-to-all-start.8 = ((bf16[8,16,1024]{2,1,0:T(8,128)(2,1)}), bf16[8,16,1024]{2,1,0:T(8,128)(2,1)}, u32[]{:S(2)}, u32[]{:S(2)}) async-start(bf16[8,16,1024]{2,1,0:T(8,128)(2,1)} %bitcast.14), calls=%async_computation.8 | async-start | bytes 524288 | tf_op jit(solution)/shard_map/all_to_all | solution.py:679
  (8 other events, 17.1 us)
